TPU v7x, 32 devices: a whole 2x2x4 slice. The times are simulated.
32 devices in a mesh: ctx: 4 (over x, core), fsdp: 8 (over z, y).
Axes of the slice: x: 2, y: 2, z: 4, core: 2. Of those that a mesh axis runs over, the one named last changes fastest.
Arguments:
- tokens: bfloat16 [2, 8, 1024, 1024], P(None, 'fsdp', 'ctx'), may hold values from -8 to 8
- cotangent: bfloat16 [2, 8, 1024, 1024], P(None, 'fsdp', 'ctx'), may hold values from -6 to 6
- random_blocks: int32 [2, 8, 16, 16, 3], P(None, 'fsdp', None, 'ctx'), may hold values from 0 to 15
- global_blocks: int32 [2, 8, 2], P(None, 'fsdp'), may hold values from 0 to 15, as said below
- attend_gain: bfloat16 [1024], P('fsdp'), may hold values from 0.099609375 to 1.8984375
- attend_bias: bfloat16 [1024], P('fsdp'), may hold values from -1.75 to 1.75
- triple_weight: bfloat16 [1024, 3072], P('fsdp'), may hold values from -0.1875 to 0.1875
- output_weight: bfloat16 [1024, 1024], P('fsdp'), may hold values from -1.5 to 1.5
- hidden_gain: bfloat16 [1024], P('fsdp'), may hold values from 0.099609375 to 1.8984375
- hidden_bias: bfloat16 [1024], P('fsdp'), may hold values from -1.75 to 1.75
- expand_weight: bfloat16 [1024, 4096], P('fsdp'), may hold values from -0.1875 to 0.1875
- expand_bias: bfloat16 [4096], P('fsdp'), may hold values from -3 to 3
- shrink_weight: bfloat16 [4096, 1024], P('fsdp'), may hold values from -0.09375 to 0.09375
- shrink_bias: bfloat16 [1024], P('fsdp'), may hold values from -1.75 to 1.75
Outputs:
- result: bfloat16 [2, 8, 1024, 1024], P(None, 'fsdp', 'ctx')
- token_grad: bfloat16 [2, 8, 1024, 1024], P(None, 'fsdp', 'ctx')
- attend_gain_grad: float32 [1024], P('fsdp')
- attend_bias_grad: float32 [1024], P('fsdp')
- triple_weight_grad: float32 [1024, 3072], P('fsdp')
- output_weight_grad: float32 [1024, 1024], P('fsdp')
- hidden_gain_grad: float32 [1024], P('fsdp')
- hidden_bias_grad: float32 [1024], P('fsdp')
- expand_weight_grad: float32 [1024, 4096], P('fsdp')
- expand_bias_grad: float32 [4096], P('fsdp')
- shrink_weight_grad: float32 [4096, 1024], P('fsdp')
- shrink_bias_grad: float32 [1024], P('fsdp')
Inputs may be any that keep to these rules, and one draw needn't show every extreme that they name: `global_blocks`: the 2 global blocks of one sequence are different.
All inputs are finite; a program needn't handle non-finite values.
Results may differ from a plain program's by a relative error of at most 0.017.
Values may be sent and summed in bfloat16 or wider, within the bound.
A program may use at most 320 MiB of HBM per device.

v0:
```python
import jax
import jax.numpy as jnp
from jax import lax
from jax.sharding import PartitionSpec as P

HEADS = 16
HEAD_DIM = 64
BLOCK = 64


epsilon = 1e-05


def layer_norm(values, scale_vector, shift_vector):
    average = jnp.mean(values, axis=-1, keepdims=True)
    centered = values - average
    variance = jnp.mean(centered * centered, axis=-1, keepdims=True)
    return centered * lax.rsqrt(variance + epsilon) * scale_vector + shift_vector


def slot_table(chosen_blocks, global_list, first_block, total_blocks):
    heads_count, local_count, picks = chosen_blocks.shape
    query_ids = first_block + jnp.arange(local_count, dtype=jnp.int32)
    window = query_ids[:, None] + jnp.arange(-1, 2, dtype=jnp.int32)[None, :]
    window = jnp.broadcast_to(window[None], (heads_count, local_count, 3))
    globals_wide = jnp.broadcast_to(
        global_list[None, None, :], (heads_count, local_count, global_list.shape[0])
    )
    slot_ids = jnp.concatenate([window, chosen_blocks, globals_wide], axis=2)
    in_range = (slot_ids >= 0) & (slot_ids < total_blocks)
    count = slot_ids.shape[2]
    earlier = jnp.arange(count)[None, :] < jnp.arange(count)[:, None]
    repeated = jnp.any(
        (slot_ids[..., :, None] == slot_ids[..., None, :]) & earlier[None, None], axis=-1
    )
    valid = in_range & jnp.logical_not(repeated)
    clipped = jnp.clip(slot_ids, 0, total_blocks - 1)
    return (clipped, valid)


def select_blocks(table, clipped):
    picked = jax.vmap(lambda rows_of, index: rows_of[index])(table, clipped)
    heads_count, local_count, slots, block_rows, head_dim = picked.shape
    return picked.reshape(heads_count, local_count, slots * block_rows, head_dim)


def sparse_scores(query_blocks, key_selected, valid, factor):
    raw = (
        jnp.einsum(
            "hqbd,hqkd->hqbk", query_blocks, key_selected, preferred_element_type=jnp.float32
        )
        * factor
    )
    heads_count, local_count, slots = valid.shape
    wide = jnp.broadcast_to(valid[:, :, :, None], (heads_count, local_count, slots, BLOCK)).reshape(
        heads_count, local_count, 1, slots * BLOCK
    )
    return jnp.where(wide, raw, -1e30)


def weight_terms(saved):
    joined = [jnp.concatenate([entry[place] for entry in saved], axis=0) for place in range(8)]
    (
        normed_all,
        d_triple_all,
        mixed_all,
        d_branch_all,
        hidden_all,
        d_before_all,
        activated_all,
        tangent_all,
    ) = joined
    grad_triple = jnp.einsum(
        "tc,te->ce", normed_all, d_triple_all, preferred_element_type=jnp.float32
    )
    grad_output = jnp.einsum(
        "tc,td->cd", mixed_all, d_branch_all, preferred_element_type=jnp.float32
    )
    grad_expand = jnp.einsum(
        "tc,tf->cf", hidden_all, d_before_all, preferred_element_type=jnp.float32
    )
    grad_shrink = jnp.einsum(
        "tf,td->fd", activated_all, tangent_all, preferred_element_type=jnp.float32
    )
    return (grad_triple, grad_output, grad_expand, grad_shrink)


def on_device(
    tokens,
    cotangent,
    random_blocks,
    global_blocks,
    attend_gain,
    attend_bias,
    triple_weight,
    output_weight,
    hidden_gain,
    hidden_bias,
    expand_weight,
    expand_bias,
    shrink_weight,
    shrink_bias,
):
    micro = tokens.shape[0]
    rows = tokens.shape[2]
    width = tokens.shape[3]
    cycle_size = lax.axis_size("ctx")
    rank = lax.axis_index("ctx")
    local_blocks = rows // BLOCK
    total_blocks = local_blocks * cycle_size
    seq_rows = total_blocks * BLOCK
    factor = HEAD_DIM ** (-0.5)
    block_index = jnp.arange(local_blocks, dtype=jnp.int32)
    kept = (
        lax.all_gather(attend_gain, "fsdp", axis=0, tiled=True),
        lax.all_gather(attend_bias, "fsdp", axis=0, tiled=True),
        lax.all_gather(triple_weight, "fsdp", axis=0, tiled=True),
        lax.all_gather(output_weight, "fsdp", axis=0, tiled=True),
        lax.all_gather(hidden_gain, "fsdp", axis=0, tiled=True),
        lax.all_gather(hidden_bias, "fsdp", axis=0, tiled=True),
        lax.all_gather(expand_weight, "fsdp", axis=0, tiled=True),
        lax.all_gather(expand_bias, "fsdp", axis=0, tiled=True),
        lax.all_gather(shrink_weight, "fsdp", axis=0, tiled=True),
        lax.all_gather(shrink_bias, "fsdp", axis=0, tiled=True),
    )
    output_rows = []
    input_rows = []
    saved_rows = []
    small_running = None
    shares = None
    for micro_step in range(micro):
        (
            gain_first,
            bias_first,
            triple_full,
            output_full,
            gain_second,
            bias_second,
            expand_full,
            expand_shift,
            shrink_full,
            shrink_shift,
        ) = kept
        gain_one = gain_first.astype(jnp.float32)
        bias_one = bias_first.astype(jnp.float32)
        gain_two = gain_second.astype(jnp.float32)
        bias_two = bias_second.astype(jnp.float32)
        inputs = tokens[micro_step, 0].astype(jnp.float32)
        normed = layer_norm(inputs, gain_one, bias_one).astype(jnp.bfloat16)
        triple = jnp.dot(normed, triple_full, preferred_element_type=jnp.float32).astype(
            jnp.bfloat16
        )
        query_blocks = (
            triple[:, :width].reshape(local_blocks, BLOCK, HEADS, HEAD_DIM).transpose(2, 0, 1, 3)
        )
        keys_whole, values_whole = (
            lax.all_gather(triple[:, width : 2 * width], "ctx", axis=0, tiled=True),
            lax.all_gather(triple[:, 2 * width :], "ctx", axis=0, tiled=True),
        )
        key_table = keys_whole.reshape(total_blocks, BLOCK, HEADS, HEAD_DIM).transpose(2, 0, 1, 3)
        value_table = values_whole.reshape(total_blocks, BLOCK, HEADS, HEAD_DIM).transpose(
            2, 0, 1, 3
        )
        key_heads = key_table.reshape(HEADS, seq_rows, HEAD_DIM)
        value_heads = value_table.reshape(HEADS, seq_rows, HEAD_DIM)
        global_list = global_blocks[micro_step, 0]
        clipped, valid = slot_table(
            random_blocks[micro_step, 0], global_list, rank * local_blocks, total_blocks
        )
        key_selected = select_blocks(key_table, clipped)
        value_selected = select_blocks(value_table, clipped)
        scores = sparse_scores(query_blocks, key_selected, valid, factor)
        row_peak = jnp.max(scores, axis=-1, keepdims=True)
        powered = jnp.exp(scores - row_peak)
        row_total = jnp.sum(powered, axis=-1, keepdims=True)
        probs = (powered / row_total).astype(jnp.bfloat16)
        sparse_lse = row_peak + jnp.log(row_total)
        mixed_blocks = jnp.einsum(
            "hqbk,hqkd->hqbd", probs, value_selected, preferred_element_type=jnp.float32
        )
        global_places = []
        global_starts = []
        global_present = []
        global_lse = []
        global_queries = []
        for which in range(global_list.shape[0]):
            offset = global_list[which] - rank * local_blocks
            present = (offset >= 0) & (offset < local_blocks)
            start = jnp.clip(offset, 0, local_blocks - 1)
            place = (block_index == offset) & present
            dense_query = lax.dynamic_slice_in_dim(query_blocks, start, 1, 1)[:, 0]
            dense = (
                jnp.einsum(
                    "hbd,hkd->hbk", dense_query, key_heads, preferred_element_type=jnp.float32
                )
                * factor
            )
            dense_peak = jnp.max(dense, axis=-1, keepdims=True)
            dense_powered = jnp.exp(dense - dense_peak)
            dense_total = jnp.sum(dense_powered, axis=-1, keepdims=True)
            dense_probs = (dense_powered / dense_total).astype(jnp.bfloat16)
            dense_mixed = jnp.einsum(
                "hbk,hkd->hbd", dense_probs, value_heads, preferred_element_type=jnp.float32
            )
            mixed_blocks = jnp.where(place[None, :, None, None], dense_mixed[:, None], mixed_blocks)
            global_places.append(place)
            global_starts.append(start)
            global_present.append(present)
            global_lse.append(dense_peak + jnp.log(dense_total))
            global_queries.append(dense_query)
        mixed = mixed_blocks.transpose(1, 2, 0, 3).reshape(rows, width).astype(jnp.bfloat16)
        attended = inputs + jnp.dot(mixed, output_full, preferred_element_type=jnp.float32)
        hidden_normed = layer_norm(attended, gain_two, bias_two).astype(jnp.bfloat16)
        before = jnp.dot(
            hidden_normed, expand_full, preferred_element_type=jnp.float32
        ) + expand_shift.astype(jnp.float32)
        activated = jax.nn.gelu(before, approximate=True).astype(jnp.bfloat16)
        output = attended + (
            jnp.dot(activated, shrink_full, preferred_element_type=jnp.float32)
            + shrink_shift.astype(jnp.float32)
        )
        output_rows.append(output.astype(jnp.bfloat16))
        tangent_low = cotangent[micro_step, 0]
        tangent = tangent_low.astype(jnp.float32)
        grad_shrink_bias = jnp.sum(tangent, axis=0)
        d_activated = jnp.einsum(
            "td,fd->tf", tangent_low, shrink_full, preferred_element_type=jnp.float32
        )
        gelu_value, gelu_pull = jax.vjp(
            lambda argument: jax.nn.gelu(argument, approximate=True), before
        )
        d_before = gelu_pull(d_activated)[0].astype(jnp.bfloat16)
        grad_expand_bias = jnp.sum(d_before.astype(jnp.float32), axis=0)
        d_hidden = jnp.einsum(
            "tf,cf->tc", d_before, expand_full, preferred_element_type=jnp.float32
        )
        second_value, second_pull = jax.vjp(layer_norm, attended, gain_two, bias_two)
        d_attended, grad_gain_two, grad_bias_two = second_pull(d_hidden)
        d_attended = d_attended + tangent
        d_branch = d_attended.astype(jnp.bfloat16)
        d_mixed = jnp.einsum(
            "td,cd->tc", d_branch, output_full, preferred_element_type=jnp.float32
        ).astype(jnp.bfloat16)
        d_mixed_blocks = d_mixed.reshape(local_blocks, BLOCK, HEADS, HEAD_DIM).transpose(2, 0, 1, 3)
        global_rows = global_places[0]
        for place in global_places[1:]:
            global_rows = global_rows | place
        d_sparse = jnp.where(
            global_rows[None, :, None, None], jnp.zeros_like(d_mixed_blocks), d_mixed_blocks
        )
        again = sparse_scores(query_blocks, key_selected, valid, factor)
        exact = jnp.exp(again - sparse_lse)
        exact_low = exact.astype(jnp.bfloat16)
        d_values_selected = jnp.einsum(
            "hqbk,hqbd->hqkd", exact_low, d_sparse, preferred_element_type=jnp.float32
        )
        d_probs = jnp.einsum(
            "hqbd,hqkd->hqbk", d_sparse, value_selected, preferred_element_type=jnp.float32
        )
        delta = jnp.sum(exact * d_probs, axis=-1, keepdims=True)
        d_scores = (exact * (d_probs - delta)).astype(jnp.bfloat16)
        d_query_blocks = (
            jnp.einsum(
                "hqbk,hqkd->hqbd", d_scores, key_selected, preferred_element_type=jnp.float32
            )
            * factor
        )
        d_keys_selected = (
            jnp.einsum(
                "hqbk,hqbd->hqkd", d_scores, query_blocks, preferred_element_type=jnp.float32
            )
            * factor
        )
        slots = clipped.shape[2]
        one_hot = (clipped[..., None] == jnp.arange(total_blocks, dtype=jnp.int32)).astype(
            jnp.float32
        )
        d_keys_heads = jnp.einsum(
            "hqsn,hqsbd->hnbd",
            one_hot,
            d_keys_selected.reshape(HEADS, local_blocks, slots, BLOCK, HEAD_DIM),
        ).reshape(HEADS, seq_rows, HEAD_DIM)
        d_values_heads = jnp.einsum(
            "hqsn,hqsbd->hnbd",
            one_hot,
            d_values_selected.reshape(HEADS, local_blocks, slots, BLOCK, HEAD_DIM),
        ).reshape(HEADS, seq_rows, HEAD_DIM)
        for which in range(len(global_places)):
            dense_query = global_queries[which]
            dense_grad = lax.dynamic_slice_in_dim(d_mixed_blocks, global_starts[which], 1, 1)[:, 0]
            dense_grad = jnp.where(global_present[which], dense_grad, jnp.zeros_like(dense_grad))
            dense = (
                jnp.einsum(
                    "hbd,hkd->hbk", dense_query, key_heads, preferred_element_type=jnp.float32
                )
                * factor
            )
            dense_exact = jnp.exp(dense - global_lse[which])
            d_values_heads = d_values_heads + jnp.einsum(
                "hbk,hbd->hkd",
                dense_exact.astype(jnp.bfloat16),
                dense_grad,
                preferred_element_type=jnp.float32,
            )
            dense_probs_grad = jnp.einsum(
                "hbd,hkd->hbk", dense_grad, value_heads, preferred_element_type=jnp.float32
            )
            dense_delta = jnp.sum(dense_exact * dense_probs_grad, axis=-1, keepdims=True)
            dense_scores_grad = (dense_exact * (dense_probs_grad - dense_delta)).astype(
                jnp.bfloat16
            )
            dense_query_grad = (
                jnp.einsum(
                    "hbk,hkd->hbd", dense_scores_grad, key_heads, preferred_element_type=jnp.float32
                )
                * factor
            )
            d_keys_heads = (
                d_keys_heads
                + jnp.einsum(
                    "hbk,hbd->hkd",
                    dense_scores_grad,
                    dense_query,
                    preferred_element_type=jnp.float32,
                )
                * factor
            )
            d_query_blocks = d_query_blocks + jnp.where(
                global_places[which][None, :, None, None], dense_query_grad[:, None], 0.0
            )
        d_queries = d_query_blocks.transpose(1, 2, 0, 3).reshape(rows, width).astype(jnp.bfloat16)
        d_keys_part = d_keys_heads.transpose(1, 0, 2).reshape(seq_rows, width)
        d_values_part = d_values_heads.transpose(1, 0, 2).reshape(seq_rows, width)
        d_keys, d_values = (
            lax.psum_scatter(
                d_keys_part.astype(jnp.bfloat16), "ctx", scatter_dimension=0, tiled=True
            ).astype(jnp.float32),
            lax.psum_scatter(
                d_values_part.astype(jnp.bfloat16), "ctx", scatter_dimension=0, tiled=True
            ).astype(jnp.float32),
        )
        d_triple = jnp.concatenate(
            [d_queries, d_keys.astype(jnp.bfloat16), d_values.astype(jnp.bfloat16)], axis=1
        )
        d_normed = jnp.einsum(
            "te,ce->tc", d_triple, triple_full, preferred_element_type=jnp.float32
        )
        first_value, first_pull = jax.vjp(layer_norm, inputs, gain_one, bias_one)
        d_inputs, grad_gain_one, grad_bias_one = first_pull(d_normed)
        input_rows.append((d_attended + d_inputs).astype(jnp.bfloat16))
        saved = (normed, d_triple, mixed, d_branch, hidden_normed, d_before, activated, tangent_low)
        smalls = (
            grad_gain_one,
            grad_bias_one,
            grad_gain_two,
            grad_bias_two,
            grad_expand_bias,
            grad_shrink_bias,
        )
        saved_rows.append(saved)
        small_running = (
            smalls
            if small_running is None
            else tuple(
                (old_value + new_value for old_value, new_value in zip(small_running, smalls))
            )
        )
    grad_triple, grad_output, grad_expand, grad_shrink = weight_terms(saved_rows)
    shares = (
        lax.psum_scatter(small_running[0], "fsdp", scatter_dimension=0, tiled=True),
        lax.psum_scatter(small_running[1], "fsdp", scatter_dimension=0, tiled=True),
        lax.psum_scatter(grad_triple, "fsdp", scatter_dimension=0, tiled=True),
        lax.psum_scatter(grad_output, "fsdp", scatter_dimension=0, tiled=True),
        lax.psum_scatter(small_running[2], "fsdp", scatter_dimension=0, tiled=True),
        lax.psum_scatter(small_running[3], "fsdp", scatter_dimension=0, tiled=True),
        lax.psum_scatter(grad_expand, "fsdp", scatter_dimension=0, tiled=True),
        lax.psum_scatter(small_running[4], "fsdp", scatter_dimension=0, tiled=True),
        lax.psum_scatter(grad_shrink, "fsdp", scatter_dimension=0, tiled=True),
        lax.psum_scatter(small_running[5], "fsdp", scatter_dimension=0, tiled=True),
    )
    final = (
        lax.psum(shares[0].astype(jnp.bfloat16), "ctx").astype(jnp.float32),
        lax.psum(shares[1].astype(jnp.bfloat16), "ctx").astype(jnp.float32),
        lax.psum(shares[2].astype(jnp.bfloat16), "ctx").astype(jnp.float32),
        lax.psum(shares[3].astype(jnp.bfloat16), "ctx").astype(jnp.float32),
        lax.psum(shares[4].astype(jnp.bfloat16), "ctx").astype(jnp.float32),
        lax.psum(shares[5].astype(jnp.bfloat16), "ctx").astype(jnp.float32),
        lax.psum(shares[6].astype(jnp.bfloat16), "ctx").astype(jnp.float32),
        lax.psum(shares[7].astype(jnp.bfloat16), "ctx").astype(jnp.float32),
        lax.psum(shares[8].astype(jnp.bfloat16), "ctx").astype(jnp.float32),
        lax.psum(shares[9].astype(jnp.bfloat16), "ctx").astype(jnp.float32),
    )
    result = jnp.stack(output_rows)[:, None]
    token_grad = jnp.stack(input_rows)[:, None]
    return (
        result,
        token_grad,
        final[0],
        final[1],
        final[2],
        final[3],
        final[4],
        final[5],
        final[6],
        final[7],
        final[8],
        final[9],
    )


def solution(mesh):
    placed = (
        P(None, "fsdp", "ctx", None),
        P(None, "fsdp", "ctx", None),
        P(None, "fsdp", None, "ctx", None),
        P(None, "fsdp", None),
        P("fsdp"),
        P("fsdp"),
        P("fsdp", None),
        P("fsdp", None),
        P("fsdp"),
        P("fsdp"),
        P("fsdp", None),
        P("fsdp"),
        P("fsdp", None),
        P("fsdp"),
    )
    return jax.shard_map(
        on_device,
        mesh=mesh,
        in_specs=placed,
        out_specs=(
            P(None, "fsdp", "ctx", None),
            P(None, "fsdp", "ctx", None),
            P("fsdp"),
            P("fsdp"),
            P("fsdp", None),
            P("fsdp", None),
            P("fsdp"),
            P("fsdp"),
            P("fsdp", None),
            P("fsdp"),
            P("fsdp", None),
            P("fsdp"),
        ),
        check_vma=False,
    )
```

profile of v0, /device:TPU:1, one launch (start us, length us, event | category | flops | bytes accessed | tf_op | source)
XLA Modules:
  0.0 1769.1 jit_solution(18361160276019182951)
XLA Ops:
  8.0 18.1 %all-gather = bf16[8,1,128]{2,1,0:T(2,128)(2,1)S(1)} all-gather(bf16[1,1,128]{2,1,0:T(2,128)(2,1)} %bitcast.519), channel_id=1, replica_groups=mesh['ctx'=4,'fsdp'=8] {'fsdp'}, dimensions={0}, use_global_device_ids=true | all-gather | bytes 2304 | tf_op jit(solution)/shard_map/all_gather | solution.py:115
  26.0 13.3 all-gather.1
  45.2 65.7 %all-gather.15.cloned.1.call-done = bf16[1024,3072]{1,0:T(8,128)(2,1)} async-done(((bf16[128,3072]{1,0:T(8,128)(2,1)}), bf16[1024,3072]{1,0:T(8,128)(2,1)}) %all-gather.15.cloned.1.call-update) | async-done | bytes 6291472 | tf_op jit(solution)/shard_map/all_gather | solution.py:117
  129.3 14.6 all-gather.2
  144.4 12.7 all-gather.3
  157.7 21.4 %all-gather.4 = bf16[8,1,512]{2,1,0:T(2,128)(2,1)S(1)} all-gather(bf16[1,1,512]{2,1,0:T(2,128)(2,1)S(1)} %reshape.653), channel_id=1, replica_groups=mesh['ctx'=4,'fsdp'=8] {'fsdp'}, dimensions={0}, use_global_device_ids=true | all-gather | bytes 9216 | tf_op jit(solution)/shard_map/all_gather | solution.py:122
  210.4 9.9 gather_fusion.2
  220.4 6.7 fusion.39
  251.4 6.6 reshape.594
  267.8 6.8 reshape.596
  285.4 9.7 gather_fusion.1
  295.1 9.8 gather_fusion
  304.9 9.8 gather_fusion.3
  368.1 20.4 %all-gather.23.cloned.1.call-done = bf16[1024,4096]{1,0:T(8,128)(2,1)} async-done(((bf16[128,4096]{1,0:T(8,128)(2,1)}), bf16[1024,4096]{1,0:T(8,128)(2,1)}) %all-gather.23.cloned.1.call-update) | async-done | bytes 8388624 | tf_op jit(solution)/shard_map/all_gather | solution.py:121
  388.5 9.6 multiply_convert_fusion.7
  404.0 109.7 %all-gather.25.cloned.1.call-done = bf16[4096,1024]{1,0:T(8,128)(2,1)} async-done(((bf16[512,1024]{1,0:T(8,128)(2,1)}), bf16[4096,1024]{1,0:T(8,128)(2,1)}) %all-gather.25.cloned.1.call-update) | async-done | bytes 8388624 | tf_op jit(solution)/shard_map/all_gather | solution.py:123
  513.8 12.1 convert_reduce_fusion.1
  525.9 8.2 convert_reduce_fusion
  545.7 10.2 multiply_reduce_fusion
  556.0 7.6 multiply_convert_fusion
  568.9 11.2 reshape.613
  580.1 8.1 convolution_bitcast_fusion.1
  588.1 7.8 reshape.614
  623.1 7.9 fusion.18
  631.1 11.2 reshape.615
  642.3 8.1 convolution_bitcast_fusion
  650.4 7.6 reshape.616
  666.8 9.8 multiply_reduce_fusion.1
  676.7 7.8 multiply_convert_fusion.1
  689.7 11.2 reshape.608
  701.0 8.1 convolution_bitcast_fusion.3
  709.0 7.7 reshape.609
  733.9 7.9 fusion.20
  741.8 11.3 reshape.610
  753.1 8.1 convolution_bitcast_fusion.2
  761.1 7.7 reshape.611
  812.7 8.3 fusion.40
  822.9 9.9 fusion.22
  834.1 10.6 fusion.26
  847.3 15.2 all-gather.5
  862.6 6.7 fusion.97
  882.6 17.0 reduce-scatter.19.cloned.1.call-done
  901.4 209.2 %reduce-scatter.17.cloned.1.call-done = f32[128,3072]{1,0:T(8,128)} async-done(((f32[1024,3072]{1,0:T(8,128)}), f32[128,3072]{1,0:T(8,128)}) %reduce-scatter.17.cloned.1.call-update) | async-done | bytes 1572880 | tf_op jit(solution)/shard_map/reduce_scatter | solution.py:372
  1113.0 283.6 %reduce-scatter.21.cloned.1.call-done = f32[128,4096]{1,0:T(8,128)} async-done(((f32[1024,4096]{1,0:T(8,128)}), f32[128,4096]{1,0:T(8,128)}) %reduce-scatter.21.cloned.1.call-update) | async-done | bytes 2097168 | tf_op jit(solution)/shard_map/reduce_scatter | solution.py:376
  1399.3 282.7 %reduce-scatter.23.cloned.1.call-done = f32[512,1024]{1,0:T(8,128)} async-done(((f32[4096,1024]{1,0:T(8,128)}), f32[512,1024]{1,0:T(8,128)}) %reduce-scatter.23.cloned.1.call-update) | async-done | bytes 2097168 | tf_op jit(solution)/shard_map/reduce_scatter | solution.py:378
  1687.4 28.5 %all-reduce.6 = (bf16[1024]{0:T(1024)(128)(2,1)S(1)}, bf16[1024]{0:T(1024)(128)(2,1)S(1)}, bf16[1024]{0:T(1024)(128)(2,1)S(1)}, bf16[1024]{0:T(1024)(128)(2,1)S(...) all-reduce(f32[1024]{0:T(1024)S(1)} %add.424, ...), channel_id=6, replica_groups=mesh['ctx'=4,'fsdp'=8] {'fsdp'}, use_global_device_ids=true, to_apply=%region_42.43.clone | all-reduce | flops 9216 | bytes 55296
  1716.3 12.7 all-reduce.7
  1735.7 18.0 %all-reduce.11.cloned.1.call-done = (bf16[128,3072]{1,0:T(8,128)(2,1)}, bf16[128,1024]{1,0:T(8,128)(2,1)}, bf16[128,4096]{1,0:T(8,128)(2,1)}, bf16[512,1024]{1,0:T(8,128)(2,1)}) async-done(((bf16[128,3072]{1,0:T(8,128)(2,1)}, bf16[128,1024]{1,0:T(8,128)(2,1)}, bf16[128,4096]{1,0:T(8,128)(2,1)}, bf16[512,1024]{1,0:T(8,128)(2,1)}), (bf16[128,3072]{1,0:T(8,128)(2,1)}, bf16[128,1024]{1,0:T(8,128)(2,1)}, ...) | async-done | bytes 3145744 | tf_op jit(solution)/shard_map/psum | solution.py:384
  (587 shorter events, 321.9 us)
Async XLA Ops:
  7.2 103.7 %all-gather.15.cloned.1.call-start = ((), (), s32[]{:S(2)}) async-start(), calls=%async_computation.8 | async-start | bytes 7077888 | tf_op jit(solution)/shard_map/all_gather | solution.py:117
  7.9 179.1 %all-gather.27.cloned.1.call-start = ((), (), s32[]{:S(2)}) async-start(), calls=%async_computation.14 | async-start | bytes 2621440 | tf_op jit(solution)/shard_map/all_gather | solution.py:157
  45.2 70.3 %copy-start.77 = (bf16[256,1024]{1,0:T(8,128)(2,1)}, bf16[256,1024]{1,0:T(8,128)(2,1)S(1)}, u32[]{:S(2)}) copy-start(bf16[256,1024]{1,0:T(8,128)(2,1)S(1)} %get-tuple-element.119) | copy-start | bytes 1572868
  45.2 72.2 %copy-start.76 = (bf16[256,1024]{1,0:T(8,128)(2,1)}, bf16[256,1024]{1,0:T(8,128)(2,1)S(1)}, u32[]{:S(2)}) copy-start(bf16[256,1024]{1,0:T(8,128)(2,1)S(1)} %get-tuple-element.118) | copy-start | bytes 1572868
  116.6 117.3 %all-gather.29.cloned.1.call-start = ((), (), s32[]{:S(2)}) async-start(), calls=%async_computation.15 | async-start | bytes 2621440 | tf_op jit(solution)/shard_map/all_gather | solution.py:158
  117.3 134.1 %all-gather.17.cloned.1.call-start = ((), (), s32[]{:S(2)}) async-start(), calls=%async_computation.9 | async-start | bytes 2621440 | tf_op jit(solution)/shard_map/all_gather | solution.py:157
  122.0 22.4 %copy-start.156 = (bf16[128]{0:T(256)(128)(2,1)S(1)}, bf16[128]{0:T(256)(128)(2,1)}, u32[]{:S(2)}) copy-start(bf16[128]{0:T(256)(128)(2,1)} %param.23) | copy-start | bytes 772
  122.0 35.7 %copy-start.131 = (s32[2,1,16,4,3]{2,3,4,1,0:T(4,128)S(1)}, s32[2,1,16,4,3]{2,3,4,1,0:T(4,128)}, u32[]{:S(2)}) copy-start(s32[2,1,16,4,3]{2,3,4,1,0:T(4,128)} %param.16) | copy-start | bytes 4612
  123.1 144.7 %all-gather.19.cloned.1.call-start = ((), (), s32[]{:S(2)}) async-start(), calls=%async_computation.10 | async-start | bytes 2621440 | tf_op jit(solution)/shard_map/all_gather | solution.py:158
  123.7 238.4 %all-gather.21.cloned.1.call-start = ((), (), s32[]{:S(2)}) async-start(), calls=%async_computation.11 | async-start | bytes 2359296 | tf_op jit(solution)/shard_map/all_gather | solution.py:118
  124.3 264.2 %all-gather.23.cloned.1.call-start = ((), (), s32[]{:S(2)}) async-start(), calls=%async_computation.12 | async-start | bytes 9437184 | tf_op jit(solution)/shard_map/all_gather | solution.py:121
  125.0 388.7 %all-gather.25.cloned.1.call-start = ((), (), s32[]{:S(2)}) async-start(), calls=%async_computation.13 | async-start | bytes 9437184 | tf_op jit(solution)/shard_map/all_gather | solution.py:123
  125.8 682.0 %reduce-scatter.13.cloned.1.call-start = ((), (), s32[]{:S(2)}) async-start(), calls=%async_computation.18 | async-start | bytes 2621440 | tf_op jit(solution)/shard_map/reduce_scatter | solution.py:335
  184.6 156.7 %copy-start.40 = (bf16[4,64,16,64]{3,2,1,0:T(8,128)(2,1)}, bf16[4,64,16,64]{3,2,1,0:T(8,128)(2,1)S(1)}, u32[]{:S(2)}) copy-start(bf16[4,64,16,64]{3,2,1,0:T(8,128)(2,1)S(1)} %reshape.593) | copy-start | bytes 1572868
  186.1 152.4 %copy-start.61 = (bf16[1,64,16,64]{3,2,1,0:T(8,128)(2,1)}, bf16[1,64,16,64]{3,2,1,0:T(8,128)(2,1)S(1)}, u32[]{:S(2)}) copy-start(bf16[1,64,16,64]{3,2,1,0:T(8,128)(2,1)S(1)} %get-tuple-element.128) | copy-start | bytes 393220
  207.2 111.6 %copy-start.102 = (f32[16,64]{1,0:T(8,128)}, f32[16,64]{1,0:T(8,128)S(1)}, u32[]{:S(2)}) copy-start(f32[16,64]{1,0:T(8,128)S(1)} %get-tuple-element.163) | copy-start | bytes 12292
  227.2 96.8 %copy-start.89 = (f32[16,4,64]{2,1,0:T(4,128)}, f32[16,4,64]{2,1,0:T(4,128)S(1)}, u32[]{:S(2)}) copy-start(f32[16,4,64]{2,1,0:T(4,128)S(1)} %get-tuple-element.161) | copy-start | bytes 49156
  231.4 92.5 %copy-start.96 = (f32[16,4,64]{2,1,0:T(4,128)}, f32[16,4,64]{2,1,0:T(4,128)S(1)}, u32[]{:S(2)}) copy-start(f32[16,4,64]{2,1,0:T(4,128)S(1)} %fusion.1) | copy-start | bytes 49156
  267.8 70.7 %copy-start.20 = (bf16[16,1024,64]{1,2,0:T(8,128)(2,1)}, bf16[16,1024,64]{1,2,0:T(8,128)(2,1)S(1)}, u32[]{:S(2)}) copy-start(bf16[16,1024,64]{1,2,0:T(8,128)(2,1)S(1)} %copy.303) | copy-start | bytes 6291460
  364.7 175.5 %copy-start.36 = (f32[256,1024]{1,0:T(8,128)}, f32[256,1024]{1,0:T(8,128)S(1)}, u32[]{:S(2)}) copy-start(f32[256,1024]{1,0:T(8,128)S(1)} %get-tuple-element.176) | copy-start | bytes 3145732
  365.1 23.4 %copy-start.128 = (f32[8,1,512]{2,1,0:T(1,128)S(1)}, f32[8,1,512]{2,1,0:T(1,128)}, u32[]{:S(2)}) copy-start(f32[8,1,512]{2,1,0:T(1,128)} %convert_element_type.380) | copy-start | bytes 49156
  365.9 174.3 %copy-start.38 = (f32[256,1024]{1,0:T(8,128)}, f32[256,1024]{1,0:T(8,128)S(1)}, u32[]{:S(2)}) copy-start(f32[256,1024]{1,0:T(8,128)S(1)} %get-tuple-element.174) | copy-start | bytes 3145732
  368.1 29.9 %copy-start.78 = (bf16[256,1024]{1,0:T(8,128)(2,1)}, bf16[256,1024]{1,0:T(8,128)(2,1)S(1)}, u32[]{:S(2)}) copy-start(bf16[256,1024]{1,0:T(8,128)(2,1)S(1)} %get-tuple-element.140) | copy-start | bytes 1572868
  398.1 115.7 %copy-start.45 = (bf16[2,1,256,1024]{3,2,1,0:T(8,128)(2,1)S(1)}, bf16[2,1,256,1024]{3,2,1,0:T(8,128)(2,1)}, u32[]{:S(2)}) copy-start(bf16[2,1,256,1024]{3,2,1,0:T(8,128)(2,1)} %param.15) | copy-start | bytes 3145732
  513.8 20.3 %slice-start.6 = ((s8[8388608]{0:T(1024)(128)(4,1)}), s8[4194304]{0:T(1024)(128)(4,1)S(1)}, s32[]{:S(2)}) async-start(s8[8388608]{0:T(1024)(128)(4,1)} %bitcast.524), calls=%async_computation.31 | async-start | bytes 8388608
  544.6 51.3 %copy-start.67 = (bf16[1,64,16,64]{3,2,1,0:T(8,128)(2,1)}, bf16[1,64,16,64]{3,2,1,0:T(8,128)(2,1)S(1)}, u32[]{:S(2)}) copy-start(bf16[1,64,16,64]{3,2,1,0:T(8,128)(2,1)S(1)} %get-tuple-element.124) | copy-start | bytes 393220
  614.1 194.8 %reduce-scatter.15.cloned.1.call-start = ((), (), s32[]{:S(2)}) async-start(), calls=%async_computation.19 | async-start | bytes 2621440 | tf_op jit(solution)/shard_map/reduce_scatter | solution.py:338
  676.6 133.5 %reduce-scatter.9.cloned.1.call-start = ((), (), s32[]{:S(2)}) async-start(), calls=%async_computation.16 | async-start | bytes 2621440 | tf_op jit(solution)/shard_map/reduce_scatter | solution.py:335
  733.4 78.1 %reduce-scatter.11.cloned.1.call-start = ((), (), s32[]{:S(2)}) async-start(), calls=%async_computation.17 | async-start | bytes 2621440 | tf_op jit(solution)/shard_map/reduce_scatter | solution.py:338
  777.6 122.0 %reduce-scatter.19.cloned.1.call-start = ((), (), s32[]{:S(2)}) async-start(), calls=%async_computation.21 | async-start | bytes 4718592 | tf_op jit(solution)/shard_map/reduce_scatter | solution.py:373
  782.4 328.2 %reduce-scatter.17.cloned.1.call-start = ((), (), s32[]{:S(2)}) async-start(), calls=%async_computation.20 | async-start | bytes 14155776 | tf_op jit(solution)/shard_map/reduce_scatter | solution.py:372
  821.0 575.6 %reduce-scatter.21.cloned.1.call-start = ((), (), s32[]{:S(2)}) async-start(), calls=%async_computation.22 | async-start | bytes 18874368 | tf_op jit(solution)/shard_map/reduce_scatter | solution.py:376
  832.8 849.2 %reduce-scatter.23.cloned.1.call-start = ((), (), s32[]{:S(2)}) async-start(), calls=%async_computation.23 | async-start | bytes 18874368 | tf_op jit(solution)/shard_map/reduce_scatter | solution.py:378
  844.7 17.7 %copy-start.151 = (f32[1024]{0:T(1024)S(1)}, f32[1024]{0:T(1024)}, u32[]{:S(2)}) copy-start(f32[1024]{0:T(1024)} %get-tuple-element.66) | copy-start | bytes 12292
  844.8 17.7 %copy-start.152 = (f32[1024]{0:T(1024)S(1)}, f32[1024]{0:T(1024)}, u32[]{:S(2)}) copy-start(f32[1024]{0:T(1024)} %get-tuple-element.154) | copy-start | bytes 12292
  844.8 17.8 %copy-start.149 = (f32[1024]{0:T(1024)S(1)}, f32[1024]{0:T(1024)}, u32[]{:S(2)}) copy-start(f32[1024]{0:T(1024)} %get-tuple-element.76) | copy-start | bytes 12292
  844.8 17.8 %copy-start.150 = (f32[1024]{0:T(1024)S(1)}, f32[1024]{0:T(1024)}, u32[]{:S(2)}) copy-start(f32[1024]{0:T(1024)} %get-tuple-element.152) | copy-start | bytes 12292
  844.8 17.8 %copy-start.129 = (f32[1024]{0:T(1024)S(1)}, f32[1024]{0:T(1024)}, u32[]{:S(2)}) copy-start(f32[1024]{0:T(1024)} %get-tuple-element.73) | copy-start | bytes 12292
  844.8 17.8 %copy-start.130 = (f32[1024]{0:T(1024)S(1)}, f32[1024]{0:T(1024)}, u32[]{:S(2)}) copy-start(f32[1024]{0:T(1024)} %get-tuple-element.74) | copy-start | bytes 12292
  844.8 17.8 %copy-start.39 = (f32[256,1024]{1,0:T(8,128)S(1)}, f32[256,1024]{1,0:T(8,128)}, u32[]{:S(2)}) copy-start(f32[256,1024]{1,0:T(8,128)} %copy-done.38) | copy-start | bytes 3145732
  844.8 908.9 %all-reduce.11.cloned.1.call-start = ((), (), s32[]{:S(2)}) async-start(), calls=%async_computation.24 | async-start | bytes 6291456 | tf_op jit(solution)/shard_map/psum | solution.py:384
  1113.0 571.8 %copy-start.136 = (f32[256]{0:T(256)S(1)}, f32[256]{0:T(256)}, u32[]{:S(2)}) copy-start(f32[256]{0:T(256)} %copy-done.135) | copy-start | bytes 3076
  1113.0 571.8 %copy-start.134 = (f32[256]{0:T(256)S(1)}, f32[256]{0:T(256)}, u32[]{:S(2)}) copy-start(f32[256]{0:T(256)} %copy-done.133) | copy-start | bytes 3076
  1113.0 571.9 %copy-start.122 = (f32[256]{0:T(256)S(1)}, f32[256]{0:T(256)}, u32[]{:S(2)}) copy-start(f32[256]{0:T(256)} %copy-done.121) | copy-start | bytes 3076
  1113.0 571.9 %copy-start.124 = (f32[256]{0:T(256)S(1)}, f32[256]{0:T(256)}, u32[]{:S(2)}) copy-start(f32[256]{0:T(256)} %copy-done.123) | copy-start | bytes 3076
  1399.3 332.9 %copy-start.50 = (f32[256,1024]{1,0:T(8,128)S(1)}, f32[256,1024]{1,0:T(8,128)}, u32[]{:S(2)}) copy-start(f32[256,1024]{1,0:T(8,128)} %copy-done.49) | copy-start | bytes 3145732
  1399.3 332.9 %copy-start.138 = (f32[256]{0:T(256)S(1)}, f32[256]{0:T(256)}, u32[]{:S(2)}) copy-start(f32[256]{0:T(256)} %copy-done.137) | copy-start | bytes 3076
  1399.3 332.9 %copy-start.140 = (f32[256]{0:T(256)S(1)}, f32[256]{0:T(256)}, u32[]{:S(2)}) copy-start(f32[256]{0:T(256)} %copy-done.139) | copy-start | bytes 3076
  (141 other events, 720.4 us)
Sparse Core Ops, SparseCore 0:
  10.2 100.6 all-gather.14
  116.7 21.6 all-gather.26
  140.6 22.5 all-gather.28
  165.2 22.5 all-gather.16
  189.8 22.5 all-gather.18
  214.4 47.7 all-gather.20
  264.3 124.1 all-gather.22
  390.6 123.1 all-gather.24
  614.2 29.9 reduce-scatter.12
  676.7 30.1 reduce-scatter.14
  733.6 30.1 reduce-scatter.8
  777.7 30.1 reduce-scatter.10
  811.6 87.9 reduce-scatter.18
  903.5 207.0 reduce-scatter.16
  1114.7 281.8 reduce-scatter.20
  1400.2 281.7 reduce-scatter.22
  1685.8 67.9 all-reduce.10
where the time goes:
time: 1780 us; the launch traced here: 1770 us
  waiting for transfers between devices  1010 us (57%)
  matrix products  264 us (15%)
  local copies, waits for them, and re-layouts  260 us (15%)
  blocking collectives  136 us (8%)
  other arithmetic  76.9 us (4%)
  between operations  20.4 us (1%)
    reduce_scatter x1, waiting for transfers between devices, on_device(): lax.psum_scatter(grad_expand, 'fsdp', scatter_dimension=0, tiled=True)  284 us
    reduce_scatter x1, waiting for transfers between devices, on_device(): lax.psum_scatter(grad_shrink, 'fsdp', scatter_dimension=0, tiled=True)  283 us
    reduce_scatter x1, waiting for transfers between devices, on_device(): lax.psum_scatter(grad_triple, 'fsdp', scatter_dimension=0, tiled=True)  209 us
    all_gather x1, waiting for transfers between devices, on_device(): lax.all_gather(shrink_weight, 'fsdp', axis=0, tiled=True)  110 us
    all_gather x1, waiting for transfers between devices, on_device(): lax.all_gather(triple_weight, 'fsdp', axis=0, tiled=True)  65.7 us
    gather x8, local copies, waits for them, and re-layouts, select_blocks(): picked = jax.vmap(lambda rows_of, index: rows_of[index])(table, clipped)  39.6 us
    unnamed x358, local copies, waits for them, and re-layouts  36.5 us
  transfers between devices with their start and end apart: 17, of which 8 were waited for; matrix products, arithmetic and copies ran while one was open for 26% of the time, Pallas kernels for 0%

commit v1 on v0

v1 whole, which is shorter than its diff:
```python
import functools

import jax
import jax.numpy as jnp
from jax import lax
from jax.experimental import pallas as pl
from jax.experimental.pallas import tpu as pltpu
from jax.sharding import PartitionSpec as P

HEAD_DIM = 64
BLOCK = 64
EPSILON = 1e-05
F32 = jnp.float32
BF16 = jnp.bfloat16
MIB = 1 << 20

VM = pl.BlockSpec(memory_space=pltpu.VMEM)
SM = pl.BlockSpec(memory_space=pltpu.SMEM)
ANY = pl.BlockSpec(memory_space=pl.ANY)

NN = (((1,), (0,)), ((), ()))
NT = (((1,), (1,)), ((), ()))
TN = (((0,), (0,)), ((), ()))


def dot(left, right, dims=NN):
    return lax.dot_general(left, right, dims, preferred_element_type=F32)


def shape(dims, kind):
    return jax.ShapeDtypeStruct(dims, kind)


def params(limit=56):
    return pltpu.CompilerParams(vmem_limit_bytes=limit * MIB)


def cost(flops, moved, special=0):
    return pl.CostEstimate(flops=flops, bytes_accessed=moved, transcendentals=special)


def swap(value, axis, step):
    size = lax.axis_size(axis)
    return lax.ppermute(value, axis, [(i, i ^ step) for i in range(size)])


def gather_rows(piece):
    size = lax.axis_size("fsdp")
    if size == 8:
        line = [piece] + [swap(piece, "fsdp", 2 * k) for k in range(1, 4)]
        return [block for mine in line for block in (mine, swap(mine, "fsdp", 1))]
    whole = lax.all_gather(piece, "fsdp", axis=0, tiled=True)
    rows = whole.shape[0] // 8
    return [whole[(1 ^ j) * rows : (1 ^ j) * rows + rows] for j in range(8)]


def place_id():
    return lax.axis_index("fsdp") if lax.axis_size("fsdp") == 8 else jnp.int32(1)


def wide_add(*terms):
    total = terms[0].astype(F32)
    for term in terms[1:]:
        total = total + term.astype(F32)
    return total


def scatter_rows(kept, sent):
    if lax.axis_size("fsdp") == 8:
        came = swap(sent, "fsdp", 1)
        sums = [wide_add(kept[k], came[k]).astype(BF16) for k in range(4)]
        return wide_add(sums[0], *(swap(sums[k], "fsdp", 2 * k) for k in range(1, 4)))
    whole = jnp.stack([sent, kept], axis=1)
    whole = whole.reshape((8 * kept.shape[1],) + kept.shape[2:])
    return lax.psum_scatter(whole.astype(F32), "fsdp", scatter_dimension=0, tiled=True)


def sum_everywhere(vector):
    if lax.axis_size("fsdp") == 8:
        for axis, step in (("ctx", 1), ("ctx", 2), ("fsdp", 1), ("fsdp", 2), ("fsdp", 4)):
            vector = vector + swap(vector, axis, step)
        return vector
    return lax.psum(vector, ("ctx", "fsdp"))


def norm_parts(values):
    average = jnp.mean(values, axis=-1, keepdims=True)
    centered = values - average
    variance = jnp.mean(centered * centered, axis=-1, keepdims=True)
    inverse = lax.rsqrt(variance + EPSILON)
    return centered * inverse, inverse


def norm_back(grad, unit, inverse, gain):
    scaled = grad * gain
    first = jnp.mean(scaled, axis=-1, keepdims=True)
    second = jnp.mean(scaled * unit, axis=-1, keepdims=True)
    return inverse * (scaled - first - unit * second)


def fetch(pieces, target, semaphores, base, rows):
    copies = []
    for j in range(8):
        start = pl.multiple_of((base ^ j) * rows, rows)
        copies.append(
            pltpu.make_async_copy(pieces[j], target.at[pl.ds(start, rows), :], semaphores.at[j])
        )
        copies[-1].start()
    return copies


def project_kernel(ids, t0, t1, t2, t3, gain, bias, *rest):
    pieces, (triple, normed), (held, semaphores) = rest[:8], rest[8:10], rest[10:]
    copies = fetch(pieces, held, semaphores, ids[0], pieces[0].shape[0])
    rows = t0.shape[0]
    for place, part in enumerate((t0, t1, t2, t3)):
        unit, _ = norm_parts(part[...].astype(F32))
        normed[place * rows : (place + 1) * rows, :] = (unit * gain[...] + bias[...]).astype(BF16)
    for copy in copies:
        copy.wait()
    for place in range(4):
        block = normed[place * rows : (place + 1) * rows, :]
        triple[place * rows : (place + 1) * rows, :] = dot(block, held[...]).astype(BF16)


def project(ids, parts, gain, bias, pieces):
    rows, width = parts[0].shape
    columns = pieces[0].shape[1]
    return pl.pallas_call(
        project_kernel,
        name="project",
        out_shape=(shape((4 * rows, columns), BF16), shape((4 * rows, width), BF16)),
        in_specs=[SM] + [VM] * 6 + [ANY] * 8,
        out_specs=(VM, VM),
        scratch_shapes=[pltpu.VMEM((width, columns), BF16), pltpu.SemaphoreType.DMA((8,))],
        compiler_params=params(),
        cost_estimate=cost(8 * rows * width * columns, 12 * rows * width + 2 * width * columns),
    )(ids, *parts, gain, bias, *pieces)


def head_mask(rows):
    return lax.broadcasted_iota(jnp.int32, (rows, 2 * HEAD_DIM), 1) // HEAD_DIM


def attend_kernel(triple, block_bias, m0, m1, m2, m3, lse):
    outs = (m0, m1, m2, m3)
    length = triple.shape[0]
    width = triple.shape[1] // 3
    rows = length // 4
    blocks = length // BLOCK
    lse[...] = jnp.zeros_like(lse)
    for pair in range(width // 128):
        keys = triple[:, width + pair * 128 : width + pair * 128 + 128]
        values = triple[:, 2 * width + pair * 128 : 2 * width + pair * 128 + 128]
        values_t = values.astype(F32).T.astype(BF16)
        for place in range(4):
            span = slice(place * rows, (place + 1) * rows)
            queries = triple[span, pair * 128 : pair * 128 + 128] * jnp.asarray(0.125, BF16)
            side = head_mask(rows)
            halves = []
            for which in range(2):
                head = 2 * pair + which
                one = jnp.where(side == which, queries, jnp.zeros_like(queries))
                scores = dot(keys, one, NT)
                scores = scores.reshape(blocks, BLOCK, rows) + block_bias[head, :, span][:, None, :]
                peak = jnp.max(jnp.max(scores, axis=0), axis=0, keepdims=True)
                powered = jnp.exp(scores - peak[None])
                total = jnp.sum(jnp.sum(powered, axis=0), axis=0, keepdims=True)
                lse[head : head + 1, span] = peak + jnp.log(total)
                low = powered.astype(BF16).reshape(length, rows)
                part = dot(values_t[which * HEAD_DIM : (which + 1) * HEAD_DIM, :], low)
                halves.append(part / total)
            joined = jnp.concatenate(halves, axis=0)
            outs[place][:, pair * 128 : pair * 128 + 128] = joined.T.astype(BF16)


def attend(triple, block_bias):
    length, columns = triple.shape
    width = columns // 3
    heads = width // HEAD_DIM
    rows = length // 4
    return pl.pallas_call(
        attend_kernel,
        name="attend",
        out_shape=tuple(shape((rows, width), BF16) for _ in range(4)) + (shape((8, length), F32),),
        in_specs=[VM, VM],
        out_specs=(VM,) * 5,
        compiler_params=params(),
        cost_estimate=cost(
            32 * heads * length * length * HEAD_DIM, 8 * length * width, heads * length * length
        ),
    )(triple, block_bias)


def attend_back_kernel(ids, triple, block_bias, lse, *rest):
    grads, mixed, pieces = rest[:4], rest[4:8], rest[8:16]
    d_triple, n0, n1, n2, n3 = rest[16:21]
    held, semaphores, key_total, value_total = rest[21:]
    copies = fetch(pieces, held, semaphores, ids[0], pieces[0].shape[0])
    length = triple.shape[0]
    width = triple.shape[1] // 3
    rows = length // 4
    blocks = length // BLOCK
    for pair in range(width // 128):
        lanes = slice(pair * 128, pair * 128 + 128)
        keys = triple[:, width + pair * 128 : width + pair * 128 + 128]
        values = triple[:, 2 * width + pair * 128 : 2 * width + pair * 128 + 128]
        keys_t = keys.astype(F32).T.astype(BF16)
        key_total[...] = jnp.zeros_like(key_total)
        value_total[...] = jnp.zeros_like(value_total)
        for place in range(4):
            span = slice(place * rows, (place + 1) * rows)
            queries = triple[span, lanes] * jnp.asarray(0.125, BF16)
            grad = grads[place][:, lanes]
            product = (grad.astype(F32) * mixed[place][:, lanes].astype(F32)).T
            side = head_mask(rows)
            halves = []
            for which in range(2):
                head = 2 * pair + which
                one = jnp.where(side == which, queries, jnp.zeros_like(queries))
                one_grad = jnp.where(side == which, grad, jnp.zeros_like(grad))
                delta = jnp.sum(
                    product[which * HEAD_DIM : (which + 1) * HEAD_DIM, :], axis=0, keepdims=True
                )
                scores = dot(keys, one, NT)
                shift = block_bias[head, :, span] - lse[head : head + 1, span]
                exact = jnp.exp(scores.reshape(blocks, BLOCK, rows) + shift[:, None, :])
                exact = exact.reshape(length, rows)
                value_total[...] += dot(exact.astype(BF16), one_grad)
                d_probs = dot(values, one_grad, NT)
                d_scores = (exact * (d_probs - delta)).astype(BF16)
                key_total[...] += dot(d_scores, one)
                halves.append(dot(keys_t[which * HEAD_DIM : (which + 1) * HEAD_DIM, :], d_scores))
            joined = jnp.concatenate(halves, axis=0) * 0.125
            d_triple[span, lanes] = joined.T.astype(BF16)
        d_triple[:, width + pair * 128 : width + pair * 128 + 128] = key_total[...].astype(BF16)
        d_triple[:, 2 * width + pair * 128 : 2 * width + pair * 128 + 128] = value_total[
            ...
        ].astype(BF16)
    for copy in copies:
        copy.wait()
    for place, out in enumerate((n0, n1, n2, n3)):
        out[...] = dot(d_triple[place * rows : (place + 1) * rows, :], held[...], NT).astype(BF16)


def attend_back(ids, triple, block_bias, lse, grads, mixed, pieces, width_all):
    length, columns = triple.shape
    width = columns // 3
    heads = width // HEAD_DIM
    rows = length // 4
    return pl.pallas_call(
        attend_back_kernel,
        name="attend_back",
        out_shape=(shape((length, columns), BF16),)
        + tuple(shape((rows, width_all), BF16) for _ in range(4)),
        in_specs=[SM] + [VM] * 11 + [ANY] * 8,
        out_specs=(VM,) * 5,
        scratch_shapes=[
            pltpu.VMEM((width_all, columns), BF16),
            pltpu.SemaphoreType.DMA((8,)),
            pltpu.VMEM((length, 128), F32),
            pltpu.VMEM((length, 128), F32),
        ],
        compiler_params=params(),
        cost_estimate=cost(
            80 * heads * length * length * HEAD_DIM, 16 * length * width, heads * length * length
        ),
    )(ids, triple, block_bias, lse, *grads, *mixed, *pieces)


def fetch_output(ids, own, other, held, semaphores):
    copies = []
    rows = own.shape[0] // 8
    half = own.shape[1]
    for j in range(8):
        block = ids[0] ^ j
        start = pl.multiple_of(((block // 2) ^ ids[1]) * (2 * rows) + (block % 2) * rows, rows)
        for side, source in enumerate((own, other)):
            column = pl.multiple_of((ids[2] ^ side) * half, half)
            copies.append(
                pltpu.make_async_copy(
                    source.at[pl.ds(j * rows, rows), :],
                    held.at[pl.ds(start, rows), pl.ds(column, half)],
                    semaphores.at[2 * j + side],
                )
            )
            copies[-1].start()
    return copies


def output_kernel(ids, tokens, *rest):
    mixed, (gain, bias, own, other) = rest[:8], rest[8:12]
    attended, normed, joined, held, semaphores = rest[12:]
    copies = fetch_output(ids, own, other, held, semaphores)
    rows, width = mixed[0].shape
    for micro in range(2):
        for place in range(4):
            joined[micro * rows : (micro + 1) * rows, place * width : (place + 1) * width] = mixed[
                4 * micro + place
            ][...]
    for copy in copies:
        copy.wait()
    for micro in range(2):
        span = slice(micro * rows, (micro + 1) * rows)
        value = tokens[micro].astype(F32) + dot(joined[span, :], held[...])
        attended[span, :] = value
        unit, _ = norm_parts(value)
        normed[span, :] = (unit * gain[...] + bias[...]).astype(BF16)


def output_project(ids, tokens, mixed, gain, bias, own, other):
    micro, rows, width = tokens.shape
    total = micro * rows
    return pl.pallas_call(
        output_kernel,
        name="output_project",
        out_shape=(
            shape((total, width), F32),
            shape((total, width), BF16),
            shape((total, width), BF16),
        ),
        in_specs=[SM] + [VM] * 11 + [ANY] * 2,
        out_specs=(VM, VM, VM),
        scratch_shapes=[
            pltpu.VMEM((width, width), BF16),
            pltpu.SemaphoreType.DMA((16,)),
        ],
        compiler_params=params(),
        cost_estimate=cost(2 * total * width * width, 12 * total * width + 2 * width * width),
    )(ids, tokens, *mixed, gain, bias, own, other)


CURVE = 0.7978845608028654
CUBIC = 0.044715


def feed_kernel(ids, h0, h1, c0, c1, shift, *rest):
    expand, shrink = rest[:8], rest[8:16]
    own_out, other_out, own_hidden, other_hidden, bias_grad = rest[16:21]
    shrink_sent, shrink_kept, expand_sent, expand_kept = rest[21:25]
    expand_held, hidden, tangent, hidden_t, out_total, hidden_total, semaphores = rest[25:]
    base = ids[0]
    copies = fetch(expand, expand_held, semaphores, base, expand[0].shape[0])
    rows, width = h0.shape
    tile = shrink[0].shape[0]
    deep = expand[0].shape[0]
    hidden[:rows, :] = h0[...]
    hidden[rows:, :] = h1[...]
    tangent[:rows, :] = c0[...]
    tangent[rows:, :] = c1[...]
    for j in range(8):
        source = pl.multiple_of((base ^ j) * deep, deep)
        hidden_t[j * deep : (j + 1) * deep, :] = (
            hidden[:, pl.ds(source, deep)].astype(F32).T.astype(BF16)
        )
    for copy in copies:
        copy.wait()
    for step, j in enumerate((1, 3, 5, 7, 0, 2, 4, 6)):
        column = pl.multiple_of((base ^ j) * tile, tile)
        up = expand_held[:, pl.ds(column, tile)]
        down = shrink[j][...]
        before = dot(hidden[...], up) + shift[:, pl.ds(column, tile)]
        d_active = dot(tangent[...], down, NT)
        square = before * before
        bend = jnp.tanh(CURVE * before * (1.0 + CUBIC * square))
        plus = 0.5 * (1.0 + bend)
        active = (before * plus).astype(BF16)
        slope = plus + (0.5 * CURVE) * before * (1.0 - bend * bend) * (1.0 + 3 * CUBIC * square)
        d_before = (d_active * slope).astype(BF16)
        bias_grad[:, pl.ds(column, tile)] = jnp.sum(d_before.astype(F32), axis=0, keepdims=True)
        out_part = dot(active, down)
        hidden_part = dot(d_before, up, NT)
        if step == 0:
            out_total[...] = out_part
            hidden_total[...] = hidden_part
        else:
            out_total[...] += out_part
            hidden_total[...] += hidden_part
        shrink_part = dot(active, tangent[...], TN).astype(BF16)
        (shrink_sent if j % 2 else shrink_kept)[j // 2] = shrink_part
        expand_part = dot(hidden_t[...], d_before).astype(BF16)
        for place in range(8):
            target = expand_sent if place % 2 else expand_kept
            target[place // 2, :, pl.ds(column, tile)] = expand_part[
                place * deep : (place + 1) * deep, :
            ]
    own_out[...] = out_total[:rows, :]
    other_out[...] = out_total[rows:, :].astype(BF16)
    own_hidden[...] = hidden_total[:rows, :]
    other_hidden[...] = hidden_total[rows:, :].astype(BF16)


def feed(ids, hidden, tangent, shift, expand, shrink):
    rows, width = hidden[0].shape
    deep, wide = expand[0].shape
    tile = shrink[0].shape[0]
    return pl.pallas_call(
        feed_kernel,
        name="feed",
        out_shape=(
            shape((rows, width), F32),
            shape((rows, width), BF16),
            shape((rows, width), F32),
            shape((rows, width), BF16),
            shape((1, wide), F32),
            shape((4, tile, width), BF16),
            shape((4, tile, width), BF16),
            shape((4, deep, wide), BF16),
            shape((4, deep, wide), BF16),
        ),
        in_specs=[SM] + [VM] * 5 + [ANY] * 8 + [VM] * 8,
        out_specs=(VM,) * 9,
        scratch_shapes=[
            pltpu.VMEM((width, wide), BF16),
            pltpu.VMEM((2 * rows, width), BF16),
            pltpu.VMEM((2 * rows, width), BF16),
            pltpu.VMEM((width, 2 * rows), BF16),
            pltpu.VMEM((2 * rows, width), F32),
            pltpu.VMEM((2 * rows, width), F32),
            pltpu.SemaphoreType.DMA((8,)),
        ],
        compiler_params=params(60),
        cost_estimate=cost(24 * rows * width * wide, 8 * width * wide + 20 * rows * width, 2 * rows * wide),
    )(ids, *hidden, *tangent, shift, *expand, *shrink)


def branch_kernel(
    ids, attended, own_hidden, came_hidden, tangent, own_out, came_out, gain, shift, own, other, *rest
):
    result, d_attended, d_branch = rest[:3]
    grads, (gain_grad, bias_grad, shift_grad), (held, semaphores) = rest[3:11], rest[11:14], rest[14:]
    copies = fetch_output(ids, own, other, held, semaphores)
    rows = tangent.shape[1]
    width = gain.shape[1] // 4
    gain_total = bias_total = shift_total = 0.0
    for micro in range(2):
        span = slice(micro * rows, (micro + 1) * rows)
        value = attended[span, :]
        cot = tangent[micro].astype(F32)
        branch = own_out[span, :] + came_out[span, :].astype(F32) + shift[...]
        result[micro] = (value + branch).astype(BF16)
        unit, inverse = norm_parts(value)
        grad = own_hidden[span, :] + came_hidden[span, :].astype(F32)
        gain_total = gain_total + jnp.sum(grad * unit, axis=0, keepdims=True)
        bias_total = bias_total + jnp.sum(grad, axis=0, keepdims=True)
        shift_total = shift_total + jnp.sum(cot, axis=0, keepdims=True)
        total = cot + norm_back(grad, unit, inverse, gain[...])
        d_attended[span, :] = total
        d_branch[span, :] = total.astype(BF16)
    gain_grad[...] = gain_total
    bias_grad[...] = bias_total
    shift_grad[...] = shift_total
    for copy in copies:
        copy.wait()
    for micro in range(2):
        mixed = dot(d_branch[micro * rows : (micro + 1) * rows, :], held[...], NT).astype(BF16)
        for place in range(4):
            grads[4 * micro + place][...] = mixed[:, place * width : (place + 1) * width]


def branch_back(ids, attended, own_hidden, came_hidden, tangent, own_out, came_out, gain, shift, own, other):
    micro, rows, width = tangent.shape
    total = micro * rows
    row = shape((1, width), F32)
    return pl.pallas_call(
        branch_kernel,
        name="branch_back",
        out_shape=(
            shape(tangent.shape, BF16),
            shape((total, width), F32),
            shape((total, width), BF16),
        )
        + tuple(shape((rows, width // 4), BF16) for _ in range(8))
        + (row, row, row),
        in_specs=[SM] + [VM] * 8 + [ANY] * 2,
        out_specs=(VM,) * 14,
        scratch_shapes=[pltpu.VMEM((width, width), BF16), pltpu.SemaphoreType.DMA((16,))],
        compiler_params=params(),
        cost_estimate=cost(2 * total * width * width, 32 * total * width),
    )(ids, attended, own_hidden, came_hidden, tangent, own_out, came_out, gain, shift, own, other)


def output_grad_kernel(ids, own_mixed, other_mixed, own_branch, other_branch, out):
    rows = out.shape[1]
    width = own_branch.shape[1]
    half = width // 2
    column = pl.multiple_of(ids[2] * half, half)
    right = own_branch[:, pl.ds(column, half)]
    for k in range(4):
        block = ids[0] ^ (2 * k + ids[3])
        first = ((block // 2) ^ ids[1]) * (2 * rows) + (block % 2) * rows
        second = ((block // 2) ^ ids[1] ^ 1) * (2 * rows) + (block % 2) * rows
        part = dot(own_mixed[:, pl.ds(pl.multiple_of(first, rows), rows)], right, TN)
        part += dot(other_mixed[:, pl.ds(pl.multiple_of(second, rows), rows)], other_branch[...], TN)
        out[k] = part.astype(BF16)


def output_grad(ids, own_mixed, other_mixed, own_branch, other_branch):
    total, width = own_mixed.shape
    return pl.pallas_call(
        output_grad_kernel,
        name="output_grad",
        out_shape=shape((4, width // 8, width // 2), BF16),
        in_specs=[SM] + [VM] * 4,
        out_specs=VM,
        compiler_params=params(),
        cost_estimate=cost(total * width * width, 8 * total * width),
    )(ids, own_mixed, other_mixed, own_branch, other_branch)


def triple_grad_kernel(ids, n0, n1, d0, d1, out):
    rows = out.shape[1]
    for k in range(4):
        column = pl.multiple_of((ids[0] ^ (2 * k + ids[3])) * rows, rows)
        part = dot(n0[:, pl.ds(column, rows)], d0[...], TN)
        part += dot(n1[:, pl.ds(column, rows)], d1[...], TN)
        out[k] = part.astype(BF16)


def triple_grad(ids, normed, grads):
    length, width = normed[0].shape
    columns = grads[0].shape[1]
    return pl.pallas_call(
        triple_grad_kernel,
        name="triple_grad",
        out_shape=shape((4, width // 8, columns), BF16),
        in_specs=[SM] + [VM] * 4,
        out_specs=VM,
        compiler_params=params(),
        cost_estimate=cost(2 * length * width * columns, 4 * length * (width + columns)),
    )(ids, *normed, *grads)


def first_back_kernel(tokens, d_attended, gain, *rest):
    parts, (grad_out, gain_grad, bias_grad) = rest[:6], rest[6:]
    rows = tokens.shape[1]
    gain_total = bias_total = 0.0
    for micro in range(2):
        one, two, three = parts[3 * micro : 3 * micro + 3]
        grad = one[...].astype(F32) + two[...].astype(F32) + three[...].astype(F32)
        unit, inverse = norm_parts(tokens[micro].astype(F32))
        gain_total = gain_total + jnp.sum(grad * unit, axis=0, keepdims=True)
        bias_total = bias_total + jnp.sum(grad, axis=0, keepdims=True)
        total = d_attended[micro * rows : (micro + 1) * rows, :]
        grad_out[micro] = (total + norm_back(grad, unit, inverse, gain[...])).astype(BF16)
    gain_grad[...] = gain_total
    bias_grad[...] = bias_total


def first_back(tokens, d_attended, gain, parts):
    micro, rows, width = tokens.shape
    row = shape((1, width), F32)
    return pl.pallas_call(
        first_back_kernel,
        name="first_back",
        out_shape=(shape(tokens.shape, BF16), row, row),
        in_specs=[VM] * 9,
        out_specs=(VM,) * 3,
        compiler_params=params(),
        cost_estimate=cost(20 * micro * rows * width, 16 * micro * rows * width),
    )(tokens, d_attended, gain, *parts)


def block_biases(chosen, globals_here, rank, local_blocks):
    heads, count, _ = chosen.shape
    place = jnp.arange(count, dtype=jnp.int32)
    true_block = ((place // local_blocks) ^ rank) * local_blocks + place % local_blocks
    near = jnp.abs(true_block[:, None] - true_block[None, :]) <= 1
    is_global = jnp.any(true_block[:, None] == globals_here[None, :], axis=1)
    picked = jnp.any(chosen[:, None, :, :] == true_block[None, :, None, None], axis=3)
    allowed = near[None] | picked | is_global[None, :, None] | is_global[None, None, :]
    bias = jnp.where(allowed, 0.0, -1e30).astype(F32)
    return jnp.repeat(bias, BLOCK, axis=2)


def on_device(
    tokens,
    cotangent,
    random_blocks,
    global_blocks,
    attend_gain,
    attend_bias,
    triple_weight,
    output_weight,
    hidden_gain,
    hidden_bias,
    expand_weight,
    expand_bias,
    shrink_weight,
    shrink_bias,
):
    tokens, cotangent = tokens[:, 0], cotangent[:, 0]
    micro, rows, width = tokens.shape
    total = micro * rows
    ways = lax.axis_size("fsdp")
    fsdp = lax.axis_index("fsdp")
    rank = lax.axis_index("ctx")
    core = rank % 2
    place = place_id()
    heads_all = random_blocks.shape[2]
    own_heads = heads_all // 4
    local_blocks = rows // BLOCK
    shard = width // ways
    wide = expand_weight.shape[1]
    deep = shrink_weight.shape[0]
    ids = jnp.stack([place, rank, core, jnp.int32(0)])
    ids_sent = jnp.stack([place, rank, core, jnp.int32(1)])

    small = jnp.concatenate(
        [attend_gain, attend_bias, hidden_gain, hidden_bias, shrink_bias, expand_bias]
    ).reshape(1, -1)
    small_rows = gather_rows(small) if ways == 8 else None
    triple_part = jnp.take(triple_weight.reshape(shard, 3, 4, width // 4), rank, axis=2)
    triple_pieces = gather_rows(triple_part.reshape(shard, 3 * width // 4))
    token_parts, chosen = [], None
    for step in range(micro):
        mine = tokens[step]
        far = swap(mine, "ctx", 2)
        token_parts.append((mine, swap(mine, "ctx", 1), far, swap(far, "ctx", 1)))
    picks = random_blocks[:, 0]
    far_picks = swap(picks, "ctx", 2)
    all_picks = jnp.stack([picks, swap(picks, "ctx", 1), far_picks, swap(far_picks, "ctx", 1)])
    chosen = lax.dynamic_slice_in_dim(all_picks, rank * own_heads, own_heads, 2)
    chosen = chosen.transpose(1, 2, 0, 3, 4).reshape(micro, own_heads, 4 * local_blocks, -1)
    output_part = lax.dynamic_slice_in_dim(output_weight, core * (width // 2), width // 2, 1)
    output_own = jnp.concatenate(gather_rows(output_part), axis=0)
    output_other = swap(output_own, "ctx", 1)
    if ways != 8:
        pass
    expand_part = jnp.take(expand_weight.reshape(shard, ways, 2, wide // (2 * ways)), core, axis=2)
    expand_pieces = gather_rows(expand_part.reshape(shard, wide // 2))
    shrink_part = lax.dynamic_slice_in_dim(shrink_weight, core * (deep // 2), deep // 2, 0)
    shrink_pieces = gather_rows(shrink_part)
    tangent_own = cotangent.reshape(total, width)
    tangent_other = swap(tangent_own, "ctx", 1)

    if ways == 8:
        table = jnp.concatenate(small_rows, axis=0)[jnp.arange(8) ^ fsdp].astype(F32)
    else:
        table = lax.all_gather(small, "fsdp", axis=0, tiled=True).astype(F32)
    gain_one, bias_one, gain_two, bias_two, shift_out = (
        table[:, k * shard : (k + 1) * shard].reshape(1, width) for k in range(5)
    )
    shift_in = jnp.take(table[:, 5 * shard :].reshape(ways, 2, wide // (2 * ways)), core, axis=1)
    shift_in = shift_in.reshape(1, wide // 2)

    biases, triples, normeds, lses, mixed_own, mixed_here = [], [], [], [], [], []
    for step in range(micro):
        biases.append(block_biases(chosen[step], global_blocks[step, 0], rank, local_blocks))
        triple, normed = project(ids, token_parts[step], gain_one, bias_one, triple_pieces)
        *mixed, lse = attend(triple, biases[step])
        triples.append(triple)
        normeds.append(normed)
        lses.append(lse)
        mixed_own.append(mixed)
        mixed_here += [mixed[0]] + [swap(mixed[p], "ctx", p) for p in range(1, 4)]
    attended, hidden, mixed_all = output_project(
        ids, tokens, mixed_here, gain_two, bias_two, output_own, output_other
    )

    hidden_other = swap(hidden, "ctx", 1)
    (
        own_out,
        other_out,
        own_hidden,
        other_hidden,
        shift_in_grad,
        shrink_sent,
        shrink_kept,
        expand_sent,
        expand_kept,
    ) = feed(ids, (hidden, hidden_other), (tangent_own, tangent_other), shift_in, expand_pieces, shrink_pieces)
    came_hidden = swap(other_hidden, "ctx", 1)
    came_out = swap(other_out, "ctx", 1)
    shrink_mine = scatter_rows(shrink_kept, shrink_sent)
    expand_mine = scatter_rows(expand_kept, expand_sent)
    result, d_attended, d_branch, *grads, gain_two_grad, bias_two_grad, shift_out_grad = branch_back(
        ids,
        attended,
        own_hidden,
        came_hidden,
        cotangent,
        own_out,
        came_out,
        gain_two,
        shift_out,
        output_own,
        output_other,
    )
    mixed_other = swap(mixed_all, "ctx", 1)
    half_sent = lax.dynamic_slice_in_dim(d_branch, (1 - core) * (width // 2), width // 2, 1)
    branch_other = swap(half_sent, "ctx", 1)
    output_sent = output_grad(ids_sent, mixed_all, mixed_other, d_branch, branch_other)
    output_kept = output_grad(ids, mixed_all, mixed_other, d_branch, branch_other)
    output_mine = scatter_rows(output_kept, output_sent)

    d_triples, norm_parts_here = [], []
    for step in range(micro):
        here = grads[4 * step : 4 * step + 4]
        here = [here[0]] + [swap(here[p], "ctx", p) for p in range(1, 4)]
        d_triple, *parts = attend_back(
            ids, triples[step], biases[step], lses[step], here, mixed_own[step], triple_pieces, width
        )
        d_triples.append(d_triple)
        near = swap(parts[1], "ctx", 1)
        far = wide_add(parts[2], swap(parts[3], "ctx", 1)).astype(BF16)
        norm_parts_here += [parts[0], near, swap(far, "ctx", 2)]
    triple_sent = triple_grad(ids_sent, normeds, d_triples)
    triple_kept = triple_grad(ids, normeds, d_triples)
    triple_mine = scatter_rows(triple_kept, triple_sent)
    token_grad, gain_one_grad, bias_one_grad = first_back(
        tokens, d_attended, gain_one, norm_parts_here
    )

    halves = shift_in_grad.reshape(ways, 1, wide // (2 * ways))
    blank = jnp.zeros_like(halves)
    spread = jnp.where(
        core == 0,
        jnp.concatenate([halves, blank], axis=1),
        jnp.concatenate([blank, halves], axis=1),
    )
    early = sum_everywhere(
        jnp.concatenate(
            [
                gain_two_grad.reshape(ways, shard),
                bias_two_grad.reshape(ways, shard),
                shift_out_grad.reshape(ways, shard),
                spread.reshape(ways, wide // ways),
            ],
            axis=1,
        )
    )
    late = sum_everywhere(
        jnp.concatenate([gain_one_grad.reshape(ways, shard), bias_one_grad.reshape(ways, shard)], axis=1)
    )
    early = lax.dynamic_index_in_dim(early, fsdp, 0, keepdims=False)
    late = lax.dynamic_index_in_dim(late, fsdp, 0, keepdims=False)

    def over_chips(part):
        low = part.astype(BF16)
        return wide_add(low, swap(low, "ctx", 2))

    def both(own, axis):
        other = swap(own, "ctx", 1)
        first = jnp.where(core == 0, own, other)
        second = jnp.where(core == 0, other, own)
        return jnp.stack([first, second], axis=axis)

    shrink_grad = both(over_chips(shrink_mine), 0).reshape(deep, width)
    expand_half = over_chips(expand_mine).reshape(shard, ways, wide // (2 * ways))
    expand_grad = both(expand_half, 2).reshape(shard, wide)
    output_grad_all = both(over_chips(output_mine), 1).reshape(shard, width)
    low = triple_mine.astype(BF16).reshape(shard, 3, width // 4)
    far = swap(low, "ctx", 2)
    pair = jnp.stack([jnp.where(rank < 2, low, far), jnp.where(rank < 2, far, low)], axis=2)
    triple_grad_all = both(pair, 3).reshape(shard, 3 * width).astype(F32)

    return (
        result[:, None],
        token_grad[:, None],
        late[:shard],
        late[shard:],
        triple_grad_all,
        output_grad_all,
        early[:shard],
        early[shard : 2 * shard],
        expand_grad,
        early[3 * shard :],
        shrink_grad,
        early[2 * shard : 3 * shard],
    )


def solution(mesh):
    token_spec = P(None, "fsdp", "ctx", None)
    flat, rows = P("fsdp"), P("fsdp", None)
    return jax.shard_map(
        on_device,
        mesh=mesh,
        in_specs=(
            token_spec,
            token_spec,
            P(None, "fsdp", None, "ctx", None),
            P(None, "fsdp", None),
            flat,
            flat,
            rows,
            rows,
            flat,
            flat,
            rows,
            flat,
            rows,
            flat,
        ),
        out_specs=(
            token_spec,
            token_spec,
            flat,
            flat,
            rows,
            rows,
            flat,
            flat,
            rows,
            flat,
            rows,
            flat,
        ),
        check_vma=False,
    )
```

time: 1780 us -> 592 us (0.33)
  waiting for transfers between devices: 1010 us -> 215 us
  matrix products: 264 us -> 0 us
  local copies, waits for them, and re-layouts: 260 us -> 37.8 us
  starting transfers between devices: 1.26 us -> 157 us
  Pallas kernels: 0 us -> 150 us
  blocking collectives: 136 us -> 0 us
  other arithmetic: 76.9 us -> 27 us
  between operations: 20.4 us -> 2.06 us
    reduce_scatter x8 -> x0, waiting for transfers between devices: 793 us -> none  [the longest x1 284 us: on_device(): lax.psum_scatter(grad_expand, 'fsdp', scatter_dimension=0, tiled=True)]
    dot_general x60 -> x0, matrix products: 264 us -> none  [the longest x2 20.3 us: on_device(): jnp.einsum('td,fd->tf', tangent_low, shrink_full, preferred_element_type=...]
    ppermute x0 -> x103, waiting for transfers between devices: none -> 215 us  [swap(): return lax.ppermute(value, axis, [(i, i ^ step) for i in range(size)])]
    all_gather x8 -> x0, waiting for transfers between devices: 196 us -> none  [the longest x1 110 us: on_device(): lax.all_gather(shrink_weight, 'fsdp', axis=0, tiled=True)]
    ppermute x0 -> x103, starting transfers between devices: none -> 157 us  [swap(): return lax.ppermute(value, axis, [(i, i ^ step) for i in range(size)])]
    pallas_call x0 -> x14, Pallas kernels: none -> 150 us  [the longest x1 37.7 us: feed(): pl.pallas_call(feed_kernel, name='feed', out_shape=(shape((rows, width),...]
    reshape x24 -> x5, local copies, waits for them, and re-layouts: 147 us -> 5.42 us  [the longest x1 2.68 us: on_device(): expand_grad = both(expand_half, 2).reshape(shard, wide)]
    all_gather x6 -> x0, blocking collectives: 95.2 us -> none  [the longest x1 21.4 us: on_device(): lax.all_gather(expand_bias, 'fsdp', axis=0, tiled=True)]
  transfers between devices with their start and end apart: 17 -> 103, of which waited for: 8 -> 29; matrix products, arithmetic and copies ran while one was open for 26% -> 8% of each run, Pallas kernels for 0% -> 18%
where the time goes in v1:
time: 592 us; the launch traced here: 588 us
  waiting for transfers between devices  215 us (36%)
  starting transfers between devices  157 us (27%)
  Pallas kernels  150 us (25%)
  local copies, waits for them, and re-layouts  37.8 us (6%)
  other arithmetic  27 us (5%)
    ppermute x103, waiting for transfers between devices, swap(): return lax.ppermute(value, axis, [(i, i ^ step) for i in range(size)])  215 us
    ppermute x103, starting transfers between devices, swap(): return lax.ppermute(value, axis, [(i, i ^ step) for i in range(size)])  157 us
    pallas_call x1, Pallas kernels, feed(): pl.pallas_call(feed_kernel, name='feed', out_shape=(shape((rows, width),...  37.7 us
    pallas_call x2, Pallas kernels, attend_back(): pl.pallas_call(attend_back_kernel, name='attend_back', out_shape=(shape((...  31.3 us
    pallas_call x2, Pallas kernels, attend(): pl.pallas_call(attend_kernel, name='attend', out_shape=tuple((shape((rows...  28.2 us
    unnamed x173, local copies, waits for them, and re-layouts  22.4 us
    pallas_call x2, Pallas kernels, project(): pl.pallas_call(project_kernel, name='project', out_shape=(shape((4 * rows...  12.1 us
    pallas_call x2, Pallas kernels, triple_grad(): pl.pallas_call(triple_grad_kernel, name='triple_grad', out_shape=shape((4...  11.9 us
  transfers between devices with their start and end apart: 103, of which 29 were waited for; matrix products, arithmetic and copies ran while one was open for 8% of the time, Pallas kernels for 18%

profile of v1, /device:TPU:1, one launch (start us, length us, event | category | flops | bytes accessed | tf_op | source)
XLA Modules:
  0.0 588.3 jit_solution(4153021827560965563)
XLA Ops:
  35.7 3.1 collective-permute-start.32
  40.9 3.0 collective-permute-start.13
  44.6 3.9 collective-permute-start.15
  51.8 10.8 %collective-permute-done.13.rest_4_.rest_12_ = bf16[128,768]{1,0:T(8,128)(2,1)S(1)} collective-permute-done((bf16[128,768]{1,0:T(8,128)(2,1)S(1)}, bf16[128,768]{1,0:T(8,128)(2,1)S(1)}, u32[]{:S(2)}, u32[]{:S(2)}) %collective-permute-start.13) | collective-permute-done | bytes 196640 | tf_op jit(solution)/shard_map/ppermute | solution.py:44
  64.5 2.8 collective-permute-start.23
  70.4 3.4 collective-permute-done.35
  75.0 3.1 collective-permute-done.12.rest_3_.rest_11_
  79.3 3.1 collective-permute-done.14.rest_5_.rest_13_
  92.0 6.1 %project.3 = (bf16[1024,768]{1,0:T(8,128)(2,1)}, bf16[1024,1024]{1,0:T(8,128)(2,1)}) custom-call(s32[4]{0:T(128)} %pad_add_fusion.ids, bf16[256,1024]{1,0:T(8,128)(2,1)} %get-tuple-element.223.t0, bf16[256,1024]{1,0:T(8,128)(2,1)} %copy-done.54, bf16[256,1024]{1,0:T(8,128)(2,1)} %collective-permute-done.24.t2, bf16[256,1024]{1,0:T(8,128)(2,1)} %copy-done.56, ...), custom_call_target="tpu_custom_call" | custom-call | flops 1610612736 | bytes 4718592 | tf_op jit(solution)/shard_map/project/pallas_call | solution.py:129
  98.1 14.0 %attend.3 = (bf16[256,256]{1,0:T(8,128)(2,1)}, bf16[256,256]{1,0:T(8,128)(2,1)}, bf16[256,256]{1,0:T(8,128)(2,1)}, bf16[256,256]{1,0:T(8,128)(2,1)}, f32[8,1024]{1,0:T(8,128)}) custom-call(bf16[1024,768]{1,0:T(8,128)(2,1)} %get-tuple-element.70.triple, f32[4,16,1024]{2,1,0:T(8,128)} %reshape.336.block_bias), custom_call_target="tpu_custom_call" | custom-call | flops 8589934592 | bytes 2097152 | tf_op jit(solution)/shard_map/attend/pallas_call | solution.py:182
  113.7 6.0 %project.2 = (bf16[1024,768]{1,0:T(8,128)(2,1)}, bf16[1024,1024]{1,0:T(8,128)(2,1)}) custom-call(s32[4]{0:T(128)} %pad_add_fusion.ids, bf16[256,1024]{1,0:T(8,128)(2,1)} %get-tuple-element.224.t0, bf16[256,1024]{1,0:T(8,128)(2,1)} %copy-done.60, bf16[256,1024]{1,0:T(8,128)(2,1)} %copy-done.51, bf16[256,1024]{1,0:T(8,128)(2,1)} %copy-done.63, ...), custom_call_target="tpu_custom_call" | custom-call | flops 1610612736 | bytes 4718592 | tf_op jit(solution)/shard_map/project/pallas_call | solution.py:129
  120.5 7.4 %collective-permute-start.28 = (bf16[256,256]{1,0:T(8,128)(2,1)}, bf16[256,256]{1,0:T(8,128)(2,1)}, u32[]{:S(2)}, u32[]{:S(2)}) collective-permute-start(bf16[256,256]{1,0:T(8,128)(2,1)} %get-tuple-element.74.rest_7_), channel_id=1, source_target_pairs={{0,24},{8,16},{16,8},{24,0},{1,25},{9,17},{17,9},{25,1},{2,26},{10... | collective-permute-start | bytes 393224 | tf_op jit(solution)/shard_map/ppermute | solution.py:44
  127.9 14.2 %attend.2 = (bf16[256,256]{1,0:T(8,128)(2,1)}, bf16[256,256]{1,0:T(8,128)(2,1)}, bf16[256,256]{1,0:T(8,128)(2,1)}, bf16[256,256]{1,0:T(8,128)(2,1)}, f32[8,1024]{1,0:T(8,128)}) custom-call(bf16[1024,768]{1,0:T(8,128)(2,1)} %get-tuple-element.65.triple, f32[4,16,1024]{2,1,0:T(8,128)} %reshape.335.block_bias), custom_call_target="tpu_custom_call" | custom-call | flops 8589934592 | bytes 2097152 | tf_op jit(solution)/shard_map/attend/pallas_call | solution.py:182
  154.4 6.9 %output_project.1 = (f32[512,1024]{1,0:T(8,128)}, bf16[512,1024]{1,0:T(8,128)(2,1)}, bf16[512,1024]{1,0:T(8,128)(2,1)}) custom-call(s32[4]{0:T(128)} %pad_add_fusion.ids, bf16[2,256,1024]{2,1,0:T(8,128)(2,1)} %bitcast.147, bf16[256,256]{1,0:T(8,128)(2,1)} %get-tuple-element.66.rest_0_.rest_4_, bf16[256,256]{1,0:T(8,128)(2,1)} %collective-permute-done.20.rest_1_, ...), custom_call_target="tpu_custom_call" | custom-call | flops 1073741824 | bytes 8388608 | tf_op jit(solution)/shard_map/output_project/pallas_call | solution.py:314
  161.6 5.9 %collective-permute-done.47.rest_10_ = bf16[256,1024]{1,0:T(8,128)(2,1)S(1)} collective-permute-done((bf16[256,1024]{1,0:T(8,128)(2,1)S(1)}, bf16[256,1024]{1,0:T(8,128)(2,1)S(1)}, u32[]{:S(2)}, u32[]{:S(2)}) %collective-permute-start.47) | collective-permute-done | bytes 524320 | tf_op jit(solution)/shard_map/ppermute | solution.py:44
  169.1 13.7 %collective-permute-done.51.rest_14_ = bf16[256,1024]{1,0:T(8,128)(2,1)S(1)} collective-permute-done((bf16[256,1024]{1,0:T(8,128)(2,1)S(1)}, bf16[256,1024]{1,0:T(8,128)(2,1)S(1)}, u32[]{:S(2)}, u32[]{:S(2)}) %collective-permute-start.51) | collective-permute-done | bytes 524320 | tf_op jit(solution)/shard_map/ppermute | solution.py:44
  183.4 6.4 %collective-permute-start.37 = (bf16[512,1024]{1,0:T(8,128)(2,1)}, bf16[512,1024]{1,0:T(8,128)(2,1)S(1)}, u32[]{:S(2)}, u32[]{:S(2)}) collective-permute-start(bf16[512,1024]{1,0:T(8,128)(2,1)} %get-tuple-element.76.h0), channel_id=1, source_target_pairs={{0,8},{8,0},{16,24},{24,16},{1,9},{9,1},{17,25},{25,17},{2,10},{10... | collective-permute-start | bytes 3145736 | tf_op jit(solution)/shard_map/ppermute | solution.py:44
  191.2 3.4 collective-permute-done.45.rest_7_
  197.0 8.8 %collective-permute-done.48.rest_11_ = bf16[256,1024]{1,0:T(8,128)(2,1)S(1)} collective-permute-done((bf16[256,1024]{1,0:T(8,128)(2,1)S(1)}, bf16[256,1024]{1,0:T(8,128)(2,1)S(1)}, u32[]{:S(2)}, u32[]{:S(2)}) %collective-permute-start.48) | collective-permute-done | bytes 524320 | tf_op jit(solution)/shard_map/ppermute | solution.py:44
  205.8 11.2 %collective-permute-done.50.rest_13_ = bf16[256,1024]{1,0:T(8,128)(2,1)S(1)} collective-permute-done((bf16[256,1024]{1,0:T(8,128)(2,1)S(1)}, bf16[256,1024]{1,0:T(8,128)(2,1)S(1)}, u32[]{:S(2)}, u32[]{:S(2)}) %collective-permute-start.50) | collective-permute-done | bytes 524320 | tf_op jit(solution)/shard_map/ppermute | solution.py:44
  217.1 11.2 %collective-permute-done.52.rest_15_ = bf16[256,1024]{1,0:T(8,128)(2,1)S(1)} collective-permute-done((bf16[256,1024]{1,0:T(8,128)(2,1)S(1)}, bf16[256,1024]{1,0:T(8,128)(2,1)S(1)}, u32[]{:S(2)}, u32[]{:S(2)}) %collective-permute-start.52) | collective-permute-done | bytes 524320 | tf_op jit(solution)/shard_map/ppermute | solution.py:44
  230.1 37.7 %feed.1 = (f32[512,1024]{1,0:T(8,128)}, bf16[512,1024]{1,0:T(8,128)(2,1)}, f32[512,1024]{1,0:T(8,128)}, bf16[512,1024]{1,0:T(8,128)(2,1)}, f32[1,2048]{1,0:T(1,1...) custom-call(s32[4]{0:T(128)} %pad_add_fusion.ids, ...), custom_call_target="tpu_custom_call" | custom-call | flops 25769803776 | bytes 27262976 | tf_op jit(solution)/shard_map/feed/pallas_call | solution.py:397
  267.8 9.8 %collective-permute-start.53 = (bf16[512,1024]{1,0:T(8,128)(2,1)}, bf16[512,1024]{1,0:T(8,128)(2,1)S(1)}, u32[]{:S(2)}, u32[]{:S(2)}) collective-permute-start(bf16[512,1024]{1,0:T(8,128)(2,1)} %get-tuple-element.78), channel_id=1, source_target_pairs={{0,8},{8,0},{16,24},{24,16},{1,9},{9,1},{17,25},{25,17},{2,10},{10... | collective-permute-start | bytes 3145736 | tf_op jit(solution)/shard_map/ppermute | solution.py:44
  282.7 8.4 %branch_back.1 = (bf16[2,256,1024]{2,1,0:T(8,128)(2,1)}, f32[512,1024]{1,0:T(8,128)}, bf16[512,1024]{1,0:T(8,128)(2,1)}, bf16[256,256]{1,0:T(8,128)(2,1)}, bf16[...) custom-call(s32[4]{0:T(128)} %pad_add_fusion.ids, ...), custom_call_target="tpu_custom_call" | custom-call | flops 1073741824 | bytes 16777216 | tf_op jit(solution)/shard_map/branch_back/pallas_call | solution.py:465
  296.1 4.3 collective-permute-done.87
  303.9 3.0 collective-permute-start.55
  308.9 15.6 %attend_back.3 = (bf16[1024,768]{1,0:T(8,128)(2,1)}, bf16[256,1024]{1,0:T(8,128)(2,1)}, bf16[256,1024]{1,0:T(8,128)(2,1)}, bf16[256,1024]{1,0:T(8,128)(2,1)}, bf16[256,1024]{1,0:T(8,128)(2,1)}) custom-call(s32[4]{0:T(128)} %pad_add_fusion.ids, bf16[1024,768]{1,0:T(8,128)(2,1)} %get-tuple-element.70.triple, f32[4,16,1024]{2,1,0:T(8,128)} %reshape.336.block_bias, ...), custom_call_target="tpu_custom_call" | custom-call | flops 21474836480 | bytes 4194304 | tf_op jit(solution)/shard_map/attend_back/pallas_call | solution.py:251
  324.5 3.4 collective-permute-start.89
  329.1 15.7 %attend_back.2 = (bf16[1024,768]{1,0:T(8,128)(2,1)}, bf16[256,1024]{1,0:T(8,128)(2,1)}, bf16[256,1024]{1,0:T(8,128)(2,1)}, bf16[256,1024]{1,0:T(8,128)(2,1)}, bf16[256,1024]{1,0:T(8,128)(2,1)}) custom-call(s32[4]{0:T(128)} %pad_add_fusion.ids, bf16[1024,768]{1,0:T(8,128)(2,1)} %get-tuple-element.65.triple, f32[4,16,1024]{2,1,0:T(8,128)} %reshape.335.block_bias, ...), custom_call_target="tpu_custom_call" | custom-call | flops 21474836480 | bytes 4194304 | tf_op jit(solution)/shard_map/attend_back/pallas_call | solution.py:251
  345.0 2.7 collective-permute-start.90
  347.8 6.0 %triple_grad.3 = bf16[4,128,768]{2,1,0:T(8,128)(2,1)} custom-call(s32[4]{0:T(128)} %get-tuple-element.203.ids, bf16[1024,1024]{1,0:T(8,128)(2,1)} %get-tuple-element.104.n0, bf16[1024,1024]{1,0:T(8,128)(2,1)} %get-tuple-element.105.n1, bf16[1024,768]{1,0:T(8,128)(2,1)} %get-tuple-element.106.d0, bf16[1024,768]{1,0:T(8,128)(2,1)} %get-tuple-element.107.d1), custom_call_target="tpu_custom_call" | custom-call | flops 1610612736 | bytes 7340032 | tf_op jit(solution)/shard_map/triple_grad/pallas_call | solution.py:523
  355.3 5.9 %triple_grad.2 = bf16[4,128,768]{2,1,0:T(8,128)(2,1)} custom-call(s32[4]{0:T(128)} %pad_add_fusion.ids, bf16[1024,1024]{1,0:T(8,128)(2,1)} %get-tuple-element.104.n0, bf16[1024,1024]{1,0:T(8,128)(2,1)} %get-tuple-element.105.n1, bf16[1024,768]{1,0:T(8,128)(2,1)} %get-tuple-element.106.d0, bf16[1024,768]{1,0:T(8,128)(2,1)} %get-tuple-element.107.d1), custom_call_target="tpu_custom_call" | custom-call | flops 1610612736 | bytes 7340032 | tf_op jit(solution)/shard_map/triple_grad/pallas_call | solution.py:523
  366.0 51.4 %collective-permute-done.72 = bf16[4,128,768]{2,1,0:T(8,128)(2,1)S(1)} collective-permute-done((bf16[4,128,768]{2,1,0:T(8,128)(2,1)}, bf16[4,128,768]{2,1,0:T(8,128)(2,1)S(1)}, u32[]{:S(2)}, u32[]{:S(2)}) %collective-permute-start.72) | collective-permute-done | bytes 786464 | tf_op jit(solution)/shard_map/ppermute | solution.py:44
  418.4 3.6 output_grad.2
  422.0 3.7 output_grad.3
  430.0 6.0 %first_back.1 = (bf16[2,256,1024]{2,1,0:T(8,128)(2,1)}, f32[1,1024]{1,0:T(1,128)}, f32[1,1024]{1,0:T(1,128)}) custom-call(bf16[2,256,1024]{2,1,0:T(8,128)(2,1)} %bitcast.148, f32[512,1024]{1,0:T(8,128)} %get-tuple-element.82.d_attended, f32[1,1024]{1,0:T(1,128)} %bitcast.180, bf16[256,1024]{1,0:T(8,128)(2,1)} %get-tuple-element.88.rest_0_, ...), custom_call_target="tpu_custom_call" | custom-call | flops 10485760 | bytes 8388608 | tf_op jit(solution)/shard_map/first_back/pallas_call | solution.py:553
  443.2 2.9 fusion.11
  453.7 9.1 %collective-permute-start.70 = (f32[8,256]{1,0:T(8,128)S(1)}, f32[8,256]{1,0:T(8,128)S(1)}, u32[]{:S(2)}, u32[]{:S(2)}) collective-permute-start(f32[8,256]{1,0:T(8,128)S(1)} %add.253), channel_id=1, source_target_pairs={{0,2},{1,3},{2,0},{3,1},{4,6},{5,7},{6,4},{7,5},{8,10},{9,11},{10,... | collective-permute-start | bytes 24584 | tf_op jit(solution)/shard_map/ppermute | solution.py:44
  464.1 2.7 collective-permute-done.70
  469.8 18.2 %collective-permute-done.82 = bf16[128,512]{1,0:T(8,128)(2,1)} collective-permute-done((bf16[128,512]{1,0:T(8,128)(2,1)}, bf16[128,512]{1,0:T(8,128)(2,1)}, u32[]{:S(2)}, u32[]{:S(2)}) %collective-permute-start.82) | collective-permute-done | bytes 131104 | tf_op jit(solution)/shard_map/ppermute | solution.py:44
  488.0 15.6 %collective-permute-start.71 = (f32[8,256]{1,0:T(8,128)S(1)}, f32[8,256]{1,0:T(8,128)S(1)}, u32[]{:S(2)}, u32[]{:S(2)}) collective-permute-start(f32[8,256]{1,0:T(8,128)S(1)} %add.254), channel_id=1, source_target_pairs={{0,4},{1,5},{2,6},{3,7},{4,0},{5,1},{6,2},{7,3},{8,12},{9,13},{10,... | collective-permute-start | bytes 24584 | tf_op jit(solution)/shard_map/ppermute | solution.py:44
  504.8 25.7 %collective-permute-done.71 = f32[8,256]{1,0:T(8,128)S(1)} collective-permute-done((f32[8,256]{1,0:T(8,128)S(1)}, f32[8,256]{1,0:T(8,128)S(1)}, u32[]{:S(2)}, u32[]{:S(2)}) %collective-permute-start.71) | collective-permute-done | bytes 8224 | tf_op jit(solution)/shard_map/ppermute | solution.py:44
  531.3 3.0 collective-permute-done.84
  537.3 3.5 collective-permute-start.85
  543.4 14.5 %collective-permute-done.98 = bf16[256,1024]{1,0:T(8,128)(2,1)S(1)} collective-permute-done((bf16[256,1024]{1,0:T(8,128)(2,1)S(1)}, bf16[256,1024]{1,0:T(8,128)(2,1)S(1)}, u32[]{:S(2)}, u32[]{:S(2)}) %collective-permute-start.98) | collective-permute-done | bytes 524320 | tf_op jit(solution)/shard_map/ppermute | solution.py:44
  560.0 3.7 collective-permute-start.77
  565.2 5.0 collective-permute-done.101
  571.4 3.9 collective-permute-start.102
  (426 shorter events, 152.5 us)
Async XLA Ops:
  5.9 21.5 %collective-permute-start.4 = (bf16[1,1152]{1,0:T(2,128)(2,1)S(1)}, bf16[1,1152]{1,0:T(2,128)(2,1)}, u32[]{:S(2)}, u32[]{:S(2)}) collective-permute-start(bf16[1,1152]{1,0:T(2,128)(2,1)S(1)} %reshape.331), channel_id=1, source_target_pairs={{0,2},{1,3},{2,0},{3,1},{4,6},{5,7},{6,4},{7,5},{8,10},{9,11},{10,... | collective-permute-start | bytes 6920 | tf_op jit(solution)/shard_map/ppermute | solution.py:44
  8.1 22.3 %collective-permute-start.6 = (bf16[1,1152]{1,0:T(2,128)(2,1)S(1)}, bf16[1,1152]{1,0:T(2,128)(2,1)}, u32[]{:S(2)}, u32[]{:S(2)}) collective-permute-start(bf16[1,1152]{1,0:T(2,128)(2,1)S(1)} %reshape.331), channel_id=1, source_target_pairs={{0,4},{1,5},{2,6},{3,7},{4,0},{5,1},{6,2},{7,3},{8,12},{9,13},{10,... | collective-permute-start | bytes 6920 | tf_op jit(solution)/shard_map/ppermute | solution.py:44
  30.8 37.6 %collective-permute-start.24 = (bf16[256,1024]{1,0:T(8,128)(2,1)}, bf16[256,1024]{1,0:T(8,128)(2,1)}, u32[]{:S(2)}, u32[]{:S(2)}) collective-permute-start(bf16[256,1024]{1,0:T(8,128)(2,1)} %get-tuple-element.223.t0), channel_id=1, source_target_pairs={{0,16},{8,24},{16,0},{24,8},{1,17},{9,25},{17,1},{25,9},{2,18},{10... | collective-permute-start | bytes 1572872 | tf_op jit(solution)/shard_map/ppermute | solution.py:44
  40.9 21.7 %collective-permute-start.13 = (bf16[128,768]{1,0:T(8,128)(2,1)S(1)}, bf16[128,768]{1,0:T(8,128)(2,1)S(1)}, u32[]{:S(2)}, u32[]{:S(2)}) collective-permute-start(bf16[128,768]{1,0:T(8,128)(2,1)S(1)} %copy.78.rest_0_.rest_8_), channel_id=1, source_target_pairs={{0,4},{1,5},{2,6},{3,7},{4,0},{5,1},{6,2},{7,3},{8,12},{9,13},{10,... | collective-permute-start | bytes 589832 | tf_op jit(solution)/shard_map/ppermute | solution.py:44
  64.5 23.3 %collective-permute-start.23 = (bf16[256,1024]{1,0:T(8,128)(2,1)}, bf16[256,1024]{1,0:T(8,128)(2,1)S(1)}, u32[]{:S(2)}, u32[]{:S(2)}) collective-permute-start(bf16[256,1024]{1,0:T(8,128)(2,1)} %get-tuple-element.223.t0), channel_id=1, source_target_pairs={{0,8},{8,0},{16,24},{24,16},{1,9},{9,1},{17,25},{25,17},{2,10},{10... | collective-permute-start | bytes 1572872 | tf_op jit(solution)/shard_map/ppermute | solution.py:44
  67.3 21.9 %collective-permute-start.1 = (bf16[256,1024]{1,0:T(8,128)(2,1)S(1)}, bf16[256,1024]{1,0:T(8,128)(2,1)S(1)}, u32[]{:S(2)}, u32[]{:S(2)}) collective-permute-start(bf16[256,1024]{1,0:T(8,128)(2,1)S(1)} %copy-done.22), channel_id=1, source_target_pairs={{0,16},{8,24},{16,0},{24,8},{1,17},{9,25},{17,1},{25,9},{2,18},{10... | collective-permute-start | bytes 1572872 | tf_op jit(solution)/shard_map/ppermute | solution.py:44
  68.4 21.6 %collective-permute-start.25 = (bf16[256,1024]{1,0:T(8,128)(2,1)}, bf16[256,1024]{1,0:T(8,128)(2,1)S(1)}, u32[]{:S(2)}, u32[]{:S(2)}) collective-permute-start(bf16[256,1024]{1,0:T(8,128)(2,1)} %collective-permute-done.24.t2), channel_id=1, source_target_pairs={{0,8},{8,0},{16,24},{24,16},{1,9},{9,1},{17,25},{25,17},{2,10},{10... | collective-permute-start | bytes 1572872 | tf_op jit(solution)/shard_map/ppermute | solution.py:44
  82.4 29.7 %collective-permute-start = (bf16[256,1024]{1,0:T(8,128)(2,1)S(1)}, bf16[256,1024]{1,0:T(8,128)(2,1)S(1)}, u32[]{:S(2)}, u32[]{:S(2)}) collective-permute-start(bf16[256,1024]{1,0:T(8,128)(2,1)S(1)} %copy-done.22), channel_id=1, source_target_pairs={{0,8},{8,0},{16,24},{24,16},{1,9},{9,1},{17,25},{25,17},{2,10},{10... | collective-permute-start | bytes 1572872 | tf_op jit(solution)/shard_map/ppermute | solution.py:44
  86.5 33.2 %collective-permute-start.40 = (bf16[128,2048]{1,0:T(8,128)(2,1)}, bf16[128,2048]{1,0:T(8,128)(2,1)S(1)}, u32[]{:S(2)}, u32[]{:S(2)}) collective-permute-start(bf16[128,2048]{1,0:T(8,128)(2,1)} %bitcast.87.rest_0_), channel_id=1, source_target_pairs={{0,2},{1,3},{2,0},{3,1},{4,6},{5,7},{6,4},{7,5},{8,10},{9,11},{10,... | collective-permute-start | bytes 1572872 | tf_op jit(solution)/shard_map/ppermute | solution.py:44
  87.8 32.7 %collective-permute-start.42 = (bf16[128,2048]{1,0:T(8,128)(2,1)}, bf16[128,2048]{1,0:T(8,128)(2,1)S(1)}, u32[]{:S(2)}, u32[]{:S(2)}) collective-permute-start(bf16[128,2048]{1,0:T(8,128)(2,1)} %bitcast.87.rest_0_), channel_id=1, source_target_pairs={{0,4},{1,5},{2,6},{3,7},{4,0},{5,1},{6,2},{7,3},{8,12},{9,13},{10,... | collective-permute-start | bytes 1572872 | tf_op jit(solution)/shard_map/ppermute | solution.py:44
  89.2 53.0 %collective-permute-start.44 = (bf16[128,2048]{1,0:T(8,128)(2,1)}, bf16[128,2048]{1,0:T(8,128)(2,1)S(1)}, u32[]{:S(2)}, u32[]{:S(2)}) collective-permute-start(bf16[128,2048]{1,0:T(8,128)(2,1)} %bitcast.87.rest_0_), channel_id=1, source_target_pairs={{0,6},{1,7},{2,4},{3,5},{4,2},{5,3},{6,0},{7,1},{8,14},{9,15},{10,... | collective-permute-start | bytes 1572872 | tf_op jit(solution)/shard_map/ppermute | solution.py:44
  90.1 22.8 %collective-permute-start.2 = (bf16[256,1024]{1,0:T(8,128)(2,1)S(1)}, bf16[256,1024]{1,0:T(8,128)(2,1)S(1)}, u32[]{:S(2)}, u32[]{:S(2)}) collective-permute-start(bf16[256,1024]{1,0:T(8,128)(2,1)S(1)} %collective-permute-done.1.t2), channel_id=1, source_target_pairs={{0,8},{8,0},{16,24},{24,16},{1,9},{9,1},{17,25},{25,17},{2,10},{10... | collective-permute-start | bytes 1572872 | tf_op jit(solution)/shard_map/ppermute | solution.py:44
  112.1 41.3 %collective-permute-start.36 = (bf16[1024,512]{1,0:T(8,128)(2,1)S(1)}, bf16[1024,512]{1,0:T(8,128)(2,1)S(1)}, u32[]{:S(2)}, u32[]{:S(2)}) collective-permute-start(bf16[1024,512]{1,0:T(8,128)(2,1)S(1)} %constant_dynamic-update-slice_fusion.rest_10_.own), channel_id=1, source_target_pairs={{0,8},{8,0},{16,24},{24,16},{1,9},{9,1},{17,25},{25,17},{2,10},{10... | collective-permute-start | bytes 3145736 | tf_op jit(solution)/shard_map/ppermute | solution.py:44
  112.9 29.4 %collective-permute-start.26 = (bf16[256,256]{1,0:T(8,128)(2,1)}, bf16[256,256]{1,0:T(8,128)(2,1)S(1)}, u32[]{:S(2)}, u32[]{:S(2)}) collective-permute-start(bf16[256,256]{1,0:T(8,128)(2,1)} %get-tuple-element.72.rest_5_), channel_id=1, source_target_pairs={{0,8},{8,0},{16,24},{24,16},{1,9},{9,1},{17,25},{25,17},{2,10},{10... | collective-permute-start | bytes 393224 | tf_op jit(solution)/shard_map/ppermute | solution.py:44
  119.7 23.7 %collective-permute-start.27 = (bf16[256,256]{1,0:T(8,128)(2,1)S(1)}, bf16[256,256]{1,0:T(8,128)(2,1)S(1)}, u32[]{:S(2)}, u32[]{:S(2)}) collective-permute-start(bf16[256,256]{1,0:T(8,128)(2,1)S(1)} %copy-done.70), channel_id=1, source_target_pairs={{0,16},{8,24},{16,0},{24,8},{1,17},{9,25},{17,1},{25,9},{2,18},{10... | collective-permute-start | bytes 393224 | tf_op jit(solution)/shard_map/ppermute | solution.py:44
  120.5 23.9 %collective-permute-start.28 = (bf16[256,256]{1,0:T(8,128)(2,1)}, bf16[256,256]{1,0:T(8,128)(2,1)}, u32[]{:S(2)}, u32[]{:S(2)}) collective-permute-start(bf16[256,256]{1,0:T(8,128)(2,1)} %get-tuple-element.74.rest_7_), channel_id=1, source_target_pairs={{0,24},{8,16},{16,8},{24,0},{1,25},{9,17},{17,9},{25,1},{2,26},{10... | collective-permute-start | bytes 393224 | tf_op jit(solution)/shard_map/ppermute | solution.py:44
  145.1 22.4 %collective-permute-start.47 = (bf16[256,1024]{1,0:T(8,128)(2,1)S(1)}, bf16[256,1024]{1,0:T(8,128)(2,1)S(1)}, u32[]{:S(2)}, u32[]{:S(2)}) collective-permute-start(bf16[256,1024]{1,0:T(8,128)(2,1)S(1)} %constant_dynamic-slice_fusion.4.rest_8_), channel_id=1, source_target_pairs={{0,2},{1,3},{2,0},{3,1},{4,6},{5,7},{6,4},{7,5},{8,10},{9,11},{10,... | collective-permute-start | bytes 1572872 | tf_op jit(solution)/shard_map/ppermute | solution.py:44
  147.3 21.1 %collective-permute-start.49 = (bf16[256,1024]{1,0:T(8,128)(2,1)S(1)}, bf16[256,1024]{1,0:T(8,128)(2,1)S(1)}, u32[]{:S(2)}, u32[]{:S(2)}) collective-permute-start(bf16[256,1024]{1,0:T(8,128)(2,1)S(1)} %constant_dynamic-slice_fusion.4.rest_8_), channel_id=1, source_target_pairs={{0,4},{1,5},{2,6},{3,7},{4,0},{5,1},{6,2},{7,3},{8,12},{9,13},{10,... | collective-permute-start | bytes 1572872 | tf_op jit(solution)/shard_map/ppermute | solution.py:44
  150.9 31.9 %collective-permute-start.51 = (bf16[256,1024]{1,0:T(8,128)(2,1)S(1)}, bf16[256,1024]{1,0:T(8,128)(2,1)S(1)}, u32[]{:S(2)}, u32[]{:S(2)}) collective-permute-start(bf16[256,1024]{1,0:T(8,128)(2,1)S(1)} %constant_dynamic-slice_fusion.4.rest_8_), channel_id=1, source_target_pairs={{0,6},{1,7},{2,4},{3,5},{4,2},{5,3},{6,0},{7,1},{8,14},{9,15},{10,... | collective-permute-start | bytes 1572872 | tf_op jit(solution)/shard_map/ppermute | solution.py:44
  153.5 29.9 %collective-permute-start.46 = (bf16[256,1024]{1,0:T(8,128)(2,1)S(1)}, bf16[256,1024]{1,0:T(8,128)(2,1)S(1)}, u32[]{:S(2)}, u32[]{:S(2)}) collective-permute-start(bf16[256,1024]{1,0:T(8,128)(2,1)S(1)} %constant_dynamic-slice_fusion.4.rest_8_), channel_id=1, source_target_pairs={{0,1},{1,0},{2,3},{3,2},{4,5},{5,4},{6,7},{7,6},{8,9},{9,8},{10,11... | collective-permute-start | bytes 1572872 | tf_op jit(solution)/shard_map/ppermute | solution.py:44
  161.4 66.9 %collective-permute-start.38 = (bf16[512,1024]{1,0:T(8,128)(2,1)S(1)}, bf16[512,1024]{1,0:T(8,128)(2,1)S(1)}, u32[]{:S(2)}, u32[]{:S(2)}) collective-permute-start(bf16[512,1024]{1,0:T(8,128)(2,1)S(1)} %bitcast.157), channel_id=1, source_target_pairs={{0,8},{8,0},{16,24},{24,16},{1,9},{9,1},{17,25},{25,17},{2,10},{10... | collective-permute-start | bytes 3145736 | tf_op jit(solution)/shard_map/ppermute | solution.py:44
  167.6 22.2 %collective-permute-start.41 = (bf16[128,2048]{1,0:T(8,128)(2,1)S(1)}, bf16[128,2048]{1,0:T(8,128)(2,1)S(1)}, u32[]{:S(2)}, u32[]{:S(2)}) collective-permute-start(bf16[128,2048]{1,0:T(8,128)(2,1)S(1)} %copy-done.42), channel_id=1, source_target_pairs={{0,1},{1,0},{2,3},{3,2},{4,5},{5,4},{6,7},{7,6},{8,9},{9,8},{10,11... | collective-permute-start | bytes 1572872 | tf_op jit(solution)/shard_map/ppermute | solution.py:44
  168.4 22.0 %collective-permute-start.43 = (bf16[128,2048]{1,0:T(8,128)(2,1)S(1)}, bf16[128,2048]{1,0:T(8,128)(2,1)S(1)}, u32[]{:S(2)}, u32[]{:S(2)}) collective-permute-start(bf16[128,2048]{1,0:T(8,128)(2,1)S(1)} %copy-done.44), channel_id=1, source_target_pairs={{0,1},{1,0},{2,3},{3,2},{4,5},{5,4},{6,7},{7,6},{8,9},{9,8},{10,11... | collective-permute-start | bytes 1572872 | tf_op jit(solution)/shard_map/ppermute | solution.py:44
  183.4 45.0 %collective-permute-start.37 = (bf16[512,1024]{1,0:T(8,128)(2,1)}, bf16[512,1024]{1,0:T(8,128)(2,1)S(1)}, u32[]{:S(2)}, u32[]{:S(2)}) collective-permute-start(bf16[512,1024]{1,0:T(8,128)(2,1)} %get-tuple-element.76.h0), channel_id=1, source_target_pairs={{0,8},{8,0},{16,24},{24,16},{1,9},{9,1},{17,25},{25,17},{2,10},{10... | collective-permute-start | bytes 3145736 | tf_op jit(solution)/shard_map/ppermute | solution.py:44
  190.4 26.7 %collective-permute-start.50 = (bf16[256,1024]{1,0:T(8,128)(2,1)S(1)}, bf16[256,1024]{1,0:T(8,128)(2,1)S(1)}, u32[]{:S(2)}, u32[]{:S(2)}) collective-permute-start(bf16[256,1024]{1,0:T(8,128)(2,1)S(1)} %collective-permute-done.49.rest_12_), channel_id=1, source_target_pairs={{0,1},{1,0},{2,3},{3,2},{4,5},{5,4},{6,7},{7,6},{8,9},{9,8},{10,11... | collective-permute-start | bytes 1572872 | tf_op jit(solution)/shard_map/ppermute | solution.py:44
  195.4 32.9 %collective-permute-start.52 = (bf16[256,1024]{1,0:T(8,128)(2,1)S(1)}, bf16[256,1024]{1,0:T(8,128)(2,1)S(1)}, u32[]{:S(2)}, u32[]{:S(2)}) collective-permute-start(bf16[256,1024]{1,0:T(8,128)(2,1)S(1)} %collective-permute-done.51.rest_14_), channel_id=1, source_target_pairs={{0,1},{1,0},{2,3},{3,2},{4,5},{5,4},{6,7},{7,6},{8,9},{9,8},{10,11... | collective-permute-start | bytes 1572872 | tf_op jit(solution)/shard_map/ppermute | solution.py:44
  301.2 52.6 %collective-permute-start.78 = (bf16[512,1024]{1,0:T(8,128)(2,1)S(1)}, bf16[512,1024]{1,0:T(8,128)(2,1)S(1)}, u32[]{:S(2)}, u32[]{:S(2)}) collective-permute-start(bf16[512,1024]{1,0:T(8,128)(2,1)S(1)} %copy-done.5), channel_id=1, source_target_pairs={{0,8},{8,0},{16,24},{24,16},{1,9},{9,1},{17,25},{25,17},{2,10},{10... | collective-permute-start | bytes 3145736 | tf_op jit(solution)/shard_map/ppermute | solution.py:44
  303.1 133.6 %collective-permute-start.91 = (bf16[4,128,2048]{2,1,0:T(8,128)(2,1)}, bf16[4,128,2048]{2,1,0:T(8,128)(2,1)S(1)}, u32[]{:S(2)}, u32[]{:S(2)}) collective-permute-start(bf16[4,128,2048]{2,1,0:T(8,128)(2,1)} %get-tuple-element.115), channel_id=1, source_target_pairs={{0,1},{1,0},{2,3},{3,2},{4,5},{5,4},{6,7},{7,6},{8,9},{9,8},{10,11... | collective-permute-start | bytes 6291464 | tf_op jit(solution)/shard_map/ppermute | solution.py:44
  306.9 21.0 %collective-permute-start.56 = (bf16[256,256]{1,0:T(8,128)(2,1)}, bf16[256,256]{1,0:T(8,128)(2,1)S(1)}, u32[]{:S(2)}, u32[]{:S(2)}) collective-permute-start(bf16[256,256]{1,0:T(8,128)(2,1)} %get-tuple-element.86), channel_id=1, source_target_pairs={{0,16},{8,24},{16,0},{24,8},{1,17},{9,25},{17,1},{25,9},{2,18},{10... | collective-permute-start | bytes 393224 | tf_op jit(solution)/shard_map/ppermute | solution.py:44
  327.9 33.9 %collective-permute-start.65 = (bf16[256,1024]{1,0:T(8,128)(2,1)}, bf16[256,1024]{1,0:T(8,128)(2,1)S(1)}, u32[]{:S(2)}, u32[]{:S(2)}) collective-permute-start(bf16[256,1024]{1,0:T(8,128)(2,1)} %get-tuple-element.100), channel_id=1, source_target_pairs={{0,8},{8,0},{16,24},{24,16},{1,9},{9,1},{17,25},{25,17},{2,10},{10... | collective-permute-start | bytes 1572872 | tf_op jit(solution)/shard_map/ppermute | solution.py:44
  353.8 88.8 %collective-permute-start.97 = (bf16[4,256,1024]{2,1,0:T(8,128)(2,1)}, bf16[4,256,1024]{2,1,0:T(8,128)(2,1)}, u32[]{:S(2)}, u32[]{:S(2)}) collective-permute-start(bf16[4,256,1024]{2,1,0:T(8,128)(2,1)} %get-tuple-element.117), channel_id=1, source_target_pairs={{0,1},{1,0},{2,3},{3,2},{4,5},{5,4},{6,7},{7,6},{8,9},{9,8},{10,11... | collective-permute-start | bytes 6291464 | tf_op jit(solution)/shard_map/ppermute | solution.py:44
  354.3 63.0 %collective-permute-start.72 = (bf16[4,128,768]{2,1,0:T(8,128)(2,1)}, bf16[4,128,768]{2,1,0:T(8,128)(2,1)S(1)}, u32[]{:S(2)}, u32[]{:S(2)}) collective-permute-start(bf16[4,128,768]{2,1,0:T(8,128)(2,1)} %triple_grad.3), channel_id=1, source_target_pairs={{0,1},{1,0},{2,3},{3,2},{4,5},{5,4},{6,7},{7,6},{8,9},{9,8},{10,11... | collective-permute-start | bytes 2359304 | tf_op jit(solution)/shard_map/ppermute | solution.py:44
  364.7 61.9 %collective-permute-start.58 = (bf16[256,1024]{1,0:T(8,128)(2,1)}, bf16[256,1024]{1,0:T(8,128)(2,1)S(1)}, u32[]{:S(2)}, u32[]{:S(2)}) collective-permute-start(bf16[256,1024]{1,0:T(8,128)(2,1)} %get-tuple-element.89), channel_id=1, source_target_pairs={{0,8},{8,0},{16,24},{24,16},{1,9},{9,1},{17,25},{25,17},{2,10},{10... | collective-permute-start | bytes 1572872 | tf_op jit(solution)/shard_map/ppermute | solution.py:44
  365.4 61.9 %collective-permute-start.66 = (bf16[256,1024]{1,0:T(8,128)(2,1)S(1)}, bf16[256,1024]{1,0:T(8,128)(2,1)S(1)}, u32[]{:S(2)}, u32[]{:S(2)}) collective-permute-start(bf16[256,1024]{1,0:T(8,128)(2,1)S(1)} %add_convert_fusion.8), channel_id=1, source_target_pairs={{0,16},{8,24},{16,0},{24,8},{1,17},{9,25},{17,1},{25,9},{2,18},{10... | collective-permute-start | bytes 1572872 | tf_op jit(solution)/shard_map/ppermute | solution.py:44
  426.6 21.0 %collective-permute-start.80 = (bf16[4,128,512]{2,1,0:T(8,128)(2,1)}, bf16[4,128,512]{2,1,0:T(8,128)(2,1)S(1)}, u32[]{:S(2)}, u32[]{:S(2)}) collective-permute-start(bf16[4,128,512]{2,1,0:T(8,128)(2,1)} %output_grad.3), channel_id=1, source_target_pairs={{0,1},{1,0},{2,3},{3,2},{4,5},{5,4},{6,7},{7,6},{8,9},{9,8},{10,11... | collective-permute-start | bytes 1572872 | tf_op jit(solution)/shard_map/ppermute | solution.py:44
  427.3 22.8 %collective-permute-start.73 = (bf16[128,768]{1,0:T(8,128)(2,1)}, bf16[128,768]{1,0:T(8,128)(2,1)}, u32[]{:S(2)}, u32[]{:S(2)}) collective-permute-start(bf16[128,768]{1,0:T(8,128)(2,1)} %get-tuple-element.217), channel_id=1, source_target_pairs={{0,2},{1,3},{2,0},{3,1},{4,6},{5,7},{6,4},{7,5},{8,10},{9,11},{10,... | collective-permute-start | bytes 589832 | tf_op jit(solution)/shard_map/ppermute | solution.py:44
  429.2 23.0 %collective-permute-start.74 = (bf16[128,768]{1,0:T(8,128)(2,1)}, bf16[128,768]{1,0:T(8,128)(2,1)}, u32[]{:S(2)}, u32[]{:S(2)}) collective-permute-start(bf16[128,768]{1,0:T(8,128)(2,1)} %get-tuple-element.219), channel_id=1, source_target_pairs={{0,4},{1,5},{2,6},{3,7},{4,0},{5,1},{6,2},{7,3},{8,12},{9,13},{10,... | collective-permute-start | bytes 589832 | tf_op jit(solution)/shard_map/ppermute | solution.py:44
  446.1 97.3 %collective-permute-start.100 = (bf16[256,1024]{1,0:T(8,128)(2,1)}, bf16[256,1024]{1,0:T(8,128)(2,1)}, u32[]{:S(2)}, u32[]{:S(2)}) collective-permute-start(bf16[256,1024]{1,0:T(8,128)(2,1)} %get-tuple-element.208), channel_id=1, source_target_pairs={{0,6},{1,7},{2,4},{3,5},{4,2},{5,3},{6,0},{7,1},{8,14},{9,15},{10,... | collective-permute-start | bytes 1572872 | tf_op jit(solution)/shard_map/ppermute | solution.py:44
  450.2 37.8 %collective-permute-start.82 = (bf16[128,512]{1,0:T(8,128)(2,1)}, bf16[128,512]{1,0:T(8,128)(2,1)}, u32[]{:S(2)}, u32[]{:S(2)}) collective-permute-start(bf16[128,512]{1,0:T(8,128)(2,1)} %get-tuple-element.222), channel_id=1, source_target_pairs={{0,4},{1,5},{2,6},{3,7},{4,0},{5,1},{6,2},{7,3},{8,12},{9,13},{10,... | collective-permute-start | bytes 393224 | tf_op jit(solution)/shard_map/ppermute | solution.py:44
  452.2 35.8 %collective-permute-start.83 = (bf16[128,512]{1,0:T(8,128)(2,1)S(1)}, bf16[128,512]{1,0:T(8,128)(2,1)}, u32[]{:S(2)}, u32[]{:S(2)}) collective-permute-start(bf16[128,512]{1,0:T(8,128)(2,1)S(1)} %get-tuple-element.221), channel_id=1, source_target_pairs={{0,6},{1,7},{2,4},{3,5},{4,2},{5,3},{6,0},{7,1},{8,14},{9,15},{10,... | collective-permute-start | bytes 393224 | tf_op jit(solution)/shard_map/ppermute | solution.py:44
  466.8 67.5 %collective-permute-start.92 = (bf16[128,2048]{1,0:T(8,128)(2,1)}, bf16[128,2048]{1,0:T(8,128)(2,1)S(1)}, u32[]{:S(2)}, u32[]{:S(2)}) collective-permute-start(bf16[128,2048]{1,0:T(8,128)(2,1)} %get-tuple-element.210), channel_id=1, source_target_pairs={{0,2},{1,3},{2,0},{3,1},{4,6},{5,7},{6,4},{7,5},{8,10},{9,11},{10,... | collective-permute-start | bytes 1572872 | tf_op jit(solution)/shard_map/ppermute | solution.py:44
  469.1 67.6 %collective-permute-start.93 = (bf16[128,2048]{1,0:T(8,128)(2,1)}, bf16[128,2048]{1,0:T(8,128)(2,1)S(1)}, u32[]{:S(2)}, u32[]{:S(2)}) collective-permute-start(bf16[128,2048]{1,0:T(8,128)(2,1)} %get-tuple-element.212), channel_id=1, source_target_pairs={{0,4},{1,5},{2,6},{3,7},{4,0},{5,1},{6,2},{7,3},{8,12},{9,13},{10,... | collective-permute-start | bytes 1572872 | tf_op jit(solution)/shard_map/ppermute | solution.py:44
  488.0 49.3 %collective-permute-start.94 = (bf16[128,2048]{1,0:T(8,128)(2,1)}, bf16[128,2048]{1,0:T(8,128)(2,1)S(1)}, u32[]{:S(2)}, u32[]{:S(2)}) collective-permute-start(bf16[128,2048]{1,0:T(8,128)(2,1)} %get-tuple-element.211), channel_id=1, source_target_pairs={{0,6},{1,7},{2,4},{3,5},{4,2},{5,3},{6,0},{7,1},{8,14},{9,15},{10,... | collective-permute-start | bytes 1572872 | tf_op jit(solution)/shard_map/ppermute | solution.py:44
  488.0 42.5 %collective-permute-start.71 = (f32[8,256]{1,0:T(8,128)S(1)}, f32[8,256]{1,0:T(8,128)S(1)}, u32[]{:S(2)}, u32[]{:S(2)}) collective-permute-start(f32[8,256]{1,0:T(8,128)S(1)} %add.254), channel_id=1, source_target_pairs={{0,4},{1,5},{2,6},{3,7},{4,0},{5,1},{6,2},{7,3},{8,12},{9,13},{10,... | collective-permute-start | bytes 24584 | tf_op jit(solution)/shard_map/ppermute | solution.py:44
  534.3 23.6 %collective-permute-start.98 = (bf16[256,1024]{1,0:T(8,128)(2,1)S(1)}, bf16[256,1024]{1,0:T(8,128)(2,1)S(1)}, u32[]{:S(2)}, u32[]{:S(2)}) collective-permute-start(bf16[256,1024]{1,0:T(8,128)(2,1)S(1)} %get-tuple-element.207), channel_id=1, source_target_pairs={{0,2},{1,3},{2,0},{3,1},{4,6},{5,7},{6,4},{7,5},{8,10},{9,11},{10,... | collective-permute-start | bytes 1572872 | tf_op jit(solution)/shard_map/ppermute | solution.py:44
  534.4 23.6 %collective-permute-start.99 = (bf16[256,1024]{1,0:T(8,128)(2,1)S(1)}, bf16[256,1024]{1,0:T(8,128)(2,1)S(1)}, u32[]{:S(2)}, u32[]{:S(2)}) collective-permute-start(bf16[256,1024]{1,0:T(8,128)(2,1)S(1)} %get-tuple-element.209), channel_id=1, source_target_pairs={{0,4},{1,5},{2,6},{3,7},{4,0},{5,1},{6,2},{7,3},{8,12},{9,13},{10,... | collective-permute-start | bytes 1572872 | tf_op jit(solution)/shard_map/ppermute | solution.py:44
  537.3 38.0 %collective-permute-start.85 = (f32[128,512]{1,0:T(8,128)S(1)}, f32[128,512]{1,0:T(8,128)S(1)}, u32[]{:S(2)}, u32[]{:S(2)}) collective-permute-start(f32[128,512]{1,0:T(8,128)S(1)} %convert_add_fusion.6), channel_id=1, source_target_pairs={{0,8},{8,0},{16,24},{24,16},{1,9},{9,1},{17,25},{25,17},{2,10},{10... | collective-permute-start | bytes 786440 | tf_op jit(solution)/shard_map/ppermute | solution.py:44
  542.4 21.3 %collective-permute-start.95 = (bf16[128,2048]{1,0:T(8,128)(2,1)S(1)}, bf16[128,2048]{1,0:T(8,128)(2,1)S(1)}, u32[]{:S(2)}, u32[]{:S(2)}) collective-permute-start(bf16[128,2048]{1,0:T(8,128)(2,1)S(1)} %fusion.5), channel_id=1, source_target_pairs={{0,16},{8,24},{16,0},{24,8},{1,17},{9,25},{17,1},{25,9},{2,18},{10... | collective-permute-start | bytes 1572872 | tf_op jit(solution)/shard_map/ppermute | solution.py:44
  (132 other events, 1841.8 us)

commit v2 on v1

--- a/solution.py
+++ b/solution.py
@@ -42,16 +42,6 @@
 def swap(value, axis, step):
     size = lax.axis_size(axis)
     return lax.ppermute(value, axis, [(i, i ^ step) for i in range(size)])
-
-
-def gather_rows(piece):
-    size = lax.axis_size("fsdp")
-    if size == 8:
-        line = [piece] + [swap(piece, "fsdp", 2 * k) for k in range(1, 4)]
-        return [block for mine in line for block in (mine, swap(mine, "fsdp", 1))]
-    whole = lax.all_gather(piece, "fsdp", axis=0, tiled=True)
-    rows = whole.shape[0] // 8
-    return [whole[(1 ^ j) * rows : (1 ^ j) * rows + rows] for j in range(8)]
 
 
 def place_id():
@@ -98,80 +88,71 @@
     return inverse * (scaled - first - unit * second)
 
 
-def fetch(pieces, target, semaphores, base, rows):
-    copies = []
-    for j in range(8):
-        start = pl.multiple_of((base ^ j) * rows, rows)
-        copies.append(
-            pltpu.make_async_copy(pieces[j], target.at[pl.ds(start, rows), :], semaphores.at[j])
-        )
-        copies[-1].start()
-    return copies
-
-
-def project_kernel(ids, t0, t1, t2, t3, gain, bias, *rest):
-    pieces, (triple, normed), (held, semaphores) = rest[:8], rest[8:10], rest[10:]
-    copies = fetch(pieces, held, semaphores, ids[0], pieces[0].shape[0])
+def normalize(source, gain, bias):
+    unit, _ = norm_parts(source.astype(F32))
+    return (unit * gain + bias).astype(BF16)
+
+
+def project_kernel(t0, t1, t2, t3, gain, bias, weight, triple, normed):
     rows = t0.shape[0]
     for place, part in enumerate((t0, t1, t2, t3)):
-        unit, _ = norm_parts(part[...].astype(F32))
-        normed[place * rows : (place + 1) * rows, :] = (unit * gain[...] + bias[...]).astype(BF16)
-    for copy in copies:
-        copy.wait()
-    for place in range(4):
-        block = normed[place * rows : (place + 1) * rows, :]
-        triple[place * rows : (place + 1) * rows, :] = dot(block, held[...]).astype(BF16)
-
-
-def project(ids, parts, gain, bias, pieces):
+        span = slice(place * rows, (place + 1) * rows)
+        normed[span, :] = normalize(part[...], gain[...], bias[...])
+        triple[span, :] = dot(normed[span, :], weight[...]).astype(BF16)
+
+
+def project(parts, gain, bias, weight):
     rows, width = parts[0].shape
-    columns = pieces[0].shape[1]
+    columns = weight.shape[1]
     return pl.pallas_call(
         project_kernel,
         name="project",
         out_shape=(shape((4 * rows, columns), BF16), shape((4 * rows, width), BF16)),
-        in_specs=[SM] + [VM] * 6 + [ANY] * 8,
+        in_specs=[VM] * 7,
         out_specs=(VM, VM),
-        scratch_shapes=[pltpu.VMEM((width, columns), BF16), pltpu.SemaphoreType.DMA((8,))],
         compiler_params=params(),
         cost_estimate=cost(8 * rows * width * columns, 12 * rows * width + 2 * width * columns),
-    )(ids, *parts, gain, bias, *pieces)
+    )(*parts, gain, bias, weight)
 
 
 def head_mask(rows):
     return lax.broadcasted_iota(jnp.int32, (rows, 2 * HEAD_DIM), 1) // HEAD_DIM
 
 
-def attend_kernel(triple, block_bias, m0, m1, m2, m3, lse):
-    outs = (m0, m1, m2, m3)
+def attend_body(triple, block_bias, mixed, lse):
     length = triple.shape[0]
     width = triple.shape[1] // 3
     rows = length // 4
     blocks = length // BLOCK
-    lse[...] = jnp.zeros_like(lse)
     for pair in range(width // 128):
         keys = triple[:, width + pair * 128 : width + pair * 128 + 128]
         values = triple[:, 2 * width + pair * 128 : 2 * width + pair * 128 + 128]
         values_t = values.astype(F32).T.astype(BF16)
-        for place in range(4):
-            span = slice(place * rows, (place + 1) * rows)
-            queries = triple[span, pair * 128 : pair * 128 + 128] * jnp.asarray(0.125, BF16)
+
+        def step(place, carry):
+            start = pl.multiple_of(place * rows, rows)
+            queries = triple[pl.ds(start, rows), pair * 128 : pair * 128 + 128]
+            queries = queries * jnp.asarray(0.125, BF16)
             side = head_mask(rows)
             halves = []
             for which in range(2):
                 head = 2 * pair + which
                 one = jnp.where(side == which, queries, jnp.zeros_like(queries))
                 scores = dot(keys, one, NT)
-                scores = scores.reshape(blocks, BLOCK, rows) + block_bias[head, :, span][:, None, :]
+                shift = block_bias[head, :, pl.ds(start, rows)]
+                scores = scores.reshape(blocks, BLOCK, rows) + shift[:, None, :]
                 peak = jnp.max(jnp.max(scores, axis=0), axis=0, keepdims=True)
                 powered = jnp.exp(scores - peak[None])
                 total = jnp.sum(jnp.sum(powered, axis=0), axis=0, keepdims=True)
-                lse[head : head + 1, span] = peak + jnp.log(total)
+                lse[head : head + 1, pl.ds(start, rows)] = peak + jnp.log(total)
                 low = powered.astype(BF16).reshape(length, rows)
                 part = dot(values_t[which * HEAD_DIM : (which + 1) * HEAD_DIM, :], low)
                 halves.append(part / total)
             joined = jnp.concatenate(halves, axis=0)
-            outs[place][:, pair * 128 : pair * 128 + 128] = joined.T.astype(BF16)
+            mixed[place, :, pair * 128 : pair * 128 + 128] = joined.T.astype(BF16)
+            return carry
+
+        lax.fori_loop(0, 4, step, 0)
 
 
 def attend(triple, block_bias):
@@ -180,11 +161,11 @@
     heads = width // HEAD_DIM
     rows = length // 4
     return pl.pallas_call(
-        attend_kernel,
+        attend_body,
         name="attend",
-        out_shape=tuple(shape((rows, width), BF16) for _ in range(4)) + (shape((8, length), F32),),
+        out_shape=(shape((4, rows, width), BF16), shape((8, length), F32)),
         in_specs=[VM, VM],
-        out_specs=(VM,) * 5,
+        out_specs=(VM, VM),
         compiler_params=params(),
         cost_estimate=cost(
             32 * heads * length * length * HEAD_DIM, 8 * length * width, heads * length * length
@@ -192,11 +173,7 @@
     )(triple, block_bias)
 
 
-def attend_back_kernel(ids, triple, block_bias, lse, *rest):
-    grads, mixed, pieces = rest[:4], rest[4:8], rest[8:16]
-    d_triple, n0, n1, n2, n3 = rest[16:21]
-    held, semaphores, key_total, value_total = rest[21:]
-    copies = fetch(pieces, held, semaphores, ids[0], pieces[0].shape[0])
+def attend_back_body(triple, block_bias, lse, grads, mixed, d_triple, key_total, value_total):
     length = triple.shape[0]
     width = triple.shape[1] // 3
     rows = length // 4
@@ -208,11 +185,12 @@
         keys_t = keys.astype(F32).T.astype(BF16)
         key_total[...] = jnp.zeros_like(key_total)
         value_total[...] = jnp.zeros_like(value_total)
-        for place in range(4):
-            span = slice(place * rows, (place + 1) * rows)
-            queries = triple[span, lanes] * jnp.asarray(0.125, BF16)
-            grad = grads[place][:, lanes]
-            product = (grad.astype(F32) * mixed[place][:, lanes].astype(F32)).T
+
+        def step(place, carry):
+            start = pl.multiple_of(place * rows, rows)
+            queries = triple[pl.ds(start, rows), lanes] * jnp.asarray(0.125, BF16)
+            grad = grads[place, :, lanes]
+            product = (grad.astype(F32) * mixed[place, :, lanes].astype(F32)).T
             side = head_mask(rows)
             halves = []
             for which in range(2):
@@ -223,7 +201,7 @@
                     product[which * HEAD_DIM : (which + 1) * HEAD_DIM, :], axis=0, keepdims=True
                 )
                 scores = dot(keys, one, NT)
-                shift = block_bias[head, :, span] - lse[head : head + 1, span]
+                shift = block_bias[head, :, pl.ds(start, rows)] - lse[head : head + 1, pl.ds(start, rows)]
                 exact = jnp.exp(scores.reshape(blocks, BLOCK, rows) + shift[:, None, :])
                 exact = exact.reshape(length, rows)
                 value_total[...] += dot(exact.astype(BF16), one_grad)
@@ -232,18 +210,27 @@
                 key_total[...] += dot(d_scores, one)
                 halves.append(dot(keys_t[which * HEAD_DIM : (which + 1) * HEAD_DIM, :], d_scores))
             joined = jnp.concatenate(halves, axis=0) * 0.125
-            d_triple[span, lanes] = joined.T.astype(BF16)
+            d_triple[pl.ds(start, rows), lanes] = joined.T.astype(BF16)
+            return carry
+
+        lax.fori_loop(0, 4, step, 0)
         d_triple[:, width + pair * 128 : width + pair * 128 + 128] = key_total[...].astype(BF16)
         d_triple[:, 2 * width + pair * 128 : 2 * width + pair * 128 + 128] = value_total[
             ...
         ].astype(BF16)
-    for copy in copies:
-        copy.wait()
-    for place, out in enumerate((n0, n1, n2, n3)):
-        out[...] = dot(d_triple[place * rows : (place + 1) * rows, :], held[...], NT).astype(BF16)
-
-
-def attend_back(ids, triple, block_bias, lse, grads, mixed, pieces, width_all):
+
+
+def attend_back_kernel(triple, block_bias, lse, g0, g1, g2, g3, mixed, weight, d_triple, norm_grad, grads, key_total, value_total):
+    rows = g0.shape[0]
+    for place, part in enumerate((g0, g1, g2, g3)):
+        grads[place] = part[...]
+    attend_back_body(triple, block_bias, lse, grads, mixed, d_triple, key_total, value_total)
+    for place in range(4):
+        part = dot(d_triple[place * rows : (place + 1) * rows, :], weight[...], NT)
+        norm_grad[place] = part.astype(BF16)
+
+
+def attend_back(triple, block_bias, lse, grads, mixed, weight):
     length, columns = triple.shape
     width = columns // 3
     heads = width // HEAD_DIM
@@ -251,13 +238,11 @@
     return pl.pallas_call(
         attend_back_kernel,
         name="attend_back",
-        out_shape=(shape((length, columns), BF16),)
-        + tuple(shape((rows, width_all), BF16) for _ in range(4)),
-        in_specs=[SM] + [VM] * 11 + [ANY] * 8,
-        out_specs=(VM,) * 5,
+        out_shape=(shape((length, columns), BF16), shape((4, rows, weight.shape[0]), BF16)),
+        in_specs=[VM] * 9,
+        out_specs=(VM,) * 2,
         scratch_shapes=[
-            pltpu.VMEM((width_all, columns), BF16),
-            pltpu.SemaphoreType.DMA((8,)),
+            pltpu.VMEM((4, rows, width), BF16),
             pltpu.VMEM((length, 128), F32),
             pltpu.VMEM((length, 128), F32),
         ],
@@ -265,69 +250,30 @@
         cost_estimate=cost(
             80 * heads * length * length * HEAD_DIM, 16 * length * width, heads * length * length
         ),
-    )(ids, triple, block_bias, lse, *grads, *mixed, *pieces)
-
-
-def fetch_output(ids, own, other, held, semaphores):
-    copies = []
-    rows = own.shape[0] // 8
-    half = own.shape[1]
-    for j in range(8):
-        block = ids[0] ^ j
-        start = pl.multiple_of(((block // 2) ^ ids[1]) * (2 * rows) + (block % 2) * rows, rows)
-        for side, source in enumerate((own, other)):
-            column = pl.multiple_of((ids[2] ^ side) * half, half)
-            copies.append(
-                pltpu.make_async_copy(
-                    source.at[pl.ds(j * rows, rows), :],
-                    held.at[pl.ds(start, rows), pl.ds(column, half)],
-                    semaphores.at[2 * j + side],
-                )
-            )
-            copies[-1].start()
-    return copies
-
-
-def output_kernel(ids, tokens, *rest):
-    mixed, (gain, bias, own, other) = rest[:8], rest[8:12]
-    attended, normed, joined, held, semaphores = rest[12:]
-    copies = fetch_output(ids, own, other, held, semaphores)
-    rows, width = mixed[0].shape
-    for micro in range(2):
-        for place in range(4):
-            joined[micro * rows : (micro + 1) * rows, place * width : (place + 1) * width] = mixed[
-                4 * micro + place
-            ][...]
-    for copy in copies:
-        copy.wait()
+    )(triple, block_bias, lse, *grads, mixed, weight)
+
+
+def output_kernel(tokens, joined, gain, bias, weight, attended, normed):
+    rows = tokens.shape[1]
     for micro in range(2):
         span = slice(micro * rows, (micro + 1) * rows)
-        value = tokens[micro].astype(F32) + dot(joined[span, :], held[...])
+        value = tokens[micro].astype(F32) + dot(joined[span, :], weight[...])
         attended[span, :] = value
-        unit, _ = norm_parts(value)
-        normed[span, :] = (unit * gain[...] + bias[...]).astype(BF16)
-
-
-def output_project(ids, tokens, mixed, gain, bias, own, other):
+        normed[span, :] = normalize(value, gain[...], bias[...])
+
+
+def output_project(tokens, joined, gain, bias, weight):
     micro, rows, width = tokens.shape
     total = micro * rows
     return pl.pallas_call(
         output_kernel,
         name="output_project",
-        out_shape=(
-            shape((total, width), F32),
-            shape((total, width), BF16),
-            shape((total, width), BF16),
-        ),
-        in_specs=[SM] + [VM] * 11 + [ANY] * 2,
-        out_specs=(VM, VM, VM),
-        scratch_shapes=[
-            pltpu.VMEM((width, width), BF16),
-            pltpu.SemaphoreType.DMA((16,)),
-        ],
+        out_shape=(shape((total, width), F32), shape((total, width), BF16)),
+        in_specs=[VM] * 5,
+        out_specs=(VM, VM),
         compiler_params=params(),
         cost_estimate=cost(2 * total * width * width, 12 * total * width + 2 * width * width),
-    )(ids, tokens, *mixed, gain, bias, own, other)
+    )(tokens, joined, gain, bias, weight)
 
 
 CURVE = 0.7978845608028654
@@ -335,15 +281,14 @@
 
 
 def feed_kernel(ids, h0, h1, c0, c1, shift, *rest):
-    expand, shrink = rest[:8], rest[8:16]
-    own_out, other_out, own_hidden, other_hidden, bias_grad = rest[16:21]
-    shrink_sent, shrink_kept, expand_sent, expand_kept = rest[21:25]
-    expand_held, hidden, tangent, hidden_t, out_total, hidden_total, semaphores = rest[25:]
+    expand_held, shrink_held = rest[:2]
+    own_out, other_out, own_hidden, other_hidden, bias_grad = rest[2:7]
+    shrink_sent, shrink_kept, expand_sent, expand_kept = rest[7:11]
+    hidden, tangent, hidden_t, out_total, hidden_total = rest[11:]
     base = ids[0]
-    copies = fetch(expand, expand_held, semaphores, base, expand[0].shape[0])
     rows, width = h0.shape
-    tile = shrink[0].shape[0]
-    deep = expand[0].shape[0]
+    tile = shrink_held.shape[0] // 8
+    deep = width // 8
     hidden[:rows, :] = h0[...]
     hidden[rows:, :] = h1[...]
     tangent[:rows, :] = c0[...]
@@ -353,12 +298,10 @@
         hidden_t[j * deep : (j + 1) * deep, :] = (
             hidden[:, pl.ds(source, deep)].astype(F32).T.astype(BF16)
         )
-    for copy in copies:
-        copy.wait()
     for step, j in enumerate((1, 3, 5, 7, 0, 2, 4, 6)):
         column = pl.multiple_of((base ^ j) * tile, tile)
         up = expand_held[:, pl.ds(column, tile)]
-        down = shrink[j][...]
+        down = shrink_held[pl.ds(column, tile), :]
         before = dot(hidden[...], up) + shift[:, pl.ds(column, tile)]
         d_active = dot(tangent[...], down, NT)
         square = before * before
@@ -392,8 +335,8 @@
 
 def feed(ids, hidden, tangent, shift, expand, shrink):
     rows, width = hidden[0].shape
-    deep, wide = expand[0].shape
-    tile = shrink[0].shape[0]
+    wide = expand.shape[1]
+    deep, tile = width // 8, wide // 8
     return pl.pallas_call(
         feed_kernel,
         name="feed",
@@ -408,28 +351,25 @@
             shape((4, deep, wide), BF16),
             shape((4, deep, wide), BF16),
         ),
-        in_specs=[SM] + [VM] * 5 + [ANY] * 8 + [VM] * 8,
+        in_specs=[SM] + [VM] * 7,
         out_specs=(VM,) * 9,
         scratch_shapes=[
-            pltpu.VMEM((width, wide), BF16),
             pltpu.VMEM((2 * rows, width), BF16),
             pltpu.VMEM((2 * rows, width), BF16),
             pltpu.VMEM((width, 2 * rows), BF16),
             pltpu.VMEM((2 * rows, width), F32),
             pltpu.VMEM((2 * rows, width), F32),
-            pltpu.SemaphoreType.DMA((8,)),
         ],
         compiler_params=params(60),
         cost_estimate=cost(24 * rows * width * wide, 8 * width * wide + 20 * rows * width, 2 * rows * wide),
-    )(ids, *hidden, *tangent, shift, *expand, *shrink)
+    )(ids, *hidden, *tangent, shift, expand, shrink)
 
 
 def branch_kernel(
-    ids, attended, own_hidden, came_hidden, tangent, own_out, came_out, gain, shift, own, other, *rest
+    ids, attended, own_hidden, came_hidden, tangent, own_out, came_out, gain, shift, weight, *rest
 ):
     result, d_attended, d_branch = rest[:3]
-    grads, (gain_grad, bias_grad, shift_grad), (held, semaphores) = rest[3:11], rest[11:14], rest[14:]
-    copies = fetch_output(ids, own, other, held, semaphores)
+    grads, (gain_grad, bias_grad, shift_grad) = rest[3:11], rest[11:14]
     rows = tangent.shape[1]
     width = gain.shape[1] // 4
     gain_total = bias_total = shift_total = 0.0
@@ -450,15 +390,14 @@
     gain_grad[...] = gain_total
     bias_grad[...] = bias_total
     shift_grad[...] = shift_total
-    for copy in copies:
-        copy.wait()
     for micro in range(2):
-        mixed = dot(d_branch[micro * rows : (micro + 1) * rows, :], held[...], NT).astype(BF16)
         for place in range(4):
-            grads[4 * micro + place][...] = mixed[:, place * width : (place + 1) * width]
-
-
-def branch_back(ids, attended, own_hidden, came_hidden, tangent, own_out, came_out, gain, shift, own, other):
+            start = pl.multiple_of((ids[1] ^ place) * width, width)
+            part = dot(d_branch[micro * rows : (micro + 1) * rows, :], weight[pl.ds(start, width), :], NT)
+            grads[4 * micro + place][...] = part.astype(BF16)
+
+
+def branch_back(ids, attended, own_hidden, came_hidden, tangent, own_out, came_out, gain, shift, weight):
     micro, rows, width = tangent.shape
     total = micro * rows
     row = shape((1, width), F32)
@@ -472,12 +411,11 @@
         )
         + tuple(shape((rows, width // 4), BF16) for _ in range(8))
         + (row, row, row),
-        in_specs=[SM] + [VM] * 8 + [ANY] * 2,
+        in_specs=[SM] + [VM] * 9,
         out_specs=(VM,) * 14,
-        scratch_shapes=[pltpu.VMEM((width, width), BF16), pltpu.SemaphoreType.DMA((16,))],
         compiler_params=params(),
         cost_estimate=cost(2 * total * width * width, 32 * total * width),
-    )(ids, attended, own_hidden, came_hidden, tangent, own_out, came_out, gain, shift, own, other)
+    )(ids, attended, own_hidden, came_hidden, tangent, own_out, came_out, gain, shift, weight)
 
 
 def output_grad_kernel(ids, own_mixed, other_mixed, own_branch, other_branch, out):
@@ -487,11 +425,9 @@
     column = pl.multiple_of(ids[2] * half, half)
     right = own_branch[:, pl.ds(column, half)]
     for k in range(4):
-        block = ids[0] ^ (2 * k + ids[3])
-        first = ((block // 2) ^ ids[1]) * (2 * rows) + (block % 2) * rows
-        second = ((block // 2) ^ ids[1] ^ 1) * (2 * rows) + (block % 2) * rows
-        part = dot(own_mixed[:, pl.ds(pl.multiple_of(first, rows), rows)], right, TN)
-        part += dot(other_mixed[:, pl.ds(pl.multiple_of(second, rows), rows)], other_branch[...], TN)
+        start = pl.multiple_of((ids[0] ^ (2 * k + ids[3])) * rows, rows)
+        part = dot(own_mixed[:, pl.ds(start, rows)], right, TN)
+        part += dot(other_mixed[:, pl.ds(start, rows)], other_branch[...], TN)
         out[k] = part.astype(BF16)
 
 
@@ -559,6 +495,297 @@
         compiler_params=params(),
         cost_estimate=cost(20 * micro * rows * width, 16 * micro * rows * width),
     )(tokens, d_attended, gain, *parts)
+
+
+def flip(index, bits):
+    out, bit = index, 1
+    while bit <= bits:
+        if bits & bit:
+            out = out + bit * (1 - 2 * lax.rem(lax.div(index, jnp.int32(bit)), jnp.int32(2)))
+        bit *= 2
+    return out
+
+
+class Moves:
+    def __init__(self, send, recv):
+        self.send, self.recv, self.started = send, recv, []
+        self.place = {"ctx": lax.axis_index("ctx"), "fsdp": lax.axis_index("fsdp")}
+
+    def greet(self):
+        barrier = pltpu.get_barrier_semaphore()
+        partners = [("ctx", 1), ("ctx", 2), ("ctx", 3), ("fsdp", 1), ("fsdp", 2), ("fsdp", 4), ("fsdp", 6)]
+        for axis, bits in partners:
+            pl.semaphore_signal(
+                barrier,
+                inc=1,
+                device_id={axis: flip(self.place[axis], bits)},
+                device_id_type=pl.DeviceIdType.MESH,
+            )
+        pl.semaphore_wait(barrier, len(partners))
+
+    def go(self, source, target, axis, bits):
+        slot = len(self.started)
+        move = pltpu.make_async_remote_copy(
+            src_ref=source,
+            dst_ref=target,
+            send_sem=self.send.at[slot],
+            recv_sem=self.recv.at[slot],
+            device_id={axis: flip(self.place[axis], bits)},
+            device_id_type=pl.DeviceIdType.MESH,
+        )
+        move.start()
+        self.started.append(move)
+        return move
+
+    def close(self):
+        for move in self.started:
+            move.wait_send()
+
+
+class Gather:
+    def __init__(self, moves, part, view, local):
+        self.moves, self.view = moves, view
+        me = moves.place["fsdp"]
+        self.along = [moves.go(part, view(me), "fsdp", 2 * k) for k in range(1, 4)]
+        self.across = [moves.go(part, view(me), "fsdp", 1)]
+        self.own = pltpu.make_async_copy(part, view(me), local)
+        self.own.start()
+
+    def forward(self):
+        me = self.moves.place["fsdp"]
+        for k in range(1, 4):
+            self.along[k - 1].wait_recv()
+            block = self.view(flip(me, 2 * k))
+            self.across.append(self.moves.go(block, block, "fsdp", 1))
+
+    def finish(self):
+        for move in self.across:
+            move.wait_recv()
+        self.own.wait()
+
+
+FORWARD_MOVES = 6 * 7 + 7 + 6 + 3 + 1 + 1 + 6 + 2
+
+
+def row_view(ref, rows, columns=slice(None)):
+    return lambda index: ref.at[pl.ds(pl.multiple_of(index * rows, rows), rows), columns]
+
+
+def forward_kernel(
+    global_ids,
+    tokens,
+    small,
+    picks,
+    triple_part,
+    output_part,
+    expand_part,
+    shrink_part,
+    tangent,
+    small_all,
+    triple_out,
+    output_out,
+    expand_all,
+    shrink_all,
+    tangent_other,
+    triple,
+    normed,
+    block_bias,
+    lse,
+    mixed,
+    joined_out,
+    mixed_other,
+    attended,
+    hidden,
+    hidden_other,
+    parts,
+    small_held,
+    picks_held,
+    triple_held,
+    output_held,
+    joined,
+    hidden_held,
+    send,
+    recv,
+    local,
+):
+    moves = Moves(send, recv)
+    rank, me = moves.place["ctx"], moves.place["fsdp"]
+    core = lax.rem(rank, jnp.int32(2))
+    micro, rows, width = tokens.shape
+    half = width // 2
+    quarter = width // 4
+    shard = triple_part.shape[0]
+    wide = expand_part.shape[1]
+    deep = shrink_part.shape[0]
+    moves.greet()
+
+    small_gather = Gather(moves, small, lambda index: small_held.at[index], local.at[0])
+    near = [moves.go(tokens.at[0], parts.at[0, 1], "ctx", 1)]
+    far = [moves.go(tokens.at[0], parts.at[0, 2], "ctx", 2)]
+    triple_gather = Gather(moves, triple_part, row_view(triple_held, shard), local.at[1])
+    picked = [moves.go(picks.at[p], picks_held.at[p], "ctx", p) for p in range(1, 4)]
+    near.append(moves.go(tokens.at[1], parts.at[1, 1], "ctx", 1))
+    far.append(moves.go(tokens.at[1], parts.at[1, 2], "ctx", 2))
+    small_gather.forward()
+    triple_gather.forward()
+    output_gather = Gather(
+        moves, output_part, row_view(output_held, shard, pl.ds(core * half, half)), local.at[2]
+    )
+    cut = wide // 2
+    chunks = [
+        (shrink_part.at[: deep // 2, :], lambda i: shrink_all.at[pl.ds(pl.multiple_of(i * deep, deep), deep // 2), :]),
+        (expand_part.at[:, :cut], row_view(expand_all, shard, slice(0, cut))),
+        (
+            shrink_part.at[deep // 2 :, :],
+            lambda i: shrink_all.at[pl.ds(pl.multiple_of(i * deep + deep // 2, deep // 2), deep // 2), :],
+        ),
+        (expand_part.at[:, cut:], row_view(expand_all, shard, slice(cut, wide))),
+    ]
+    gathers = [Gather(moves, *chunks[0], local.at[3])]
+    tangent_move = moves.go(tangent, tangent_other, "ctx", 1)
+
+    for move in picked:
+        move.wait_recv()
+    count = block_bias.shape[2]
+    each = count // 4
+    ranks = [flip(rank, p) if p else rank for p in range(4)]
+    key_row = lax.broadcasted_iota(jnp.int32, (count, rows), 0)
+    key_place = key_row // each
+    key_rank = ranks[0]
+    for p in range(1, 4):
+        key_rank = jnp.where(key_place == p, ranks[p], key_rank)
+    key_block = key_rank * each + key_row % each
+    lane = lax.broadcasted_iota(jnp.int32, (count, rows), 1) // BLOCK
+    for step in range(micro):
+        first, second = global_ids[step, 0], global_ids[step, 1]
+        key_global = (key_block == first) | (key_block == second)
+        for p in range(4):
+            source = picks.at[0] if p == 0 else picks_held.at[p]
+            query_block = ranks[p] * each + lane
+            base = key_global | (jnp.abs(query_block - key_block) <= 1)
+            base = base | (query_block == first) | (query_block == second)
+            for head in range(block_bias.shape[1]):
+                hit = base
+                for pick in range(3):
+                    hit = hit | (source[step, head, pick : pick + 1, :] == key_block)
+                block_bias[step, head, :, p * rows : (p + 1) * rows] = jnp.where(hit, 0.0, -1e30)
+
+    small_gather.finish()
+    small_all[...] = small_held[...]
+
+    def vector(line):
+        return jnp.concatenate([small_held[b, line : line + 1, :] for b in range(8)], axis=1)
+
+    gain_one, bias_one, gain_two, bias_two = (vector(line) for line in range(4))
+
+    for step in range(micro):
+        far[step].wait_recv()
+        near.append(moves.go(parts.at[step, 2], parts.at[step, 3], "ctx", 1))
+    mixed_moves = []
+    for step in range(micro):
+        near[step].wait_recv()
+        near[2 + step].wait_recv()
+        for p in range(4):
+            source = tokens[step] if p == 0 else parts[step, p]
+            normed[step, p * rows : (p + 1) * rows, :] = normalize(source, gain_one, bias_one)
+        if step == 0:
+            triple_gather.finish()
+        for p in range(4):
+            span = slice(p * rows, (p + 1) * rows)
+            triple[step, span, :] = dot(normed[step, span, :], triple_held[...]).astype(BF16)
+        if step == 0:
+            output_gather.forward()
+            gathers.append(Gather(moves, *chunks[1], local.at[4]))
+        else:
+            output_gather.finish()
+            piece = output_held.at[:, pl.ds(core * half, half)]
+            output_move = moves.go(piece, piece, "ctx", 1)
+            gathers[1].forward()
+            gathers.append(Gather(moves, *chunks[3], local.at[6]))
+        attend_body(triple.at[step], block_bias.at[step], mixed.at[step], lse.at[step])
+        own = pl.ds(pl.multiple_of(rank * quarter, quarter), quarter)
+        span = slice(step * rows, (step + 1) * rows)
+        joined[span, own] = mixed[step, 0]
+        for p in range(1, 4):
+            mixed_moves.append(moves.go(mixed.at[step, p], joined.at[span, own], "ctx", p))
+        if step == 0:
+            gathers[0].forward()
+            gathers.append(Gather(moves, *chunks[2], local.at[5]))
+    output_move.wait_recv()
+    for move in mixed_moves:
+        move.wait_recv()
+    keep = [
+        pltpu.make_async_copy(triple_held, triple_out, local.at[7]),
+        pltpu.make_async_copy(output_held, output_out, local.at[8]),
+    ]
+    for copy in keep:
+        copy.start()
+    output_kernel(tokens, joined, gain_two, bias_two, output_held, attended, hidden_held)
+    last = [
+        moves.go(hidden_held, hidden_other, "ctx", 1),
+        moves.go(joined, mixed_other, "ctx", 1),
+    ]
+    hidden[...] = hidden_held[...]
+    joined_out[...] = joined[...]
+    gathers[2].forward()
+    gathers[3].forward()
+    for gather in gathers:
+        gather.finish()
+    for move in [tangent_move] + last:
+        move.wait_recv()
+    for copy in keep:
+        copy.wait()
+    moves.close()
+
+
+def forward_together(global_ids, tokens, small, picks, triple_part, output_part, expand_part, shrink_part, tangent):
+    micro, rows, width = tokens.shape
+    total = micro * rows
+    columns = triple_part.shape[1]
+    wide = expand_part.shape[1]
+    length = 4 * rows
+    heads = picks.shape[2]
+    outs = (
+        (VM, (8,) + small.shape, F32),
+        (ANY, (width, columns), BF16),
+        (ANY, (width, width), BF16),
+        (ANY, (width, wide), BF16),
+        (ANY, (wide, width), BF16),
+        (ANY, (total, width), BF16),
+        (VM, (micro, length, columns), BF16),
+        (VM, (micro, length, width), BF16),
+        (VM, (micro, heads, length // BLOCK, length), F32),
+        (VM, (micro, 8, length), F32),
+        (VM, (micro, 4, rows, width // 4), BF16),
+        (VM, (total, width), BF16),
+        (ANY, (total, width), BF16),
+        (VM, (total, width), F32),
+        (VM, (total, width), BF16),
+        (ANY, (total, width), BF16),
+    )
+    return pl.pallas_call(
+        forward_kernel,
+        name="forward_together",
+        out_shape=tuple(shape(dims, kind) for _, dims, kind in outs),
+        in_specs=[SM] + [VM] * 3 + [ANY] * 5,
+        out_specs=tuple(spec for spec, _, _ in outs),
+        scratch_shapes=[
+            pltpu.VMEM((micro, 4, rows, width), BF16),
+            pltpu.VMEM((8,) + small.shape, F32),
+            pltpu.VMEM(picks.shape, jnp.int32),
+            pltpu.VMEM((width, columns), BF16),
+            pltpu.VMEM((width, width), BF16),
+            pltpu.VMEM((total, width), BF16),
+            pltpu.VMEM((total, width), BF16),
+            pltpu.SemaphoreType.DMA((FORWARD_MOVES,)),
+            pltpu.SemaphoreType.DMA((FORWARD_MOVES,)),
+            pltpu.SemaphoreType.DMA((9,)),
+        ],
+        compiler_params=pltpu.CompilerParams(
+            collective_id=0, has_side_effects=True, vmem_limit_bytes=56 * MIB
+        ),
+        cost_estimate=cost(16 * total * width * width, 64 * MIB),
+    )(global_ids, tokens, small, picks, triple_part, output_part, expand_part, shrink_part, tangent)
 
 
 def block_biases(chosen, globals_here, rank, local_blocks):
@@ -606,59 +833,110 @@
     ids = jnp.stack([place, rank, core, jnp.int32(0)])
     ids_sent = jnp.stack([place, rank, core, jnp.int32(1)])
 
-    small = jnp.concatenate(
-        [attend_gain, attend_bias, hidden_gain, hidden_bias, shrink_bias, expand_bias]
-    ).reshape(1, -1)
-    small_rows = gather_rows(small) if ways == 8 else None
-    triple_part = jnp.take(triple_weight.reshape(shard, 3, 4, width // 4), rank, axis=2)
-    triple_pieces = gather_rows(triple_part.reshape(shard, 3 * width // 4))
-    token_parts, chosen = [], None
-    for step in range(micro):
-        mine = tokens[step]
-        far = swap(mine, "ctx", 2)
-        token_parts.append((mine, swap(mine, "ctx", 1), far, swap(far, "ctx", 1)))
+    half_units = wide // (2 * ways)
+    vectors = [attend_gain, attend_bias, hidden_gain, hidden_bias, shrink_bias]
+    triple_part = jnp.concatenate(
+        [
+            lax.dynamic_slice_in_dim(triple_weight, k * width + rank * (width // 4), width // 4, 1)
+            for k in range(3)
+        ],
+        axis=1,
+    )
+    output_part = lax.dynamic_slice_in_dim(output_weight, core * (width // 2), width // 2, 1)
+    expand_part = jnp.concatenate(
+        [
+            lax.dynamic_slice_in_dim(expand_weight, (2 * k + core) * half_units, half_units, 1)
+            for k in range(ways)
+        ],
+        axis=1,
+    )
+    shrink_part = lax.dynamic_slice_in_dim(shrink_weight, core * (deep // 2), deep // 2, 0)
+    tangent_own = cotangent.reshape(total, width)
     picks = random_blocks[:, 0]
-    far_picks = swap(picks, "ctx", 2)
-    all_picks = jnp.stack([picks, swap(picks, "ctx", 1), far_picks, swap(far_picks, "ctx", 1)])
-    chosen = lax.dynamic_slice_in_dim(all_picks, rank * own_heads, own_heads, 2)
-    chosen = chosen.transpose(1, 2, 0, 3, 4).reshape(micro, own_heads, 4 * local_blocks, -1)
-    output_part = lax.dynamic_slice_in_dim(output_weight, core * (width // 2), width // 2, 1)
-    output_own = jnp.concatenate(gather_rows(output_part), axis=0)
-    output_other = swap(output_own, "ctx", 1)
-    if ways != 8:
-        pass
-    expand_part = jnp.take(expand_weight.reshape(shard, ways, 2, wide // (2 * ways)), core, axis=2)
-    expand_pieces = gather_rows(expand_part.reshape(shard, wide // 2))
-    shrink_part = lax.dynamic_slice_in_dim(shrink_weight, core * (deep // 2), deep // 2, 0)
-    shrink_pieces = gather_rows(shrink_part)
-    tangent_own = cotangent.reshape(total, width)
-    tangent_other = swap(tangent_own, "ctx", 1)
-
     if ways == 8:
-        table = jnp.concatenate(small_rows, axis=0)[jnp.arange(8) ^ fsdp].astype(F32)
+        small = jnp.concatenate(
+            [v.reshape(1, shard) for v in vectors]
+            + [expand_bias.reshape(-1, shard), jnp.zeros((7, shard), BF16)]
+        ).astype(F32)
+        sets = picks.reshape(micro, 4, own_heads, local_blocks, -1).transpose(1, 0, 2, 4, 3)
+        order = [rank ^ p for p in range(4)]
+        sets = jnp.concatenate([lax.dynamic_slice_in_dim(sets, r, 1, 0) for r in order], axis=0)
+        sets = jnp.pad(jnp.repeat(sets, BLOCK, axis=4), ((0, 0),) * 3 + ((0, 5), (0, 0)))
+        (
+            table,
+            triple_full,
+            output_full,
+            expand_full,
+            shrink_full,
+            tangent_other,
+            triples,
+            normeds,
+            biases,
+            lses,
+            mixed_own,
+            mixed_all,
+            mixed_other,
+            attended,
+            hidden,
+            hidden_other,
+        ) = forward_together(
+            global_blocks[:, 0],
+            tokens,
+            small,
+            sets,
+            triple_part,
+            output_part,
+            expand_part,
+            shrink_part,
+            tangent_own,
+        )
+        gain_one, bias_one, gain_two, bias_two, shift_out = (
+            table[:, k].reshape(1, width) for k in range(5)
+        )
+        shift_in = lax.dynamic_slice_in_dim(
+            table[:, 5:9].reshape(8, 2, half_units), core, 1, 1
+        ).reshape(1, wide // 2)
     else:
-        table = lax.all_gather(small, "fsdp", axis=0, tiled=True).astype(F32)
-    gain_one, bias_one, gain_two, bias_two, shift_out = (
-        table[:, k * shard : (k + 1) * shard].reshape(1, width) for k in range(5)
-    )
-    shift_in = jnp.take(table[:, 5 * shard :].reshape(ways, 2, wide // (2 * ways)), core, axis=1)
-    shift_in = shift_in.reshape(1, wide // 2)
-
-    biases, triples, normeds, lses, mixed_own, mixed_here = [], [], [], [], [], []
-    for step in range(micro):
-        biases.append(block_biases(chosen[step], global_blocks[step, 0], rank, local_blocks))
-        triple, normed = project(ids, token_parts[step], gain_one, bias_one, triple_pieces)
-        *mixed, lse = attend(triple, biases[step])
-        triples.append(triple)
-        normeds.append(normed)
-        lses.append(lse)
-        mixed_own.append(mixed)
-        mixed_here += [mixed[0]] + [swap(mixed[p], "ctx", p) for p in range(1, 4)]
-    attended, hidden, mixed_all = output_project(
-        ids, tokens, mixed_here, gain_two, bias_two, output_own, output_other
-    )
-
-    hidden_other = swap(hidden, "ctx", 1)
+
+        def whole(part):
+            return lax.all_gather(part, "fsdp", axis=0, tiled=True)
+
+        gain_one, bias_one, gain_two, bias_two, shift_out = (
+            whole(v).astype(F32).reshape(1, width) for v in vectors
+        )
+        halves = whole(expand_bias).astype(F32).reshape(ways, 2, half_units)
+        shift_in = jnp.where(core == 0, halves[:, 0], halves[:, 1]).reshape(1, wide // 2)
+        triple_full, expand_full, shrink_full = whole(triple_part), whole(expand_part), whole(shrink_part)
+        output_full = whole(output_weight)
+        tangent_other = swap(tangent_own, "ctx", 1)
+        far_picks = swap(picks, "ctx", 2)
+        all_picks = jnp.stack([picks, swap(picks, "ctx", 1), far_picks, swap(far_picks, "ctx", 1)])
+        chosen = lax.dynamic_slice_in_dim(all_picks, rank * own_heads, own_heads, 2)
+        chosen = chosen.transpose(1, 2, 0, 3, 4).reshape(micro, own_heads, 4 * local_blocks, -1)
+        triples, normeds, biases, lses, mixed_own, joined = [], [], [], [], [], []
+        for step in range(micro):
+            biases.append(block_biases(chosen[step], global_blocks[step, 0], rank, local_blocks))
+            near, far = swap(tokens[step], "ctx", 1), swap(tokens[step], "ctx", 2)
+            places = (tokens[step], near, far, swap(far, "ctx", 1))
+            triple, normed = project(places, gain_one, bias_one, triple_full)
+            mixed, lse = attend(triple, biases[step])
+            here = [mixed[0]] + [swap(mixed[p], "ctx", p) for p in range(1, 4)]
+            for low_bit, high in ((core == 1, False), (rank >= 2, True)):
+                pairs = ((0, 2), (1, 3)) if high else ((0, 1), (2, 3))
+                for one, two in pairs:
+                    first = jnp.where(low_bit, here[two], here[one])
+                    here[two] = jnp.where(low_bit, here[one], here[two])
+                    here[one] = first
+            joined.append(jnp.concatenate(here, axis=1))
+            for kept, value in zip(
+                (triples, normeds, lses, mixed_own), (triple, normed, lse, mixed)
+            ):
+                kept.append(value)
+        mixed_all = jnp.concatenate(joined, axis=0)
+        mixed_other = swap(mixed_all, "ctx", 1)
+        attended, hidden = output_project(tokens, mixed_all, gain_two, bias_two, output_full)
+        hidden_other = swap(hidden, "ctx", 1)
+
     (
         own_out,
         other_out,
@@ -669,7 +947,7 @@
         shrink_kept,
         expand_sent,
         expand_kept,
-    ) = feed(ids, (hidden, hidden_other), (tangent_own, tangent_other), shift_in, expand_pieces, shrink_pieces)
+    ) = feed(ids, (hidden, hidden_other), (tangent_own, tangent_other), shift_in, expand_full, shrink_full)
     came_hidden = swap(other_hidden, "ctx", 1)
     came_out = swap(other_out, "ctx", 1)
     shrink_mine = scatter_rows(shrink_kept, shrink_sent)
@@ -684,10 +962,8 @@
         came_out,
         gain_two,
         shift_out,
-        output_own,
-        output_other,
+        output_full,
     )
-    mixed_other = swap(mixed_all, "ctx", 1)
     half_sent = lax.dynamic_slice_in_dim(d_branch, (1 - core) * (width // 2), width // 2, 1)
     branch_other = swap(half_sent, "ctx", 1)
     output_sent = output_grad(ids_sent, mixed_all, mixed_other, d_branch, branch_other)
@@ -698,15 +974,16 @@
     for step in range(micro):
         here = grads[4 * step : 4 * step + 4]
         here = [here[0]] + [swap(here[p], "ctx", p) for p in range(1, 4)]
-        d_triple, *parts = attend_back(
-            ids, triples[step], biases[step], lses[step], here, mixed_own[step], triple_pieces, width
+        d_triple, parts = attend_back(
+            triples[step], biases[step], lses[step], here, mixed_own[step], triple_full
         )
         d_triples.append(d_triple)
         near = swap(parts[1], "ctx", 1)
         far = wide_add(parts[2], swap(parts[3], "ctx", 1)).astype(BF16)
         norm_parts_here += [parts[0], near, swap(far, "ctx", 2)]
-    triple_sent = triple_grad(ids_sent, normeds, d_triples)
-    triple_kept = triple_grad(ids, normeds, d_triples)
+    normed_pair = (normeds[0], normeds[1])
+    triple_sent = triple_grad(ids_sent, normed_pair, d_triples)
+    triple_kept = triple_grad(ids, normed_pair, d_triples)
     triple_mine = scatter_rows(triple_kept, triple_sent)
     token_grad, gain_one_grad, bias_one_grad = first_back(
         tokens, d_attended, gain_one, norm_parts_here

time: 592 us -> 545 us (0.921)
  Pallas kernels: 150 us -> 264 us
  starting transfers between devices: 157 us -> 57.8 us
  waiting for transfers between devices: 215 us -> 150 us
    pallas_call x5 -> x1, Pallas kernels: 47.2 us -> 152 us  [forward_together(): pl.pallas_call(forward_kernel, name='forward_together', out_shape=tuple((...]
    ppermute x103 -> x49, starting transfers between devices: 157 us -> 57.8 us  [swap(): return lax.ppermute(value, axis, [(i, i ^ step) for i in range(size)])]
    ppermute x103 -> x49, waiting for transfers between devices: 215 us -> 150 us  [swap(): return lax.ppermute(value, axis, [(i, i ^ step) for i in range(size)])]
    unnamed x173 -> x85, local copies, waits for them, and re-layouts: 22.4 us -> 7 us
    squeeze x1 -> x7, local copies, waits for them, and re-layouts: 1.03 us -> 11.6 us  [the longest x2 4.63 us: on_device(): far = wide_add(parts[2], swap(parts[3], 'ctx', 1)).astype(BF16)]
    pallas_call x2, Pallas kernels: 31.3 us -> 41.8 us  [attend_back(): pl.pallas_call(attend_back_kernel, name='attend_back', out_shape=(shape((...]
  transfers between devices with their start and end apart: 103 -> 49, of which waited for: 29 -> 11; matrix products, arithmetic and copies ran while one was open for 8% -> 9% of each run, Pallas kernels for 18% -> 14%
where the time goes in v2:
time: 545 us; the launch traced here: 536 us
  Pallas kernels  264 us (48%)
  waiting for transfers between devices  150 us (28%)
  starting transfers between devices  57.8 us (11%)
  local copies, waits for them, and re-layouts  35.4 us (6%)
  other arithmetic  27.4 us (5%)
    pallas_call x1, Pallas kernels, forward_together(): pl.pallas_call(forward_kernel, name='forward_together', out_shape=tuple((...  152 us
    ppermute x49, waiting for transfers between devices, swap(): return lax.ppermute(value, axis, [(i, i ^ step) for i in range(size)])  150 us
    ppermute x49, starting transfers between devices, swap(): return lax.ppermute(value, axis, [(i, i ^ step) for i in range(size)])  57.8 us
    pallas_call x2, Pallas kernels, attend_back(): pl.pallas_call(attend_back_kernel, name='attend_back', out_shape=(shape((...  41.8 us
    pallas_call x1, Pallas kernels, feed(): pl.pallas_call(feed_kernel, name='feed', out_shape=(shape((rows, width),...  36.6 us
    pallas_call x2, Pallas kernels, triple_grad(): pl.pallas_call(triple_grad_kernel, name='triple_grad', out_shape=shape((4...  12.1 us
  transfers between devices with their start and end apart: 49, of which 11 were waited for; matrix products, arithmetic and copies ran while one was open for 9% of the time, Pallas kernels for 14%

profile of v2, /device:TPU:1, one launch (start us, length us, event | category | flops | bytes accessed | tf_op | source)
XLA Modules:
  0.0 535.7 jit_solution(6420019742558188859)
XLA Ops:
  0.7 1.7 concatenate.24
  5.3 1.6 constant_dynamic-slice_fusion.7.output_part
  9.7 151.6 %forward_together.1 = (f32[8,16,128]{2,1,0:T(8,128)}, bf16[1024,768]{1,0:T(8,128)(2,1)}, bf16[1024,1024]{1,0:T(8,128)(2,1)}, bf16[1024,2048]{1,0:T(8,128)(2,1)},...) custom-call(s32[2,2]{1,0:T(2,128)} %bitcast.205, ...), custom_call_target="tpu_custom_call" | custom-call | flops 8589934592 | bytes 67108864 | tf_op jit(solution)/shard_map/forward_together/pallas_call | solution.py:766
  164.0 36.6 %feed.1 = (f32[512,1024]{1,0:T(8,128)}, bf16[512,1024]{1,0:T(8,128)(2,1)}, f32[512,1024]{1,0:T(8,128)}, bf16[512,1024]{1,0:T(8,128)(2,1)}, f32[1,2048]{1,0:T(1,1...) custom-call(s32[4]{0:T(128)} %pad_add_fusion.1.ids, ...), custom_call_target="tpu_custom_call" | custom-call | flops 25769803776 | bytes 27262976 | tf_op jit(solution)/shard_map/feed/pallas_call | solution.py:340
  202.0 1.5 slice_bitcast_fusion.16
  203.5 1.9 slice_bitcast_fusion.2
  206.9 2.5 slice_bitcast_fusion
  209.4 9.0 %branch_back.1 = (bf16[2,256,1024]{2,1,0:T(8,128)(2,1)}, f32[512,1024]{1,0:T(8,128)}, bf16[512,1024]{1,0:T(8,128)(2,1)}, bf16[256,256]{1,0:T(8,128)(2,1)}, bf16[...) custom-call(s32[4]{0:T(128)} %pad_add_fusion.1.ids, ...), custom_call_target="tpu_custom_call" | custom-call | flops 1073741824 | bytes 16777216 | tf_op jit(solution)/shard_map/branch_back/pallas_call | solution.py:404
  226.2 23.0 %collective-permute-done.34 = f32[8,896]{1,0:T(8,128)S(1)} collective-permute-done((f32[8,896]{1,0:T(8,128)S(1)}, f32[8,896]{1,0:T(8,128)S(1)}, u32[]{:S(2)}, u32[]{:S(2)}) %collective-permute-start.34) | collective-permute-done | bytes 28704 | tf_op jit(solution)/shard_map/ppermute | solution.py:44
  251.8 6.8 %collective-permute-start.35 = (f32[8,896]{1,0:T(8,128)S(1)}, f32[8,896]{1,0:T(8,128)S(1)}, u32[]{:S(2)}, u32[]{:S(2)}) collective-permute-start(f32[8,896]{1,0:T(8,128)S(1)} %add.276), channel_id=1, source_target_pairs={{0,2},{1,3},{2,0},{3,1},{4,6},{5,7},{6,4},{7,5},{8,10},{9,11},{10,... | collective-permute-start | bytes 86024 | tf_op jit(solution)/shard_map/ppermute | solution.py:44
  258.5 20.8 %attend_back.3 = (bf16[1024,768]{1,0:T(8,128)(2,1)}, bf16[4,256,1024]{2,1,0:T(8,128)(2,1)}) custom-call(bf16[1024,768]{1,0:T(8,128)(2,1)} %get-tuple-element.150.triple, f32[4,16,1024]{2,1,0:T(8,128)} %get-tuple-element.177.block_bias, f32[8,1024]{1,0:T(8,128)} %get-tuple-element.181.lse, bf16[256,256]{1,0:T(8,128)(2,1)} %get-tuple-element.82.g0, ...), custom_call_target="tpu_custom_call" | custom-call | flops 21474836480 | bytes 4194304 | tf_op jit(solution)/shard_map/attend_back/pallas_call | solution.py:238
  279.4 2.3 slice_bitcast_fusion.4
  282.8 21.0 %attend_back.2 = (bf16[1024,768]{1,0:T(8,128)(2,1)}, bf16[4,256,1024]{2,1,0:T(8,128)(2,1)}) custom-call(bf16[1024,768]{1,0:T(8,128)(2,1)} %get-tuple-element.151.triple, f32[4,16,1024]{2,1,0:T(8,128)} %get-tuple-element.178.block_bias, f32[8,1024]{1,0:T(8,128)} %get-tuple-element.182.lse, bf16[256,256]{1,0:T(8,128)(2,1)} %get-tuple-element.75.g0, ...), custom_call_target="tpu_custom_call" | custom-call | flops 21474836480 | bytes 4194304 | tf_op jit(solution)/shard_map/attend_back/pallas_call | solution.py:238
  303.8 2.4 slice_bitcast_fusion.8
  306.3 1.7 collective-permute-start.36
  307.9 6.1 %triple_grad.3 = bf16[4,128,768]{2,1,0:T(8,128)(2,1)} custom-call(s32[4]{0:T(128)} %get-tuple-element.140.ids, bf16[1024,1024]{1,0:T(8,128)(2,1)} %get-tuple-element.149.n0, bf16[1024,1024]{1,0:T(8,128)(2,1)} %get-tuple-element.148.n1, bf16[1024,768]{1,0:T(8,128)(2,1)} %get-tuple-element.91.d0, bf16[1024,768]{1,0:T(8,128)(2,1)} %get-tuple-element.92.d1), custom_call_target="tpu_custom_call" | custom-call | flops 1610612736 | bytes 7340032 | tf_op jit(solution)/shard_map/triple_grad/pallas_call | solution.py:459
  314.1 6.0 %triple_grad.2 = bf16[4,128,768]{2,1,0:T(8,128)(2,1)} custom-call(s32[4]{0:T(128)} %pad_add_fusion.1.ids, bf16[1024,1024]{1,0:T(8,128)(2,1)} %get-tuple-element.149.n0, bf16[1024,1024]{1,0:T(8,128)(2,1)} %get-tuple-element.148.n1, bf16[1024,768]{1,0:T(8,128)(2,1)} %get-tuple-element.91.d0, bf16[1024,768]{1,0:T(8,128)(2,1)} %get-tuple-element.92.d1), custom_call_target="tpu_custom_call" | custom-call | flops 1610612736 | bytes 7340032 | tf_op jit(solution)/shard_map/triple_grad/pallas_call | solution.py:459
  326.5 1.4 collective-permute-start.13
  327.9 4.7 collective-permute-done.19
  332.6 1.8 collective-permute-start.7
  334.9 3.5 output_grad.2
  338.5 3.7 output_grad.3
  343.7 7.5 %collective-permute-done.7.rest_2_ = bf16[256,1024]{1,0:T(8,128)(2,1)S(1)} collective-permute-done((bf16[256,1024]{1,0:T(8,128)(2,1)S(1)}, bf16[256,1024]{1,0:T(8,128)(2,1)S(1)}, u32[]{:S(2)}, u32[]{:S(2)}) %collective-permute-start.7) | collective-permute-done | bytes 524320 | tf_op jit(solution)/shard_map/ppermute | solution.py:44
  352.2 5.8 %first_back.1 = (bf16[2,256,1024]{2,1,0:T(8,128)(2,1)}, f32[1,1024]{1,0:T(1,128)}, f32[1,1024]{1,0:T(1,128)}) custom-call(bf16[2,256,1024]{2,1,0:T(8,128)(2,1)} %bitcast.178, f32[512,1024]{1,0:T(8,128)} %get-tuple-element.71.d_attended, f32[1,1024]{1,0:T(1,128)} %get-tuple-element.183.gain, bf16[256,1024]{1,0:T(8,128)(2,1)} %get-tuple-element.161.rest_0_, ...), custom_call_target="tpu_custom_call" | custom-call | flops 10485760 | bytes 8388608 | tf_op jit(solution)/shard_map/first_back/pallas_call | solution.py:489
  359.7 3.0 fusion.9
  364.2 24.6 %collective-permute-done.26 = bf16[4,128,512]{2,1,0:T(8,128)(2,1)S(1)} collective-permute-done((bf16[4,128,512]{2,1,0:T(8,128)(2,1)}, bf16[4,128,512]{2,1,0:T(8,128)(2,1)S(1)}, u32[]{:S(2)}, u32[]{:S(2)}) %collective-permute-start.26) | collective-permute-done | bytes 524320 | tf_op jit(solution)/shard_map/ppermute | solution.py:44
  388.7 1.8 collective-permute-start.15
  392.3 3.0 fusion.13
  397.4 1.5 collective-permute-start.38
  400.4 14.6 %collective-permute-done.17 = f32[8,256]{1,0:T(8,128)S(1)} collective-permute-done((f32[8,256]{1,0:T(8,128)S(1)}, f32[8,256]{1,0:T(8,128)S(1)}, u32[]{:S(2)}, u32[]{:S(2)}) %collective-permute-start.17) | collective-permute-done | bytes 8224 | tf_op jit(solution)/shard_map/ppermute | solution.py:44
  416.0 2.5 collective-permute-start.44
  419.8 39.2 %collective-permute-done.18 = f32[8,256]{1,0:T(8,128)S(1)} collective-permute-done((f32[8,256]{1,0:T(8,128)S(1)}, f32[8,256]{1,0:T(8,128)S(1)}, u32[]{:S(2)}, u32[]{:S(2)}) %collective-permute-start.18) | collective-permute-done | bytes 8224 | tf_op jit(solution)/shard_map/ppermute | solution.py:44
  459.0 1.4 collective-permute-start.30
  461.0 1.9 collective-permute-done.30
  464.1 1.5 collective-permute-start.23
  465.7 5.2 collective-permute-start.31
  470.9 1.6 fusion.5
  473.6 31.3 %collective-permute-done.45 = bf16[256,1024]{1,0:T(8,128)(2,1)S(1)} collective-permute-done((bf16[256,1024]{1,0:T(8,128)(2,1)}, bf16[256,1024]{1,0:T(8,128)(2,1)S(1)}, u32[]{:S(2)}, u32[]{:S(2)}) %collective-permute-start.45) | collective-permute-done | bytes 524320 | tf_op jit(solution)/shard_map/ppermute | solution.py:44
  504.9 1.7 fusion.2
  506.6 1.6 collective-permute-start.47
  508.2 4.6 collective-permute-start.24
  514.2 1.6 collective-permute-done.47
  517.0 5.2 collective-permute-start.48
  524.7 1.6 copy.50
  526.4 1.7 select_bitcast_fusion.3
  528.2 1.6 copy.47
  529.8 2.7 reshape.191
  534.0 1.5 pad_maximum_fusion.1
  (219 shorter events, 52.6 us)
Async XLA Ops:
  200.6 8.8 %collective-permute-start = (bf16[512,1024]{1,0:T(8,128)(2,1)}, bf16[512,1024]{1,0:T(8,128)(2,1)}, u32[]{:S(2)}, u32[]{:S(2)}) collective-permute-start(bf16[512,1024]{1,0:T(8,128)(2,1)} %get-tuple-element.66), channel_id=1, source_target_pairs={{0,8},{8,0},{16,24},{24,16},{1,9},{9,1},{17,25},{25,17},{2,10},{10... | collective-permute-start | bytes 3145736 | tf_op jit(solution)/shard_map/ppermute | solution.py:44
  200.6 8.8 %collective-permute-start.1 = (bf16[512,1024]{1,0:T(8,128)(2,1)}, bf16[512,1024]{1,0:T(8,128)(2,1)}, u32[]{:S(2)}, u32[]{:S(2)}) collective-permute-start(bf16[512,1024]{1,0:T(8,128)(2,1)} %get-tuple-element.68), channel_id=1, source_target_pairs={{0,8},{8,0},{16,24},{24,16},{1,9},{9,1},{17,25},{25,17},{2,10},{10... | collective-permute-start | bytes 3145736 | tf_op jit(solution)/shard_map/ppermute | solution.py:44
  201.1 157.6 %collective-permute-start.37 = (bf16[4,128,2048]{2,1,0:T(8,128)(2,1)}, bf16[4,128,2048]{2,1,0:T(8,128)(2,1)}, u32[]{:S(2)}, u32[]{:S(2)}) collective-permute-start(bf16[4,128,2048]{2,1,0:T(8,128)(2,1)} %get-tuple-element.101), channel_id=1, source_target_pairs={{0,1},{1,0},{2,3},{3,2},{4,5},{5,4},{6,7},{7,6},{8,9},{9,8},{10,11... | collective-permute-start | bytes 6291464 | tf_op jit(solution)/shard_map/ppermute | solution.py:44
  220.8 3.5 collective-permute-start.33
  222.2 27.8 %collective-permute-start.8 = (bf16[256,256]{1,0:T(8,128)(2,1)S(1)}, bf16[256,256]{1,0:T(8,128)(2,1)S(1)}, u32[]{:S(2)}, u32[]{:S(2)}) collective-permute-start(bf16[256,256]{1,0:T(8,128)(2,1)S(1)} %copy-done.30), channel_id=1, source_target_pairs={{0,8},{8,0},{16,24},{24,16},{1,9},{9,1},{17,25},{25,17},{2,10},{10... | collective-permute-start | bytes 393224 | tf_op jit(solution)/shard_map/ppermute | solution.py:44
  222.6 27.9 %collective-permute-start.9 = (bf16[256,256]{1,0:T(8,128)(2,1)S(1)}, bf16[256,256]{1,0:T(8,128)(2,1)S(1)}, u32[]{:S(2)}, u32[]{:S(2)}) collective-permute-start(bf16[256,256]{1,0:T(8,128)(2,1)S(1)} %copy-done.29), channel_id=1, source_target_pairs={{0,16},{8,24},{16,0},{24,8},{1,17},{9,25},{17,1},{25,9},{2,18},{10... | collective-permute-start | bytes 393224 | tf_op jit(solution)/shard_map/ppermute | solution.py:44
  223.6 28.2 %collective-permute-start.10 = (bf16[256,256]{1,0:T(8,128)(2,1)S(1)}, bf16[256,256]{1,0:T(8,128)(2,1)S(1)}, u32[]{:S(2)}, u32[]{:S(2)}) collective-permute-start(bf16[256,256]{1,0:T(8,128)(2,1)S(1)} %copy-done.28), channel_id=1, source_target_pairs={{0,24},{8,16},{16,8},{24,0},{1,25},{9,17},{17,9},{25,1},{2,26},{10... | collective-permute-start | bytes 393224 | tf_op jit(solution)/shard_map/ppermute | solution.py:44
  224.3 24.9 %collective-permute-start.34 = (f32[8,896]{1,0:T(8,128)S(1)}, f32[8,896]{1,0:T(8,128)S(1)}, u32[]{:S(2)}, u32[]{:S(2)}) collective-permute-start(f32[8,896]{1,0:T(8,128)S(1)} %add.275), channel_id=1, source_target_pairs={{0,1},{1,0},{2,3},{3,2},{4,5},{5,4},{6,7},{7,6},{8,9},{9,8},{10,11... | collective-permute-start | bytes 86024 | tf_op jit(solution)/shard_map/ppermute | solution.py:44
  249.2 32.4 %collective-permute-start.2 = (bf16[256,256]{1,0:T(8,128)(2,1)S(1)}, bf16[256,256]{1,0:T(8,128)(2,1)S(1)}, u32[]{:S(2)}, u32[]{:S(2)}) collective-permute-start(bf16[256,256]{1,0:T(8,128)(2,1)S(1)} %copy-done.27), channel_id=1, source_target_pairs={{0,8},{8,0},{16,24},{24,16},{1,9},{9,1},{17,25},{25,17},{2,10},{10... | collective-permute-start | bytes 393224 | tf_op jit(solution)/shard_map/ppermute | solution.py:44
  250.0 32.1 %collective-permute-start.3 = (bf16[256,256]{1,0:T(8,128)(2,1)S(1)}, bf16[256,256]{1,0:T(8,128)(2,1)S(1)}, u32[]{:S(2)}, u32[]{:S(2)}) collective-permute-start(bf16[256,256]{1,0:T(8,128)(2,1)S(1)} %copy-done.26), channel_id=1, source_target_pairs={{0,16},{8,24},{16,0},{24,8},{1,17},{9,25},{17,1},{25,9},{2,18},{10... | collective-permute-start | bytes 393224 | tf_op jit(solution)/shard_map/ppermute | solution.py:44
  250.6 31.6 %collective-permute-start.4 = (bf16[256,256]{1,0:T(8,128)(2,1)S(1)}, bf16[256,256]{1,0:T(8,128)(2,1)S(1)}, u32[]{:S(2)}, u32[]{:S(2)}) collective-permute-start(bf16[256,256]{1,0:T(8,128)(2,1)S(1)} %copy-done.25), channel_id=1, source_target_pairs={{0,24},{8,16},{16,8},{24,0},{1,25},{9,17},{17,9},{25,1},{2,26},{10... | collective-permute-start | bytes 393224 | tf_op jit(solution)/shard_map/ppermute | solution.py:44
  251.8 54.5 %collective-permute-start.35 = (f32[8,896]{1,0:T(8,128)S(1)}, f32[8,896]{1,0:T(8,128)S(1)}, u32[]{:S(2)}, u32[]{:S(2)}) collective-permute-start(f32[8,896]{1,0:T(8,128)S(1)} %add.276), channel_id=1, source_target_pairs={{0,2},{1,3},{2,0},{3,1},{4,6},{5,7},{6,4},{7,5},{8,10},{9,11},{10,... | collective-permute-start | bytes 86024 | tf_op jit(solution)/shard_map/ppermute | solution.py:44
  281.6 40.5 %collective-permute-start.12 = (bf16[256,1024]{1,0:T(8,128)(2,1)S(1)}, bf16[256,1024]{1,0:T(8,128)(2,1)S(1)}, u32[]{:S(2)}, u32[]{:S(2)}) collective-permute-start(bf16[256,1024]{1,0:T(8,128)(2,1)S(1)} %get-tuple-element.156), channel_id=1, source_target_pairs={{0,8},{8,0},{16,24},{24,16},{1,9},{9,1},{17,25},{25,17},{2,10},{10... | collective-permute-start | bytes 1572872 | tf_op jit(solution)/shard_map/ppermute | solution.py:44
  306.2 17.2 %collective-permute-start.6 = (bf16[256,1024]{1,0:T(8,128)(2,1)S(1)}, bf16[256,1024]{1,0:T(8,128)(2,1)S(1)}, u32[]{:S(2)}, u32[]{:S(2)}) collective-permute-start(bf16[256,1024]{1,0:T(8,128)(2,1)S(1)} %get-tuple-element.159), channel_id=1, source_target_pairs={{0,8},{8,0},{16,24},{24,16},{1,9},{9,1},{17,25},{25,17},{2,10},{10... | collective-permute-start | bytes 1572872 | tf_op jit(solution)/shard_map/ppermute | solution.py:44
  306.3 13.8 %collective-permute-start.36 = (f32[8,896]{1,0:T(8,128)S(1)}, f32[8,896]{1,0:T(8,128)S(1)}, u32[]{:S(2)}, u32[]{:S(2)}) collective-permute-start(f32[8,896]{1,0:T(8,128)S(1)} %add.277), channel_id=1, source_target_pairs={{0,4},{1,5},{2,6},{3,7},{4,0},{5,1},{6,2},{7,3},{8,12},{9,13},{10,... | collective-permute-start | bytes 86024 | tf_op jit(solution)/shard_map/ppermute | solution.py:44
  314.0 18.6 %collective-permute-start.19 = (bf16[4,128,768]{2,1,0:T(8,128)(2,1)}, bf16[4,128,768]{2,1,0:T(8,128)(2,1)S(1)}, u32[]{:S(2)}, u32[]{:S(2)}) collective-permute-start(bf16[4,128,768]{2,1,0:T(8,128)(2,1)} %triple_grad.3), channel_id=1, source_target_pairs={{0,1},{1,0},{2,3},{3,2},{4,5},{5,4},{6,7},{7,6},{8,9},{9,8},{10,11... | collective-permute-start | bytes 2359304 | tf_op jit(solution)/shard_map/ppermute | solution.py:44
  320.1 72.2 %collective-permute-start.43 = (bf16[4,256,1024]{2,1,0:T(8,128)(2,1)}, bf16[4,256,1024]{2,1,0:T(8,128)(2,1)}, u32[]{:S(2)}, u32[]{:S(2)}) collective-permute-start(bf16[4,256,1024]{2,1,0:T(8,128)(2,1)} %get-tuple-element.103), channel_id=1, source_target_pairs={{0,1},{1,0},{2,3},{3,2},{4,5},{5,4},{6,7},{7,6},{8,9},{9,8},{10,11... | collective-permute-start | bytes 6291464 | tf_op jit(solution)/shard_map/ppermute | solution.py:44
  322.1 3.8 collective-permute-start.25
  323.4 3.1 collective-permute-start.11
  325.9 17.1 %collective-permute-start.5 = (bf16[256,1024]{1,0:T(8,128)(2,1)S(1)}, bf16[256,1024]{1,0:T(8,128)(2,1)S(1)}, u32[]{:S(2)}, u32[]{:S(2)}) collective-permute-start(bf16[256,1024]{1,0:T(8,128)(2,1)S(1)} %get-tuple-element.160), channel_id=1, source_target_pairs={{0,8},{8,0},{16,24},{24,16},{1,9},{9,1},{17,25},{25,17},{2,10},{10... | collective-permute-start | bytes 1572872 | tf_op jit(solution)/shard_map/ppermute | solution.py:44
  326.5 16.7 %collective-permute-start.13 = (bf16[256,1024]{1,0:T(8,128)(2,1)S(1)}, bf16[256,1024]{1,0:T(8,128)(2,1)S(1)}, u32[]{:S(2)}, u32[]{:S(2)}) collective-permute-start(bf16[256,1024]{1,0:T(8,128)(2,1)S(1)} %fusion.6), channel_id=1, source_target_pairs={{0,16},{8,24},{16,0},{24,8},{1,17},{9,25},{17,1},{25,9},{2,18},{10... | collective-permute-start | bytes 1572872 | tf_op jit(solution)/shard_map/ppermute | solution.py:44
  332.6 18.7 %collective-permute-start.7 = (bf16[256,1024]{1,0:T(8,128)(2,1)S(1)}, bf16[256,1024]{1,0:T(8,128)(2,1)S(1)}, u32[]{:S(2)}, u32[]{:S(2)}) collective-permute-start(bf16[256,1024]{1,0:T(8,128)(2,1)S(1)} %fusion.7), channel_id=1, source_target_pairs={{0,16},{8,24},{16,0},{24,8},{1,17},{9,25},{17,1},{25,9},{2,18},{10... | collective-permute-start | bytes 1572872 | tf_op jit(solution)/shard_map/ppermute | solution.py:44
  343.0 45.7 %collective-permute-start.26 = (bf16[4,128,512]{2,1,0:T(8,128)(2,1)}, bf16[4,128,512]{2,1,0:T(8,128)(2,1)S(1)}, u32[]{:S(2)}, u32[]{:S(2)}) collective-permute-start(bf16[4,128,512]{2,1,0:T(8,128)(2,1)} %output_grad.3), channel_id=1, source_target_pairs={{0,1},{1,0},{2,3},{3,2},{4,5},{5,4},{6,7},{7,6},{8,9},{9,8},{10,11... | collective-permute-start | bytes 1572872 | tf_op jit(solution)/shard_map/ppermute | solution.py:44
  343.1 53.1 %collective-permute-start.20 = (bf16[128,768]{1,0:T(8,128)(2,1)}, bf16[128,768]{1,0:T(8,128)(2,1)S(1)}, u32[]{:S(2)}, u32[]{:S(2)}) collective-permute-start(bf16[128,768]{1,0:T(8,128)(2,1)} %get-tuple-element.162), channel_id=1, source_target_pairs={{0,2},{1,3},{2,0},{3,1},{4,6},{5,7},{6,4},{7,5},{8,10},{9,11},{10,... | collective-permute-start | bytes 589832 | tf_op jit(solution)/shard_map/ppermute | solution.py:44
  351.3 46.1 %collective-permute-start.22 = (bf16[128,768]{1,0:T(8,128)(2,1)}, bf16[128,768]{1,0:T(8,128)(2,1)}, u32[]{:S(2)}, u32[]{:S(2)}) collective-permute-start(bf16[128,768]{1,0:T(8,128)(2,1)} %get-tuple-element.163), channel_id=1, source_target_pairs={{0,6},{1,7},{2,4},{3,5},{4,2},{5,3},{6,0},{7,1},{8,14},{9,15},{10,... | collective-permute-start | bytes 589832 | tf_op jit(solution)/shard_map/ppermute | solution.py:44
  358.7 4.1 collective-permute-start.14
  362.8 36.1 %collective-permute-start.21 = (bf16[128,768]{1,0:T(8,128)(2,1)S(1)}, bf16[128,768]{1,0:T(8,128)(2,1)S(1)}, u32[]{:S(2)}, u32[]{:S(2)}) collective-permute-start(bf16[128,768]{1,0:T(8,128)(2,1)S(1)} %get-tuple-element.164), channel_id=1, source_target_pairs={{0,4},{1,5},{2,6},{3,7},{4,0},{5,1},{6,2},{7,3},{8,12},{9,13},{10,... | collective-permute-start | bytes 589832 | tf_op jit(solution)/shard_map/ppermute | solution.py:44
  388.7 2.9 collective-permute-start.15
  391.6 24.4 %collective-permute-start.27 = (bf16[128,512]{1,0:T(8,128)(2,1)}, bf16[128,512]{1,0:T(8,128)(2,1)}, u32[]{:S(2)}, u32[]{:S(2)}) collective-permute-start(bf16[128,512]{1,0:T(8,128)(2,1)} %get-tuple-element.165), channel_id=1, source_target_pairs={{0,2},{1,3},{2,0},{3,1},{4,6},{5,7},{6,4},{7,5},{8,10},{9,11},{10,... | collective-permute-start | bytes 393224 | tf_op jit(solution)/shard_map/ppermute | solution.py:44
  392.2 3.1 collective-permute-start.16
  395.3 20.7 %collective-permute-start.29 = (bf16[128,512]{1,0:T(8,128)(2,1)}, bf16[128,512]{1,0:T(8,128)(2,1)}, u32[]{:S(2)}, u32[]{:S(2)}) collective-permute-start(bf16[128,512]{1,0:T(8,128)(2,1)} %get-tuple-element.166), channel_id=1, source_target_pairs={{0,6},{1,7},{2,4},{3,5},{4,2},{5,3},{6,0},{7,1},{8,14},{9,15},{10,... | collective-permute-start | bytes 393224 | tf_op jit(solution)/shard_map/ppermute | solution.py:44
  396.3 22.3 %collective-permute-start.28 = (bf16[128,512]{1,0:T(8,128)(2,1)}, bf16[128,512]{1,0:T(8,128)(2,1)}, u32[]{:S(2)}, u32[]{:S(2)}) collective-permute-start(bf16[128,512]{1,0:T(8,128)(2,1)} %get-tuple-element.167), channel_id=1, source_target_pairs={{0,4},{1,5},{2,6},{3,7},{4,0},{5,1},{6,2},{7,3},{8,12},{9,13},{10,... | collective-permute-start | bytes 393224 | tf_op jit(solution)/shard_map/ppermute | solution.py:44
  397.4 66.7 %collective-permute-start.38 = (bf16[128,2048]{1,0:T(8,128)(2,1)}, bf16[128,2048]{1,0:T(8,128)(2,1)}, u32[]{:S(2)}, u32[]{:S(2)}) collective-permute-start(bf16[128,2048]{1,0:T(8,128)(2,1)} %get-tuple-element.145), channel_id=1, source_target_pairs={{0,2},{1,3},{2,0},{3,1},{4,6},{5,7},{6,4},{7,5},{8,10},{9,11},{10,... | collective-permute-start | bytes 1572872 | tf_op jit(solution)/shard_map/ppermute | solution.py:44
  398.9 16.1 %collective-permute-start.17 = (f32[8,256]{1,0:T(8,128)S(1)}, f32[8,256]{1,0:T(8,128)S(1)}, u32[]{:S(2)}, u32[]{:S(2)}) collective-permute-start(f32[8,256]{1,0:T(8,128)S(1)} %add.254), channel_id=1, source_target_pairs={{0,2},{1,3},{2,0},{3,1},{4,6},{5,7},{6,4},{7,5},{8,10},{9,11},{10,... | collective-permute-start | bytes 24584 | tf_op jit(solution)/shard_map/ppermute | solution.py:44
  415.0 49.1 %collective-permute-start.40 = (bf16[128,2048]{1,0:T(8,128)(2,1)}, bf16[128,2048]{1,0:T(8,128)(2,1)S(1)}, u32[]{:S(2)}, u32[]{:S(2)}) collective-permute-start(bf16[128,2048]{1,0:T(8,128)(2,1)} %get-tuple-element.146), channel_id=1, source_target_pairs={{0,6},{1,7},{2,4},{3,5},{4,2},{5,3},{6,0},{7,1},{8,14},{9,15},{10,... | collective-permute-start | bytes 1572872 | tf_op jit(solution)/shard_map/ppermute | solution.py:44
  416.0 49.6 %collective-permute-start.39 = (bf16[128,2048]{1,0:T(8,128)(2,1)S(1)}, bf16[128,2048]{1,0:T(8,128)(2,1)S(1)}, u32[]{:S(2)}, u32[]{:S(2)}) collective-permute-start(bf16[128,2048]{1,0:T(8,128)(2,1)S(1)} %get-tuple-element.147), channel_id=1, source_target_pairs={{0,4},{1,5},{2,6},{3,7},{4,0},{5,1},{6,2},{7,3},{8,12},{9,13},{10,... | collective-permute-start | bytes 1572872 | tf_op jit(solution)/shard_map/ppermute | solution.py:44
  416.0 56.6 %collective-permute-start.44 = (bf16[256,1024]{1,0:T(8,128)(2,1)}, bf16[256,1024]{1,0:T(8,128)(2,1)S(1)}, u32[]{:S(2)}, u32[]{:S(2)}) collective-permute-start(bf16[256,1024]{1,0:T(8,128)(2,1)} %get-tuple-element.142), channel_id=1, source_target_pairs={{0,2},{1,3},{2,0},{3,1},{4,6},{5,7},{6,4},{7,5},{8,10},{9,11},{10,... | collective-permute-start | bytes 1572872 | tf_op jit(solution)/shard_map/ppermute | solution.py:44
  418.5 40.4 %collective-permute-start.18 = (f32[8,256]{1,0:T(8,128)S(1)}, f32[8,256]{1,0:T(8,128)S(1)}, u32[]{:S(2)}, u32[]{:S(2)}) collective-permute-start(f32[8,256]{1,0:T(8,128)S(1)} %add.255), channel_id=1, source_target_pairs={{0,4},{1,5},{2,6},{3,7},{4,0},{5,1},{6,2},{7,3},{8,12},{9,13},{10,... | collective-permute-start | bytes 24584 | tf_op jit(solution)/shard_map/ppermute | solution.py:44
  459.0 3.8 collective-permute-start.30
  462.8 10.8 %collective-permute-start.46 = (bf16[256,1024]{1,0:T(8,128)(2,1)}, bf16[256,1024]{1,0:T(8,128)(2,1)S(1)}, u32[]{:S(2)}, u32[]{:S(2)}) collective-permute-start(bf16[256,1024]{1,0:T(8,128)(2,1)} %get-tuple-element.143), channel_id=1, source_target_pairs={{0,6},{1,7},{2,4},{3,5},{4,2},{5,3},{6,0},{7,1},{8,14},{9,15},{10,... | collective-permute-start | bytes 1572872 | tf_op jit(solution)/shard_map/ppermute | solution.py:44
  464.0 40.8 %collective-permute-start.45 = (bf16[256,1024]{1,0:T(8,128)(2,1)}, bf16[256,1024]{1,0:T(8,128)(2,1)S(1)}, u32[]{:S(2)}, u32[]{:S(2)}) collective-permute-start(bf16[256,1024]{1,0:T(8,128)(2,1)} %get-tuple-element.144), channel_id=1, source_target_pairs={{0,4},{1,5},{2,6},{3,7},{4,0},{5,1},{6,2},{7,3},{8,12},{9,13},{10,... | collective-permute-start | bytes 1572872 | tf_op jit(solution)/shard_map/ppermute | solution.py:44
  464.1 8.4 %collective-permute-start.23 = (bf16[128,3,256]{0,2,1:T(8,128)(2,1)S(1)}, bf16[128,3,256]{0,2,1:T(8,128)(2,1)S(1)}, u32[]{:S(2)}, u32[]{:S(2)}) collective-permute-start(bf16[128,3,256]{0,2,1:T(8,128)(2,1)S(1)} %bitcast.179), channel_id=1, source_target_pairs={{0,16},{8,24},{16,0},{24,8},{1,17},{9,25},{17,1},{25,9},{2,18},{10... | collective-permute-start | bytes 589832 | tf_op jit(solution)/shard_map/ppermute | solution.py:44
  465.7 56.5 %collective-permute-start.31 = (f32[128,512]{1,0:T(8,128)S(1)}, f32[128,512]{1,0:T(8,128)S(1)}, u32[]{:S(2)}, u32[]{:S(2)}) collective-permute-start(f32[128,512]{1,0:T(8,128)S(1)} %convert_add_fusion.8), channel_id=1, source_target_pairs={{0,8},{8,0},{16,24},{24,16},{1,9},{9,1},{17,25},{25,17},{2,10},{10... | collective-permute-start | bytes 786440 | tf_op jit(solution)/shard_map/ppermute | solution.py:44
  472.5 40.3 %collective-permute-start.41 = (bf16[128,2048]{1,0:T(8,128)(2,1)S(1)}, bf16[128,2048]{1,0:T(8,128)(2,1)S(1)}, u32[]{:S(2)}, u32[]{:S(2)}) collective-permute-start(bf16[128,2048]{1,0:T(8,128)(2,1)S(1)} %fusion.5), channel_id=1, source_target_pairs={{0,16},{8,24},{16,0},{24,8},{1,17},{9,25},{17,1},{25,9},{2,18},{10... | collective-permute-start | bytes 1572872 | tf_op jit(solution)/shard_map/ppermute | solution.py:44
  506.6 9.3 %collective-permute-start.47 = (bf16[256,1024]{1,0:T(8,128)(2,1)S(1)}, bf16[256,1024]{1,0:T(8,128)(2,1)S(1)}, u32[]{:S(2)}, u32[]{:S(2)}) collective-permute-start(bf16[256,1024]{1,0:T(8,128)(2,1)S(1)} %fusion.2), channel_id=1, source_target_pairs={{0,16},{8,24},{16,0},{24,8},{1,17},{9,25},{17,1},{25,9},{2,18},{10... | collective-permute-start | bytes 1572872 | tf_op jit(solution)/shard_map/ppermute | solution.py:44
  508.2 15.3 %collective-permute-start.24 = (bf16[128,3,2,256]{0,3,1,2:T(8,128)(2,1)S(1)}, bf16[128,3,2,256]{0,3,1,2:T(8,128)(2,1)}, u32[]{:S(2)}, u32[]{:S(2)}) collective-permute-start(bf16[128,3,2,256]{0,3,1,2:T(8,128)(2,1)S(1)} %pad_maximum_fusion.3), channel_id=1, source_target_pairs={{0,8},{8,0},{16,24},{24,16},{1,9},{9,1},{17,25},{25,17},{2,10},{10... | collective-permute-start | bytes 1179656 | tf_op jit(solution)/shard_map/ppermute | solution.py:44
  514.2 12.2 %collective-permute-start.42 = (f32[128,8,256]{2,1,0:T(8,128)}, f32[128,8,256]{2,1,0:T(8,128)}, u32[]{:S(2)}, u32[]{:S(2)}) collective-permute-start(f32[128,8,256]{2,1,0:T(8,128)} %bitcast.96), channel_id=1, source_target_pairs={{0,8},{8,0},{16,24},{24,16},{1,9},{9,1},{17,25},{25,17},{2,10},{10... | collective-permute-start | bytes 3145736 | tf_op jit(solution)/shard_map/ppermute | solution.py:44
  517.0 15.5 %collective-permute-start.48 = (f32[256,1024]{1,0:T(8,128)}, f32[256,1024]{1,0:T(8,128)}, u32[]{:S(2)}, u32[]{:S(2)}) collective-permute-start(f32[256,1024]{1,0:T(8,128)} %convert_add_fusion.4), channel_id=1, source_target_pairs={{0,8},{8,0},{16,24},{24,16},{1,9},{9,1},{17,25},{25,17},{2,10},{10... | collective-permute-start | bytes 3145736 | tf_op jit(solution)/shard_map/ppermute | solution.py:44
  (38 other events, 353.5 us)
